TPU v7x, 32 devices: a whole 2x2x4 slice. The times are simulated.
32 devices in a mesh: row: 16 (over z, x, core), col: 2 (over y).
Axes of the slice: x: 2, y: 2, z: 4, core: 2. Of those that a mesh axis runs over, the one named last changes fastest.
Arguments:
- object_slices: float32 [2, 2, 1536, 192], P(None, None, 'row', 'col'), may hold values from -4 to 4
- probe: float32 [2, 192, 192], replicated, may hold values from -4 to 4
- propagator_phase: float32 [192, 192], replicated, may hold values from -3.140625 to 3.140625
- measured: float32 [16, 2, 2, 192, 192], P('row', 'col'), may hold values from 0 to 2
- offsets: int32 [16, 2, 2, 2], P('row', 'col'), may hold values from 0 to 95
- counts: int32 [16, 2], P('row', 'col'), may hold values from 1 to 2
Outputs:
- object_out: float32 [2, 2, 1536, 192], P(None, None, 'row', 'col')
- probe_out: float32 [2, 192, 192], replicated
Inputs may be any that keep to these rules, and one draw needn't show every extreme that they name: The slots below counts hold the tile's scan positions; the others are unused.
All inputs are finite; a program needn't handle non-finite values.
Results may differ from a plain program's by a relative error of at most 0.00014.
Values sent between devices are 32-bit elements; how exact they have to be, the bound alone decides.
No kernel may reach another device: no remote copies, remote signals or barrier semaphores. Data moves between devices by JAX's collectives and lax.ppermute only.
A program may use at most 64 MiB of HBM per device.

v0:
```python
import math

import jax
import jax.numpy as jnp
from jax import lax
from jax.sharding import PartitionSpec as P

object_rate = 0.02
probe_rate = 0.3


def extended(cells, sides, width):
    for axis, dim in sides:
        count = lax.axis_size(axis)
        ends = count - 1
        head = lax.slice_in_dim(cells, 0, width, axis=dim)
        tail = lax.slice_in_dim(cells, cells.shape[dim] - width, cells.shape[dim], axis=dim)
        cells = jnp.concatenate(
            [
                lax.ppermute(tail, axis, [(i, (i + 1) % count) for i in range(ends)]),
                cells,
                lax.ppermute(head, axis, [((i + 1) % count, i) for i in range(ends)]),
            ],
            axis=dim,
        )
    return cells


def passed_along(x, axis, by):
    peers = lax.axis_size(axis)
    pairs = [(i, i + by) for i in range(peers) if 0 <= i + by < peers]
    return lax.ppermute(x, axis, pairs)


def times(a_real, a_imag, b_real, b_imag):
    return (a_real * b_real - a_imag * b_imag, a_real * b_imag + a_imag * b_real)


def times_conj(a_real, a_imag, b_real, b_imag):
    return (a_real * b_real + a_imag * b_imag, a_real * b_imag - a_imag * b_real)


def transform(x_real, x_imag, cosine, sine):
    highest = lax.Precision.HIGHEST

    def on_left(matrix, value):
        return jnp.einsum("jk,...kl->...jl", matrix, value, precision=highest)

    def on_right(value, matrix):
        return jnp.einsum("...jk,kl->...jl", value, matrix, precision=highest)

    mid_real = on_left(cosine, x_real) - on_left(sine, x_imag)
    mid_imag = on_left(cosine, x_imag) + on_left(sine, x_real)
    out_real = on_right(mid_real, cosine) - on_right(mid_imag, sine)
    out_imag = on_right(mid_imag, cosine) + on_right(mid_real, sine)
    return (out_real, out_imag)


def shards(object_slices, probe, propagator_phase, measured, offsets, counts):
    tile = object_slices.shape[-1]
    width = probe.shape[-1]
    slots = measured.shape[2]
    devices = lax.axis_size("row") * lax.axis_size("col")
    indices = jnp.arange(width, dtype=jnp.int32)
    products = indices[:, None] * indices[None, :] % width
    angles = products.astype(jnp.float32) * (2.0 * math.pi / width)
    norm_scale = 1.0 / math.sqrt(width)
    cosine = jnp.cos(angles) * norm_scale
    sine = jnp.sin(angles) * norm_scale
    minus_sine = -sine
    trans_real = jnp.cos(propagator_phase)
    trans_imag = jnp.sin(propagator_phase)
    intensities = measured[0, 0]
    starts = offsets[0, 0] + (tile - width // 2)
    live = counts[0, 0]
    zero = jnp.zeros((), jnp.int32)
    current = object_slices
    wave = probe
    padded = extended(current, (("row", 2), ("col", 3)), tile)
    wave_real = wave[0]
    wave_imag = wave[1]

    def process_position(row_offset, column_offset, measured_intensity):
        object_window = lax.dynamic_slice(
            padded, (zero, zero, row_offset, column_offset), (2, 2, width, width)
        )
        entry_real, entry_imag = times(
            wave_real, wave_imag, object_window[0, 0], object_window[0, 1]
        )
        spec_real, spec_imag = transform(entry_real, entry_imag, cosine, minus_sine)
        spec_real, spec_imag = times(trans_real, trans_imag, spec_real, spec_imag)
        carried_real, carried_imag = transform(spec_real, spec_imag, cosine, sine)
        leave_real, leave_imag = times(
            carried_real, carried_imag, object_window[1, 0], object_window[1, 1]
        )
        detector_real, detector_imag = transform(leave_real, leave_imag, cosine, minus_sine)
        amplitude_residual = (
            detector_real * detector_real + detector_imag * detector_imag - measured_intensity
        )
        back_real, back_imag = transform(
            amplitude_residual * detector_real, amplitude_residual * detector_imag, cosine, sine
        )
        second_real, second_imag = times_conj(carried_real, carried_imag, back_real, back_imag)
        before_real, before_imag = times_conj(
            object_window[1, 0], object_window[1, 1], back_real, back_imag
        )
        before_real, before_imag = transform(before_real, before_imag, cosine, minus_sine)
        before_real, before_imag = times_conj(trans_real, trans_imag, before_real, before_imag)
        inner_real, inner_imag = transform(before_real, before_imag, cosine, sine)
        first_real, first_imag = times_conj(wave_real, wave_imag, inner_real, inner_imag)
        grad_real, grad_imag = times_conj(
            object_window[0, 0], object_window[0, 1], inner_real, inner_imag
        )
        object_term = jnp.stack(
            [jnp.stack([first_real, first_imag]), jnp.stack([second_real, second_imag])]
        )
        return (object_term, jnp.stack([grad_real, grad_imag]))

    grad_pad = jnp.zeros(padded.shape, jnp.float32)
    wave_gradient = jnp.zeros(wave.shape, jnp.float32)
    object_terms, wave_terms = jax.vmap(process_position)(starts[:, 0], starts[:, 1], intensities)
    for slot in range(slots):
        position_weight = (slot < live).astype(jnp.float32)
        corner = (zero, zero, starts[slot, 0], starts[slot, 1])
        previous = lax.dynamic_slice(grad_pad, corner, (2, 2, width, width))
        grad_pad = lax.dynamic_update_slice(
            grad_pad, previous + position_weight * object_terms[slot], corner
        )
        wave_gradient = wave_gradient + position_weight * wave_terms[slot]
    from_right = passed_along(grad_pad[:, :, :, :tile], "col", -1)
    from_left = passed_along(grad_pad[:, :, :, 2 * tile :], "col", 1)
    folded = grad_pad[:, :, :, tile : 2 * tile] + from_right + from_left
    from_below = passed_along(folded[:, :, :tile], "row", -1)
    from_above = passed_along(folded[:, :, 2 * tile :], "row", 1)
    grad_object = folded[:, :, tile : 2 * tile] + from_below + from_above
    current = current - object_rate * grad_object
    rate = probe_rate / (slots * devices)
    total = lax.psum(wave_gradient, ("row", "col"))
    wave = wave - rate * total
    return (current, wave)


def solution(mesh):
    return jax.shard_map(
        shards,
        mesh=mesh,
        in_specs=(
            P(None, None, "row", "col"),
            P(),
            P(),
            P("row", "col", None, None, None),
            P("row", "col", None, None),
            P("row", "col"),
        ),
        out_specs=(P(None, None, "row", "col"), P()),
        check_vma=False,
    )
```

profile of v0, /device:TPU:0, one launch (start us, length us, event | category | flops | bytes accessed | tf_op | source)
XLA Modules:
  0.0 284.7 jit_solution(16453844640987404774)
XLA Ops:
  7.2 1.4 collective-permute-start.1
  8.7 3.0 %collective-permute-start = (f32[2,2,96,96]{3,2,1,0:T(8,128)}, f32[2,2,96,96]{3,2,1,0:T(8,128)S(1)}, u32[]{:S(2)}, u32[]{:S(2)}) collective-permute-start(f32[2,2,96,96]{3,2,1,0:T(8,128)} %param.6), channel_id=1, source_target_pairs={{0,2},{2,4},{4,6},{6,8},{8,10},{10,12},{12,14},{14,16},{16,18},{18... | collective-permute-start | bytes 442376 | tf_op jit(solution)/shard_map/ppermute | solution.py:20
  11.7 1.4 fusion.379
  18.8 1.6 fusion.378
  24.8 1.3 collective-permute-start.3
  26.1 5.0 %collective-permute-start.2 = (f32[2,2,288,96]{3,2,1,0:T(8,128)S(1)}, f32[2,2,288,96]{3,2,1,0:T(8,128)S(1)}, u32[]{:S(2)}, u32[]{:S(2)}) collective-permute-start(f32[2,2,288,96]{3,2,1,0:T(8,128)S(1)} %constant_dynamic-update-slice_fusion), channel_id=1, source_target_pairs={{0,1},{2,3},{4,5},{6,7},{8,9},{10,11},{12,13},{14,15},{16,17},{18,... | collective-permute-start | bytes 1327112 | tf_op jit(solution)/shard_map/ppermute | solution.py:20
  31.2 10.8 %collective-permute-done.3 = f32[2,2,288,96]{3,2,1,0:T(8,128)S(1)} collective-permute-done((f32[2,2,288,96]{3,2,1,0:T(8,128)S(1)}, f32[2,2,288,96]{3,2,1,0:T(8,128)S(1)}, u32[]{:S(2)}, u32[]{:S(2)}) %collective-permute-start.3) | collective-permute-done | bytes 442400 | tf_op jit(solution)/shard_map/ppermute | solution.py:22
  42.0 1.8 collective-permute-done.2
  44.5 6.7 %while.1 = (s32[]{:T(128)}, f32[2,2,288,288]{3,2,1,0:T(8,128)S(1)}, s32[2,4]{1,0:T(2,128)S(1)}, f32[2,2,2,192,192]{4,3,0,2,1:T(8,128)}, s32[]{:T(128)}) while((s32[]{:T(128)}, f32[2,2,288,288]{3,2,1,0:T(8,128)S(1)}, s32[2,4]{1,0:T(2,128)S(1)}, f32[2,2,2,192,192]{4,3,0,2,1:T(8,128)}, s32[]{:T(128)}) %tuple.40), condition=%wide.while_cond, body=%wide.while_body.sunk | while | flops 2 | bytes 1377405 | solution.py:84
  45.2 2.5 bitcast_dynamic-update-slice_fusion.2
  48.4 2.5 bitcast_dynamic-update-slice_fusion.2
  51.2 2.6 fusion.109
  53.7 2.4 fusion.105
  56.2 1.3 convolution_subtract_fusion.11
  58.8 1.3 convolution_add_fusion.11
  63.9 1.3 fusion.24
  65.2 1.9 fusion.28
  67.1 1.3 convolution_add_fusion.9
  69.7 1.3 convolution_subtract_fusion.9
  73.5 1.3 fusion.22
  74.8 1.3 fusion.95
  76.1 1.3 fusion.91
  77.4 1.5 convolution_subtract_fusion.7
  78.8 1.3 convolution_add_fusion.7
  85.1 1.4 fusion.83
  86.5 1.4 fusion.87
  87.9 1.4 convolution_add_fusion.5
  90.5 1.6 convolution_subtract_fusion.5
  95.8 1.3 fusion.79
  97.1 1.3 fusion.75
  98.4 1.3 convolution_subtract_fusion.3
  99.7 1.3 convolution_add_fusion.3
  102.2 1.7 fusion.77
  106.4 1.3 fusion.14
  107.8 1.3 fusion.18
  109.1 1.3 convolution_add_fusion.1
  111.7 1.3 convolution_subtract_fusion.1
  115.7 2.4 fusion.33
  119.3 7.6 %dynamic_update_slice.6 = f32[2,2,288,288]{3,2,1,0:T(8,128)S(1)} dynamic-update-slice(f32[2,2,288,288]{3,2,1,0:T(8,128)S(1)} %broadcast_in_dim.2, f32[2,2,192,192]{3,2,1,0:T(8,128)} %fusion.7, s32[]{:T(128)} %constant.13.clone.1, s32[]{:T(128)} %constant.13.clone.1, s32[]{:T(128)S(6)} %select_n.126, s32[]{:T(128)S(6)} %select_n.127) | dynamic-update-slice | bytes 1179652 | tf_op jit(solution)/shard_map/dynamic_update_slice | solution.py:126
  128.1 7.9 %dynamic_update_slice.7 = f32[2,2,288,288]{3,2,1,0:T(8,128)S(1)} dynamic-update-slice(f32[2,2,288,288]{3,2,1,0:T(8,128)S(1)} %dynamic_update_slice.6, f32[2,2,192,192]{3,2,1,0:T(8,128)} %fusion.10, s32[]{:T(128)} %constant.13.clone.1, s32[]{:T(128)} %constant.13.clone.1, s32[]{:T(128)S(6)} %select_n.128, s32[]{:T(128)S(6)} %select_n.129) | dynamic-update-slice | bytes 1179652 | tf_op jit(solution)/shard_map/dynamic_update_slice | solution.py:126
  137.1 1.3 collective-permute-start.4
  138.4 5.4 %collective-permute-start.5 = (f32[2,2,288,96]{3,2,1,0:T(8,128)S(1)}, f32[2,2,288,96]{3,2,1,0:T(8,128)}, u32[]{:S(2)}, u32[]{:S(2)}) collective-permute-start(f32[2,2,288,96]{3,2,1,0:T(8,128)S(1)} %get-tuple-element.27), channel_id=1, source_target_pairs={{0,1},{2,3},{4,5},{6,7},{8,9},{10,11},{12,13},{14,15},{16,17},{18,... | collective-permute-start | bytes 1327112 | tf_op jit(solution)/shard_map/ppermute | solution.py:32
  144.7 10.5 %collective-permute-done.4 = f32[2,2,288,96]{3,2,1,0:T(8,128)S(1)} collective-permute-done((f32[2,2,288,96]{3,2,1,0:T(8,128)}, f32[2,2,288,96]{3,2,1,0:T(8,128)S(1)}, u32[]{:S(2)}, u32[]{:S(2)}) %collective-permute-start.4) | collective-permute-done | bytes 442400 | tf_op jit(solution)/shard_map/ppermute | solution.py:32
  156.3 1.3 fusion.11
  157.7 1.4 collective-permute-start.6
  159.1 3.0 %collective-permute-start.7 = (f32[2,2,96,96]{3,2,1,0:T(8,128)S(1)}, f32[2,2,96,96]{3,2,1,0:T(8,128)S(1)}, u32[]{:S(2)}, u32[]{:S(2)}) collective-permute-start(f32[2,2,96,96]{3,2,1,0:T(8,128)S(1)} %get-tuple-element.35), channel_id=1, source_target_pairs={{0,2},{2,4},{4,6},{6,8},{8,10},{10,12},{12,14},{14,16},{16,18},{18... | collective-permute-start | bytes 442376 | tf_op jit(solution)/shard_map/ppermute | solution.py:32
  162.2 113.0 %all-reduce.2.cloned.1.call-done = f32[2,192,192]{2,1,0:T(8,128)} async-done(((f32[2,192,192]{2,1,0:T(8,128)}), f32[2,192,192]{2,1,0:T(8,128)}) %all-reduce.2.cloned.1.call-update) | async-done | bytes 294928 | tf_op jit(solution)/shard_map/psum | solution.py:138
  275.2 1.8 multiply_subtract_fusion
  (67 shorter events, 36.3 us)
Async XLA Ops:
  7.2 24.0 %copy-start.4 = (f32[2,192,192]{2,1,0:T(8,128)S(1)}, f32[2,192,192]{2,1,0:T(8,128)}, u32[]{:S(2)}) copy-start(f32[2,192,192]{2,1,0:T(8,128)} %param.7) | copy-start | bytes 884740
  7.2 268.0 %all-reduce.2.cloned.1.call-start = ((), (), s32[]{:S(2)}) async-start(), calls=%async_computation | async-start | bytes 786432 | tf_op jit(solution)/shard_map/psum | solution.py:138
  7.2 17.6 %collective-permute-start.1 = (f32[2,2,96,96]{3,2,1,0:T(8,128)}, f32[2,2,96,96]{3,2,1,0:T(8,128)S(1)}, u32[]{:S(2)}, u32[]{:S(2)}) collective-permute-start(f32[2,2,96,96]{3,2,1,0:T(8,128)} %param.6), channel_id=1, source_target_pairs={{2,0},{4,2},{6,4},{8,6},{10,8},{12,10},{14,12},{16,14},{18,16},{20... | collective-permute-start | bytes 442376 | tf_op jit(solution)/shard_map/ppermute | solution.py:22
  8.7 15.2 %collective-permute-start = (f32[2,2,96,96]{3,2,1,0:T(8,128)}, f32[2,2,96,96]{3,2,1,0:T(8,128)S(1)}, u32[]{:S(2)}, u32[]{:S(2)}) collective-permute-start(f32[2,2,96,96]{3,2,1,0:T(8,128)} %param.6), channel_id=1, source_target_pairs={{0,2},{2,4},{4,6},{6,8},{8,10},{10,12},{12,14},{14,16},{16,18},{18... | collective-permute-start | bytes 442376 | tf_op jit(solution)/shard_map/ppermute | solution.py:20
  24.8 17.2 %collective-permute-start.3 = (f32[2,2,288,96]{3,2,1,0:T(8,128)S(1)}, f32[2,2,288,96]{3,2,1,0:T(8,128)S(1)}, u32[]{:S(2)}, u32[]{:S(2)}) collective-permute-start(f32[2,2,288,96]{3,2,1,0:T(8,128)S(1)} %constant_dynamic-update-slice_fusion), channel_id=1, source_target_pairs={{1,0},{3,2},{5,4},{7,6},{9,8},{11,10},{13,12},{15,14},{17,16},{19,... | collective-permute-start | bytes 1327112 | tf_op jit(solution)/shard_map/ppermute | solution.py:22
  26.1 17.7 %collective-permute-start.2 = (f32[2,2,288,96]{3,2,1,0:T(8,128)S(1)}, f32[2,2,288,96]{3,2,1,0:T(8,128)S(1)}, u32[]{:S(2)}, u32[]{:S(2)}) collective-permute-start(f32[2,2,288,96]{3,2,1,0:T(8,128)S(1)} %constant_dynamic-update-slice_fusion), channel_id=1, source_target_pairs={{0,1},{2,3},{4,5},{6,7},{8,9},{10,11},{12,13},{14,15},{16,17},{18,... | collective-permute-start | bytes 1327112 | tf_op jit(solution)/shard_map/ppermute | solution.py:20
  51.2 5.0 %copy-start.1 = (f32[2,2,2,192,192]{4,3,0,2,1:T(8,128)S(1)}, f32[2,2,2,192,192]{4,3,0,2,1:T(8,128)}, u32[]{:S(2)}) copy-start(f32[2,2,2,192,192]{4,3,0,2,1:T(8,128)} %get-tuple-element.9) | copy-start | bytes 3538948
  81.4 3.8 %copy-start = (f32[1,1,2,192,192]{4,3,2,1,0:T(8,128)S(1)}, f32[1,1,2,192,192]{4,3,2,1,0:T(8,128)}, u32[]{:S(2)}) copy-start(f32[1,1,2,192,192]{4,3,2,1,0:T(8,128)} %param.9) | copy-start | bytes 884740
  136.0 7.8 %copy-start.2 = (f32[1,2,192,192]{3,2,1,0:T(8,128)S(1)}, f32[1,2,192,192]{3,2,1,0:T(8,128)}, u32[]{:S(2)}) copy-start(f32[1,2,192,192]{3,2,1,0:T(8,128)} %get-tuple-element.20) | copy-start | bytes 884740
  136.1 7.7 %copy-start.3 = (f32[1,2,192,192]{3,2,1,0:T(8,128)S(1)}, f32[1,2,192,192]{3,2,1,0:T(8,128)}, u32[]{:S(2)}) copy-start(f32[1,2,192,192]{3,2,1,0:T(8,128)} %get-tuple-element.21) | copy-start | bytes 884740
  137.1 18.1 %collective-permute-start.4 = (f32[2,2,288,96]{3,2,1,0:T(8,128)}, f32[2,2,288,96]{3,2,1,0:T(8,128)S(1)}, u32[]{:S(2)}, u32[]{:S(2)}) collective-permute-start(f32[2,2,288,96]{3,2,1,0:T(8,128)} %get-tuple-element.26), channel_id=1, source_target_pairs={{1,0},{3,2},{5,4},{7,6},{9,8},{11,10},{13,12},{15,14},{17,16},{19,... | collective-permute-start | bytes 1327112 | tf_op jit(solution)/shard_map/ppermute | solution.py:32
  138.4 18.0 %collective-permute-start.5 = (f32[2,2,288,96]{3,2,1,0:T(8,128)S(1)}, f32[2,2,288,96]{3,2,1,0:T(8,128)}, u32[]{:S(2)}, u32[]{:S(2)}) collective-permute-start(f32[2,2,288,96]{3,2,1,0:T(8,128)S(1)} %get-tuple-element.27), channel_id=1, source_target_pairs={{0,1},{2,3},{4,5},{6,7},{8,9},{10,11},{12,13},{14,15},{16,17},{18,... | collective-permute-start | bytes 1327112 | tf_op jit(solution)/shard_map/ppermute | solution.py:32
  144.7 130.5 %copy-start.5 = (f32[2,192,192]{2,1,0:T(8,128)S(1)}, f32[2,192,192]{2,1,0:T(8,128)}, u32[]{:S(2)}) copy-start(f32[2,192,192]{2,1,0:T(8,128)} %param.7) | copy-start | bytes 884740
  157.6 119.3 %copy-start.6 = (f32[2,2,96,96]{3,2,1,0:T(8,128)S(1)}, f32[2,2,96,96]{3,2,1,0:T(8,128)}, u32[]{:S(2)}) copy-start(f32[2,2,96,96]{3,2,1,0:T(8,128)} %param.6) | copy-start | bytes 442372
  157.7 119.3 %collective-permute-start.6 = (f32[2,2,96,96]{3,2,1,0:T(8,128)S(1)}, f32[2,2,96,96]{3,2,1,0:T(8,128)S(1)}, u32[]{:S(2)}, u32[]{:S(2)}) collective-permute-start(f32[2,2,96,96]{3,2,1,0:T(8,128)S(1)} %get-tuple-element.34), channel_id=1, source_target_pairs={{2,0},{4,2},{6,4},{8,6},{10,8},{12,10},{14,12},{16,14},{18,16},{20... | collective-permute-start | bytes 442376 | tf_op jit(solution)/shard_map/ppermute | solution.py:32
  159.1 117.9 %collective-permute-start.7 = (f32[2,2,96,96]{3,2,1,0:T(8,128)S(1)}, f32[2,2,96,96]{3,2,1,0:T(8,128)S(1)}, u32[]{:S(2)}, u32[]{:S(2)}) collective-permute-start(f32[2,2,96,96]{3,2,1,0:T(8,128)S(1)} %get-tuple-element.35), channel_id=1, source_target_pairs={{0,2},{2,4},{4,6},{6,8},{8,10},{10,12},{12,14},{14,16},{16,18},{18... | collective-permute-start | bytes 442376 | tf_op jit(solution)/shard_map/ppermute | solution.py:32
Sparse Core Ops, SparseCore 0:
  144.8 130.3 all-reduce.1
where the time goes:
time: 288 us; the launch traced here: 285 us
  waiting for transfers between devices  137 us (48%)
  matrix products  66.4 us (23%)
  local copies, waits for them, and re-layouts  27.2 us (9%)
  between operations  23 us (8%)
  starting transfers between devices  21.9 us (8%)
  other arithmetic  8.57 us (3%)
    psum x1, waiting for transfers between devices, shards(): total = lax.psum(wave_gradient, ('row', 'col'))  113 us
    dot_general x24, matrix products, on_left(): return jnp.einsum('jk,...kl->...jl', matrix, value, precision=highest)  35 us
    dot_general x24, matrix products, on_right(): return jnp.einsum('...jk,kl->...jl', value, matrix, precision=highest)  31.4 us
    dynamic_update_slice x2, local copies, waits for them, and re-layouts, shards(): lax.dynamic_update_slice(grad_pad, previous + position_weight * object_te...  15.6 us
    ppermute x4, waiting for transfers between devices, passed_along(): return lax.ppermute(x, axis, pairs)  11.7 us
    ppermute x4, starting transfers between devices, passed_along(): return lax.ppermute(x, axis, pairs)  11.2 us
    ppermute x2, waiting for transfers between devices, extended(): lax.ppermute(head, axis, [((i + 1) % count, i) for i in range(ends)])  10.8 us
    ppermute x2, starting transfers between devices, extended(): lax.ppermute(tail, axis, [(i, (i + 1) % count) for i in range(ends)])  8.02 us
  transfers between devices with their start and end apart: 9, of which 5 were waited for; matrix products, arithmetic and copies ran while one was open for 3% of the time, Pallas kernels for 0%

commit v1 on v0

v1 whole, which is shorter than its diff:
```python
import functools
import math

import jax
import jax.numpy as jnp
import numpy as np
from jax import lax
from jax.experimental import pallas as pl
from jax.experimental.pallas import tpu as pltpu
from jax.sharding import Mesh
from jax.sharding import PartitionSpec as P

object_rate = 0.02
probe_rate = 0.3

LANES = 128
f32 = jnp.float32
bf16 = jnp.bfloat16
VMEM = pl.BlockSpec(memory_space=pltpu.VMEM)
SMEM = pl.BlockSpec(memory_space=pltpu.SMEM)


def round_up(value, unit):
    return -(-value // unit) * unit


def split_matrices(width, padded):
    k = np.arange(width)
    angle = (k[:, None] * k[None, :] % width) * (2.0 * math.pi / width)
    cosine = np.cos(angle) / math.sqrt(width)
    sine = np.sin(angle) / math.sqrt(width)
    right = np.zeros((2, padded, 2, padded))
    right[0, :width, 0, :width] = cosine
    right[0, :width, 1, :width] = -sine
    right[1, :width, 0, :width] = sine
    right[1, :width, 1, :width] = cosine
    right = right.reshape(2 * padded, 2 * padded)
    left = np.block([[cosine, sine], [-sine, cosine]])

    def halves(matrix):
        high = matrix.astype(np.float32).astype(bf16)
        low = (matrix - high.astype(np.float64)).astype(np.float32).astype(bf16)
        return high, low

    right_high, right_low = halves(right)
    left_high, left_low = halves(left)
    return (
        np.concatenate([right_high, right_high, right_low], 0),
        np.concatenate([left_high, left_high, left_low], 1),
    )


def times(a_real, a_imag, b_real, b_imag):
    return (a_real * b_real - a_imag * b_imag, a_real * b_imag + a_imag * b_real)


def times_conj(a_real, a_imag, b_real, b_imag):
    return (a_real * b_real + a_imag * b_imag, a_real * b_imag - a_imag * b_real)


def halves_of(value):
    high = value.astype(bf16)
    return high, (value - high.astype(f32)).astype(bf16)


def lane_ids(rows):
    return lax.broadcasted_iota(jnp.int32, (rows, LANES), 1)


def pack_strip_kernel(own_ref, other_ref, out_ref):
    tile = own_ref.shape[2]
    first = lax.axis_index("col") == 0
    lane = lane_ids(tile)
    pad = jnp.zeros((tile, LANES - tile), f32)
    ends = []
    for plane in range(4):
        own = jnp.concatenate([own_ref[plane // 2, plane % 2], pad], 1)
        other = jnp.concatenate([other_ref[plane // 2, plane % 2], pad], 1)
        head = jnp.where(first, own, other)
        tail = pltpu.roll(jnp.where(first, other, own), tile, 1)
        out_ref[:, plane * LANES : (plane + 1) * LANES] = jnp.where(lane < tile, head, tail)
        ends.append(tail)
    half = LANES // 2
    for pair in range(2):
        even, odd = ends[2 * pair], ends[2 * pair + 1]
        out_ref[:, (4 + pair) * LANES : (5 + pair) * LANES] = jnp.where(
            lane < half, even, pltpu.roll(odd, half, 1)
        )


def unpack_strip(strip_ref, obj_ref, row):
    tile = strip_ref.shape[0]
    rows = pl.ds(row, tile)
    half = LANES // 2
    lane = lane_ids(tile)
    zero = jnp.zeros((tile, LANES), f32)
    for plane in range(4):
        obj_ref[plane, 1, rows, :] = strip_ref[:, plane * LANES : (plane + 1) * LANES]
        end = strip_ref[:, (4 + plane // 2) * LANES : (5 + plane // 2) * LANES]
        if plane % 2:
            end = pltpu.roll(end, half, 1)
        obj_ref[plane, 2, rows, :] = jnp.where(lane < half, end, zero)


def pack_strip(acc_ref, out_ref, row):
    tile = out_ref.shape[0]
    rows = pl.ds(row, tile)
    half = LANES // 2
    lane = lane_ids(tile)
    for plane in range(4):
        out_ref[:, plane * LANES : (plane + 1) * LANES] = acc_ref[plane, 1, rows, :]
    for pair in range(2):
        even = acc_ref[2 * pair, 2, rows, :]
        odd = pltpu.roll(acc_ref[2 * pair + 1, 2, rows, :], half, 1)
        out_ref[:, (4 + pair) * LANES : (5 + pair) * LANES] = jnp.where(lane < half, even, odd)


def unpack_wide(strip_ref, obj_ref, row):
    tile = strip_ref.shape[1]
    for plane in range(4):
        for j in range(3):
            obj_ref[plane, j, pl.ds(row, tile), :] = strip_ref[
                plane, :, j * LANES : (j + 1) * LANES
            ]


def pack_wide(acc_ref, out_ref, row):
    tile = out_ref.shape[1]
    for plane in range(4):
        for j in range(3):
            out_ref[plane, :, j * LANES : (j + 1) * LANES] = acc_ref[
                plane, j, pl.ds(row, tile), :
            ]


def position_kernel(
    paired,
    offsets_ref,
    counts_ref,
    above_ref,
    middle_ref,
    below_ref,
    wave_ref,
    trans_ref,
    measured_ref,
    right_ref,
    left_ref,
    top_out,
    middle_out,
    bottom_out,
    probe_out,
    obj,
    acc,
    window,
    carried,
    data,
    mid,
    field,
):
    slots = measured_ref.shape[0]
    width = wave_ref.shape[1]
    padded = wave_ref.shape[2]
    tile = obj.shape[2] // 3
    unpack, pack = (unpack_strip, pack_strip) if paired else (unpack_wide, pack_wide)
    zero_tiles = (0, 3) if paired else (3,)
    for plane in range(4):
        for j in zero_tiles:
            obj[plane, j] = jnp.zeros((3 * tile, LANES), f32)
    unpack(above_ref, obj, 0)
    unpack(middle_ref, obj, tile)
    unpack(below_ref, obj, 2 * tile)
    acc[...] = jnp.zeros(acc.shape, f32)

    shift = tile - width // 2
    base = LANES - tile if paired else 0
    if paired:
        base = base + lax.axis_index("col") * tile
    corners = []
    for slot in range(slots):
        row = offsets_ref[0, 0, slot, 0] + shift
        column = offsets_ref[0, 0, slot, 1] + shift + base
        corners.append((row, column // LANES, column % LANES))

    chunk = width // 2
    lane = lane_ids(chunk)
    for slot in range(slots):
        row, first, lanes = corners[slot]
        back = lax.rem(LANES - lanes, LANES)
        for plane in range(4):
            for start in range(0, width, chunk):
                parts = [
                    pltpu.roll(obj[plane, first + j, pl.ds(row + start, chunk), :], back, 1)
                    for j in range(3)
                ]
                for j in range(2):
                    window[plane, pl.ds(slot * width + start, chunk), j * LANES : (j + 1) * LANES] = (
                        jnp.where(lane < LANES - lanes, parts[j], parts[j + 1])
                    )

    total = slots * width
    step = 48
    chunks = [(s, s % width) for s in range(0, total, step)]

    def put(start, a, b):
        rows = pl.ds(start, step)
        for j, value in enumerate((a, b)):
            high, low = halves_of(value)
            data[rows, j * padded : (j + 1) * padded] = high
            data[rows, (2 + j) * padded : (3 + j) * padded] = low

    def transform():
        for j in range(2):
            columns = slice(j * padded, (j + 1) * padded)
            out = jnp.dot(
                data[...], right_ref[: 4 * padded, columns], preferred_element_type=f32
            ) + jnp.dot(
                data[:, : 2 * padded], right_ref[4 * padded :, columns], preferred_element_type=f32
            )
            high, low = halves_of(out)
            for slot in range(slots):
                rows = slice(slot * width, (slot + 1) * width)
                mid[slot, j * width : (j + 1) * width, :] = high[rows]
                mid[slot, (2 + j) * width : (3 + j) * width, :] = low[rows]
        for slot in range(slots):
            out = jnp.dot(
                left_ref[:, : 4 * width], mid[slot], preferred_element_type=f32
            ) + jnp.dot(
                left_ref[:, 4 * width :], mid[slot, : 2 * width], preferred_element_type=f32
            )
            for j in range(2):
                field[j, slot * width : (slot + 1) * width, :] = out[j * width : (j + 1) * width]

    def at(ref, first, start):
        rows = pl.ds(start, step)
        return ref[first, rows, :], ref[first + 1, rows, :]

    for start, inner in chunks:
        real, imag = times(*at(wave_ref, 0, inner), *at(window, 0, start))
        put(start, real, imag)
    transform()
    for start, inner in chunks:
        real, imag = times(*at(trans_ref, 0, inner), *at(field, 0, start))
        put(start, imag, real)
    transform()
    for start, inner in chunks:
        imag, real = at(field, 0, start)
        rows = pl.ds(start, step)
        carried[0, rows, :] = real
        carried[1, rows, :] = imag
        real, imag = times(real, imag, *at(window, 2, start))
        put(start, real, imag)
    transform()
    for start, inner in chunks:
        real, imag = at(field, 0, start)
        residual = real * real + imag * imag - measured_ref[start // width, pl.ds(inner, step), :]
        put(start, residual * imag, residual * real)
    transform()
    for start, inner in chunks:
        imag, real = at(field, 0, start)
        rows = pl.ds(start, step)
        second = times_conj(*at(carried, 0, start), real, imag)
        before_real, before_imag = times_conj(*at(window, 2, start), real, imag)
        put(start, before_real, before_imag)
        window[2, rows, :] = second[0]
        window[3, rows, :] = second[1]
    transform()
    for start, inner in chunks:
        real, imag = times_conj(*at(trans_ref, 0, inner), *at(field, 0, start))
        put(start, imag, real)
    transform()

    live = [(slot < counts_ref[0, 0]).astype(f32) for slot in range(slots)]
    core = lax.rem(lax.axis_index("row"), 2)
    half_lanes = lane_ids(step) < LANES // 2
    for inner in range(0, width, step):
        sum_real = jnp.zeros((step, padded), f32)
        sum_imag = jnp.zeros((step, padded), f32)
        for slot in range(slots):
            start = slot * width + inner
            rows = pl.ds(start, step)
            imag, real = at(field, 0, start)
            grad_real, grad_imag = times_conj(*at(window, 0, start), real, imag)
            sum_real = sum_real + live[slot] * grad_real
            sum_imag = sum_imag + live[slot] * grad_imag
            first_real, first_imag = times_conj(*at(wave_ref, 0, inner), real, imag)
            window[0, rows, :] = first_real
            window[1, rows, :] = first_imag
        blocks = (
            sum_real[:, :LANES],
            sum_imag[:, :LANES],
            jnp.where(
                half_lanes,
                sum_real[:, LANES:],
                pltpu.roll(sum_imag[:, LANES:], LANES // 2, 1),
            ),
        )
        for j, block in enumerate(blocks):
            probe_out[pl.ds(j * width + inner, step), :] = block

    for slot in range(slots):
        row, first, lanes = corners[slot]
        inside = lane >= lanes
        for plane in range(4):
            for start in range(0, width, chunk):
                rows = pl.ds(slot * width + start, chunk)
                target = pl.ds(row + start, chunk)
                parts = [
                    pltpu.roll(
                        live[slot] * window[plane, rows, j * LANES : (j + 1) * LANES], lanes, 1
                    )
                    for j in range(2)
                ]
                zero = jnp.zeros((chunk, LANES), f32)
                pieces = (
                    jnp.where(inside, parts[0], zero),
                    jnp.where(inside, parts[1], parts[0]),
                    jnp.where(inside, zero, parts[1]),
                )
                for j, piece in enumerate(pieces):
                    acc[plane, first + j, target, :] = acc[plane, first + j, target, :] + piece
    pack(acc, top_out, 0)
    pack(acc, middle_out, tile)
    pack(acc, bottom_out, 2 * tile)


def fold_kernel(middle_ref, below_ref, above_ref, own_out, other_out):
    tile = middle_ref.shape[0]
    first = lax.axis_index("col") == 0
    half = LANES // 2
    lane = lane_ids(tile)

    def total(j):
        columns = slice(j * LANES, (j + 1) * LANES)
        return middle_ref[:, columns] + below_ref[:, columns] + above_ref[:, columns]

    ends = [total(4), total(5)]
    for plane in range(4):
        head = total(plane)
        end = ends[plane // 2]
        if plane % 2:
            end = pltpu.roll(end, half, 1)
        tail = pltpu.roll(jnp.where(lane < tile, end, head), LANES - tile, 1)
        own_out[plane] = jnp.where(first, head, tail)
        other_out[plane] = jnp.where(first, tail, head)


def update_kernel(object_ref, own_ref, other_ref, out_ref):
    tile = object_ref.shape[2]
    for plane in range(4):
        grad = own_ref[plane] + other_ref[plane]
        out_ref[plane // 2, plane % 2] = (
            object_ref[plane // 2, plane % 2] - object_rate * grad[:, :tile]
        )


def probe_kernel(rate, probe_ref, total_ref, out_ref):
    width = probe_ref.shape[1]
    rest = width - LANES
    last = total_ref[2 * width :]
    for j in range(2):
        out_ref[j, :, :LANES] = probe_ref[j, :, :LANES] - rate * total_ref[j * width : (j + 1) * width]
        end = last if j == 0 else pltpu.roll(last, LANES // 2, 1)
        out_ref[j, :, LANES:] = probe_ref[j, :, LANES:] - rate * end[:, :rest]


def passed_along(x, axis, by):
    peers = lax.axis_size(axis)
    pairs = [(i, i + by) for i in range(peers) if 0 <= i + by < peers]
    return lax.ppermute(x, axis, pairs)


def all_sum(x, group):
    count = math.prod(lax.axis_size(axis) for axis in group)
    rows, lanes = x.shape
    piece = -(-rows // count)
    x = jnp.pad(x, ((0, piece * count - rows), (0, 0))).reshape(count, piece, lanes)
    x = lax.all_to_all(x, group, 0, 0, tiled=True)
    x = jnp.broadcast_to(jnp.sum(x, 0)[None], x.shape)
    x = lax.all_to_all(x, group, 0, 0, tiled=True)
    return x.reshape(count * piece, lanes)[:rows]


def shards(object_slices, probe, propagator_phase, measured, offsets, counts):
    tile = object_slices.shape[-1]
    width = probe.shape[-1]
    padded = round_up(width, LANES)
    slots = measured.shape[2]
    rows_count = lax.axis_size("row")
    cols_count = lax.axis_size("col")
    devices = rows_count * cols_count
    paired = cols_count == 2
    right, left = split_matrices(width, padded)
    params = pltpu.CompilerParams(vmem_limit_bytes=60 * 1024 * 1024)

    if paired:
        other = lax.ppermute(object_slices, "col", [(0, 1), (1, 0)])
        middle = pl.pallas_call(
            pack_strip_kernel,
            out_shape=jax.ShapeDtypeStruct((tile, 6 * LANES), f32),
            in_specs=[VMEM, VMEM],
            out_specs=VMEM,
        )(object_slices, other)
    else:
        cells = object_slices.reshape(4, tile, tile)
        middle = jnp.concatenate(
            [passed_along(cells, "col", 1), cells, passed_along(cells, "col", -1)], -1
        )
        middle = jnp.pad(middle, ((0, 0), (0, 0), (0, 3 * LANES - 3 * tile)))
    above = passed_along(middle, "row", 1)
    below = passed_along(middle, "row", -1)

    edge = ((0, 0), (0, 0), (0, padded - width))
    wave = jnp.pad(probe, edge)
    trans = jnp.pad(jnp.stack([jnp.cos(propagator_phase), jnp.sin(propagator_phase)]), edge)
    intensities = jnp.pad(measured[0, 0], edge)

    total = slots * width
    strip = jax.ShapeDtypeStruct(middle.shape, f32)
    top, center, bottom, terms = pl.pallas_call(
        functools.partial(position_kernel, paired),
        out_shape=[strip, strip, strip, jax.ShapeDtypeStruct((3 * width, LANES), f32)],
        in_specs=[SMEM, SMEM] + [VMEM] * 8,
        out_specs=[VMEM] * 4,
        scratch_shapes=[
            pltpu.VMEM((4, 4, 3 * tile, LANES), f32),
            pltpu.VMEM((4, 4, 3 * tile, LANES), f32),
            pltpu.VMEM((4, total, padded), f32),
            pltpu.VMEM((2, total, padded), f32),
            pltpu.VMEM((total, 4 * padded), bf16),
            pltpu.VMEM((slots, 4 * width, padded), bf16),
            pltpu.VMEM((2, total, padded), f32),
        ],
        compiler_params=params,
    )(offsets, counts, above, middle, below, wave, trans, intensities, right, left)

    from_below = passed_along(top, "row", -1)
    from_above = passed_along(bottom, "row", 1)
    all_terms = all_sum(terms, ("row", "col"))
    if paired:
        share = jax.ShapeDtypeStruct((4, tile, LANES), f32)
        mine, theirs = pl.pallas_call(
            fold_kernel,
            out_shape=[share, share],
            in_specs=[VMEM] * 3,
            out_specs=[VMEM] * 2,
        )(center, from_below, from_above)
        received = lax.ppermute(theirs, "col", [(0, 1), (1, 0)])
        object_out = pl.pallas_call(
            update_kernel,
            out_shape=jax.ShapeDtypeStruct(object_slices.shape, f32),
            in_specs=[VMEM] * 3,
            out_specs=VMEM,
        )(object_slices, mine, received)
    else:
        folded = center + from_below + from_above
        folded = (
            folded[:, :, tile : 2 * tile]
            + passed_along(folded[:, :, :tile], "col", -1)
            + passed_along(folded[:, :, 2 * tile : 3 * tile], "col", 1)
        )
        object_out = object_slices - object_rate * folded.reshape(object_slices.shape)
    probe_out = pl.pallas_call(
        functools.partial(probe_kernel, probe_rate / (slots * devices)),
        out_shape=jax.ShapeDtypeStruct(probe.shape, f32),
        in_specs=[VMEM] * 2,
        out_specs=VMEM,
    )(probe, all_terms)
    return (object_out, probe_out)


def solution(mesh):
    return jax.shard_map(
        shards,
        mesh=mesh,
        in_specs=(
            P(None, None, "row", "col"),
            P(),
            P(),
            P("row", "col", None, None, None),
            P("row", "col", None, None),
            P("row", "col"),
        ),
        out_specs=(P(None, None, "row", "col"), P()),
        check_vma=False,
    )
```

time: 288 us -> 87.2 us (0.30)
  the two profiles are of different devices: /device:TPU:0 before, /device:TPU:14 now
where the time goes in v1:
time: 87.2 us; the launch traced here: 86.7 us
  waiting for transfers between devices  23.9 us (27%)
  Pallas kernels  20.4 us (23%)
  starting transfers between devices  15.6 us (18%)
  blocking collectives  15 us (17%)
  local copies, waits for them, and re-layouts  9.55 us (11%)
  between operations  1.39 us (2%)
    ppermute x4, waiting for transfers between devices, passed_along(): return lax.ppermute(x, axis, pairs)  15.6 us
    all_to_all x1, blocking collectives, all_sum(): x = lax.all_to_all(x, group, 0, 0, tiled=True)  15 us
    pallas_call x1, Pallas kernels, shards(): pl.pallas_call(functools.partial(position_kernel, paired), out_shape=[str...  12.7 us
    ppermute x4, starting transfers between devices, passed_along(): return lax.ppermute(x, axis, pairs)  8.64 us
    ppermute x1, waiting for transfers between devices, shards(): received = lax.ppermute(theirs, 'col', [(0, 1), (1, 0)])  6.08 us
    all_to_all x1, starting transfers between devices, all_sum(): x = lax.all_to_all(x, group, 0, 0, tiled=True)  5.56 us
    unnamed x18, local copies, waits for them, and re-layouts  2.77 us
    ppermute x1, waiting for transfers between devices, shards(): other = lax.ppermute(object_slices, 'col', [(0, 1), (1, 0)])  2.16 us
  transfers between devices with their start and end apart: 7, of which 6 were waited for; matrix products, arithmetic and copies ran while one was open for 6% of the time, Pallas kernels for 4%

profile of v1, /device:TPU:14, one launch (start us, length us, event | category | flops | bytes accessed | tf_op | source)
XLA Modules:
  0.0 86.7 jit_solution(7251919381883585866)
XLA Ops:
  0.6 0.0 copy-start.4
  0.6 0.6 collective-permute-start
  1.9 1.8 %pad.12.measured_ref = f32[2,192,256]{2,1,0:T(8,128)} pad(f32[2,192,192]{2,1,0:T(8,128)} %bitcast.5, f32[]{:T(128)} %constant.3.clone.1), padding=0_0x0_0x0_64 | pad | bytes 688132 | tf_op jit(solution)/shard_map/jit(_pad)/pad | solution.py:415
  3.6 1.8 %pad.10.wave_ref = f32[2,192,256]{2,1,0:T(8,128)} pad(f32[2,192,192]{2,1,0:T(8,128)} %probe_ref.1, f32[]{:T(128)} %constant.3.clone.1), padding=0_0x0_0x0_64 | pad | bytes 688132 | tf_op jit(solution)/shard_map/jit(_pad)/pad | solution.py:413
  5.4 2.2 %collective-permute-done.other_ref = f32[2,2,96,96]{3,2,1,0:T(8,128)S(1)} collective-permute-done((f32[2,2,96,96]{3,2,1,0:T(8,128)}, f32[2,2,96,96]{3,2,1,0:T(8,128)S(1)}, u32[]{:S(2)}, u32[]{:S(2)}) %collective-permute-start) | collective-permute-done | bytes 147488 | tf_op jit(solution)/shard_map/ppermute | solution.py:396
  7.6 0.0 copy-start.5
  7.6 0.7 copy-done.5
  8.2 1.9 %shard_map.95.middle_ref = f32[96,768]{1,0:T(8,128)} custom-call(f32[2,2,96,96]{3,2,1,0:T(8,128)} %object_ref.1, f32[2,2,96,96]{3,2,1,0:T(8,128)} %copy-done.5), custom_call_target="tpu_custom_call" | custom-call | tf_op jit(solution)/shard_map/pallas_call | solution.py:397
  10.2 1.9 %collective-permute-start.2 = (f32[96,768]{1,0:T(8,128)}, f32[96,768]{1,0:T(8,128)S(1)}, u32[]{:S(2)}, u32[]{:S(2)}) collective-permute-start(f32[96,768]{1,0:T(8,128)} %shard_map.95.middle_ref), channel_id=1, source_target_pairs={{2,0},{4,2},{6,4},{8,6},{10,8},{12,10},{14,12},{16,14},{18,16},{20... | collective-permute-start | bytes 884744 | tf_op jit(solution)/shard_map/ppermute | solution.py:369
  12.1 2.4 %collective-permute-start.1 = (f32[96,768]{1,0:T(8,128)}, f32[96,768]{1,0:T(8,128)S(1)}, u32[]{:S(2)}, u32[]{:S(2)}) collective-permute-start(f32[96,768]{1,0:T(8,128)} %shard_map.95.middle_ref), channel_id=1, source_target_pairs={{0,2},{2,4},{4,6},{6,8},{8,10},{10,12},{12,14},{14,16},{16,18},{18... | collective-permute-start | bytes 884744 | tf_op jit(solution)/shard_map/ppermute | solution.py:369
  14.5 0.0 copy-done.4
  14.5 0.7 cosine_bitcast_fusion
  15.2 0.8 select_maximum_fusion.trans_ref
  16.0 3.8 %collective-permute-done.2.below_ref = f32[96,768]{1,0:T(8,128)S(1)} collective-permute-done((f32[96,768]{1,0:T(8,128)}, f32[96,768]{1,0:T(8,128)S(1)}, u32[]{:S(2)}, u32[]{:S(2)}) %collective-permute-start.2) | collective-permute-done | bytes 294944 | tf_op jit(solution)/shard_map/ppermute | solution.py:369
  19.8 0.0 copy-start.2
  19.8 1.9 %collective-permute-done.1.above_ref = f32[96,768]{1,0:T(8,128)S(1)} collective-permute-done((f32[96,768]{1,0:T(8,128)}, f32[96,768]{1,0:T(8,128)S(1)}, u32[]{:S(2)}, u32[]{:S(2)}) %collective-permute-start.1) | collective-permute-done | bytes 294944 | tf_op jit(solution)/shard_map/ppermute | solution.py:369
  21.7 0.0 copy-done.2
  21.7 0.0 copy-start.3
  21.7 0.7 copy-done.3
  22.4 12.7 %shard_map.96 = (f32[96,768]{1,0:T(8,128)}, f32[96,768]{1,0:T(8,128)}, f32[96,768]{1,0:T(8,128)}, f32[576,128]{1,0:T(8,128)}) custom-call(s32[1,1,2,2]{3,2,1,0:T(2,128)} %offsets_ref.1, s32[1,1]{1,0:T(1,128)S(6)} %copy.10.counts_ref, f32[96,768]{1,0:T(8,128)} %copy-done.3, f32[96,768]{1,0:T(8,128)} %shard_map.95.middle_ref, f32[96,768]{1,0:T(8,128)} %copy-done.2, ...), custom_call_target="tpu_custom_call" | custom-call | tf_op jit(solution)/shard_map/pallas_call | solution.py:419
  35.1 0.0 copy-start.8
  35.1 0.0 copy-start.7
  35.1 1.0 %reshape.11 = f32[32,18,128]{2,1,0:T(8,128)S(1)} reshape(f32[576,128]{1,0:T(8,128)} %get-tuple-element.13) | data formatting | bytes 589824 | tf_op jit(solution)/shard_map/reshape | solution.py:376
  36.2 15.0 %all_to_all.10 = f32[32,18,128]{2,1,0:T(8,128)S(1)} all-to-all(f32[32,18,128]{2,1,0:T(8,128)S(1)} %reshape.11), channel_id=1, replica_groups=mesh['row'=16,'col'=2] {'row','col'}, dimensions={0} | all-to-all | bytes 589824 | tf_op jit(solution)/shard_map/all_to_all | solution.py:377
  51.2 0.8 broadcast_in_dim.2
  52.0 5.6 %all-to-all-start.1 = ((f32[32,18,128]{2,1,0:T(8,128)}), f32[32,18,128]{2,1,0:T(8,128)S(1)}, u32[]{:S(2)}, u32[]{:S(2)}) async-start(f32[32,18,128]{2,1,0:T(8,128)} %broadcast_in_dim.2), calls=%async_computation.1 | async-start | bytes 786432 | tf_op jit(solution)/shard_map/all_to_all | solution.py:379
  57.6 0.0 copy-done.8
  57.6 2.2 %collective-permute-start.3 = (f32[96,768]{1,0:T(8,128)S(1)}, f32[96,768]{1,0:T(8,128)S(1)}, u32[]{:S(2)}, u32[]{:S(2)}) collective-permute-start(f32[96,768]{1,0:T(8,128)S(1)} %copy-done.8), channel_id=1, source_target_pairs={{2,0},{4,2},{6,4},{8,6},{10,8},{12,10},{14,12},{16,14},{18,16},{20... | collective-permute-start | bytes 884744 | tf_op jit(solution)/shard_map/ppermute | solution.py:369
  59.8 0.0 copy-done.7
  59.8 2.1 %collective-permute-start.4 = (f32[96,768]{1,0:T(8,128)S(1)}, f32[96,768]{1,0:T(8,128)S(1)}, u32[]{:S(2)}, u32[]{:S(2)}) collective-permute-start(f32[96,768]{1,0:T(8,128)S(1)} %copy-done.7), channel_id=1, source_target_pairs={{0,2},{2,4},{4,6},{6,8},{8,10},{10,12},{12,14},{14,16},{16,18},{18... | collective-permute-start | bytes 884744 | tf_op jit(solution)/shard_map/ppermute | solution.py:369
  61.9 7.3 %collective-permute-done.3.below_ref = f32[96,768]{1,0:T(8,128)S(1)} collective-permute-done((f32[96,768]{1,0:T(8,128)S(1)}, f32[96,768]{1,0:T(8,128)S(1)}, u32[]{:S(2)}, u32[]{:S(2)}) %collective-permute-start.3) | collective-permute-done | bytes 294944 | tf_op jit(solution)/shard_map/ppermute | solution.py:369
  69.3 0.0 copy-start
  69.3 2.6 %collective-permute-done.4.above_ref = f32[96,768]{1,0:T(8,128)S(1)} collective-permute-done((f32[96,768]{1,0:T(8,128)S(1)}, f32[96,768]{1,0:T(8,128)S(1)}, u32[]{:S(2)}, u32[]{:S(2)}) %collective-permute-start.4) | collective-permute-done | bytes 294944 | tf_op jit(solution)/shard_map/ppermute | solution.py:369
  71.9 0.0 copy-start.1
  71.9 0.0 copy-done
  71.9 0.7 copy-done.1
  72.6 2.1 %shard_map.97 = (f32[4,96,128]{2,1,0:T(8,128)}, f32[4,96,128]{2,1,0:T(8,128)}) custom-call(f32[96,768]{1,0:T(8,128)} %get-tuple-element.8.middle_ref, f32[96,768]{1,0:T(8,128)} %copy-done, f32[96,768]{1,0:T(8,128)} %copy-done.1), custom_call_target="tpu_custom_call" | custom-call | tf_op jit(solution)/shard_map/pallas_call | solution.py:441
  74.7 0.8 collective-permute-start.5
  75.5 6.1 %collective-permute-done.5.other_ref = f32[4,96,128]{2,1,0:T(8,128)S(1)} collective-permute-done((f32[4,96,128]{2,1,0:T(8,128)}, f32[4,96,128]{2,1,0:T(8,128)S(1)}, u32[]{:S(2)}, u32[]{:S(2)}) %collective-permute-start.5) | collective-permute-done | bytes 196640 | tf_op jit(solution)/shard_map/ppermute | solution.py:447
  81.5 0.0 copy-start.6
  81.5 0.7 copy-done.6
  82.2 1.8 %shard_map.98 = f32[2,2,96,96]{3,2,1,0:T(8,128)} custom-call(f32[2,2,96,96]{3,2,1,0:T(8,128)} %object_ref.1, f32[4,96,128]{2,1,0:T(8,128)} %get-tuple-element.11.own_ref, f32[4,96,128]{2,1,0:T(8,128)} %copy-done.6), custom_call_target="tpu_custom_call" | custom-call | tf_op jit(solution)/shard_map/pallas_call | solution.py:448
  84.0 0.0 all-to-all-done.1
  84.0 0.7 reshape.12.total_ref
  84.8 1.9 %shard_map.99 = f32[2,192,192]{2,1,0:T(8,128)} custom-call(f32[2,192,192]{2,1,0:T(8,128)} %probe_ref.1, f32[576,128]{1,0:T(8,128)} %reshape.12.total_ref), custom_call_target="tpu_custom_call" | custom-call | tf_op jit(solution)/shard_map/pallas_call | solution.py:462
  (1 shorter events, 0.0 us)
Async XLA Ops:
  0.6 13.9 %copy-start.4 = (f32[192,192]{1,0:T(8,128)S(1)}, f32[192,192]{1,0:T(8,128)}, u32[]{:S(2)}) copy-start(f32[192,192]{1,0:T(8,128)} %param.10) | copy-start | bytes 442372
  0.6 6.9 %collective-permute-start = (f32[2,2,96,96]{3,2,1,0:T(8,128)}, f32[2,2,96,96]{3,2,1,0:T(8,128)S(1)}, u32[]{:S(2)}, u32[]{:S(2)}) collective-permute-start(f32[2,2,96,96]{3,2,1,0:T(8,128)} %object_ref.1), channel_id=1, source_target_pairs={{0,1},{1,0},{2,3},{3,2},{4,5},{5,4},{6,7},{7,6},{8,9},{9,8},{10,11... | collective-permute-start | bytes 442376 | tf_op jit(solution)/shard_map/ppermute | solution.py:396
  7.6 0.7 copy-start.5
  10.2 9.6 %collective-permute-start.2 = (f32[96,768]{1,0:T(8,128)}, f32[96,768]{1,0:T(8,128)S(1)}, u32[]{:S(2)}, u32[]{:S(2)}) collective-permute-start(f32[96,768]{1,0:T(8,128)} %shard_map.95.middle_ref), channel_id=1, source_target_pairs={{2,0},{4,2},{6,4},{8,6},{10,8},{12,10},{14,12},{16,14},{18,16},{20... | collective-permute-start | bytes 884744 | tf_op jit(solution)/shard_map/ppermute | solution.py:369
  12.1 9.6 %collective-permute-start.1 = (f32[96,768]{1,0:T(8,128)}, f32[96,768]{1,0:T(8,128)S(1)}, u32[]{:S(2)}, u32[]{:S(2)}) collective-permute-start(f32[96,768]{1,0:T(8,128)} %shard_map.95.middle_ref), channel_id=1, source_target_pairs={{0,2},{2,4},{4,6},{6,8},{8,10},{10,12},{12,14},{14,16},{16,18},{18... | collective-permute-start | bytes 884744 | tf_op jit(solution)/shard_map/ppermute | solution.py:369
  19.8 1.9 %copy-start.2 = (f32[96,768]{1,0:T(8,128)}, f32[96,768]{1,0:T(8,128)S(1)}, u32[]{:S(2)}) copy-start(f32[96,768]{1,0:T(8,128)S(1)} %collective-permute-done.2.below_ref) | copy-start | bytes 884740
  21.7 0.7 copy-start.3
  35.1 22.5 %copy-start.8 = (f32[96,768]{1,0:T(8,128)S(1)}, f32[96,768]{1,0:T(8,128)}, u32[]{:S(2)}) copy-start(f32[96,768]{1,0:T(8,128)} %get-tuple-element.9) | copy-start | bytes 884740
  35.1 24.7 %copy-start.7 = (f32[96,768]{1,0:T(8,128)S(1)}, f32[96,768]{1,0:T(8,128)}, u32[]{:S(2)}) copy-start(f32[96,768]{1,0:T(8,128)} %get-tuple-element.10) | copy-start | bytes 884740
  52.0 32.0 %all-to-all-start.1 = ((f32[32,18,128]{2,1,0:T(8,128)}), f32[32,18,128]{2,1,0:T(8,128)S(1)}, u32[]{:S(2)}, u32[]{:S(2)}) async-start(f32[32,18,128]{2,1,0:T(8,128)} %broadcast_in_dim.2), calls=%async_computation.1 | async-start | bytes 786432 | tf_op jit(solution)/shard_map/all_to_all | solution.py:379
  57.6 11.7 %collective-permute-start.3 = (f32[96,768]{1,0:T(8,128)S(1)}, f32[96,768]{1,0:T(8,128)S(1)}, u32[]{:S(2)}, u32[]{:S(2)}) collective-permute-start(f32[96,768]{1,0:T(8,128)S(1)} %copy-done.8), channel_id=1, source_target_pairs={{2,0},{4,2},{6,4},{8,6},{10,8},{12,10},{14,12},{16,14},{18,16},{20... | collective-permute-start | bytes 884744 | tf_op jit(solution)/shard_map/ppermute | solution.py:369
  59.8 12.1 %collective-permute-start.4 = (f32[96,768]{1,0:T(8,128)S(1)}, f32[96,768]{1,0:T(8,128)S(1)}, u32[]{:S(2)}, u32[]{:S(2)}) collective-permute-start(f32[96,768]{1,0:T(8,128)S(1)} %copy-done.7), channel_id=1, source_target_pairs={{0,2},{2,4},{4,6},{6,8},{8,10},{10,12},{12,14},{14,16},{16,18},{18... | collective-permute-start | bytes 884744 | tf_op jit(solution)/shard_map/ppermute | solution.py:369
  69.3 2.6 %copy-start = (f32[96,768]{1,0:T(8,128)}, f32[96,768]{1,0:T(8,128)S(1)}, u32[]{:S(2)}) copy-start(f32[96,768]{1,0:T(8,128)S(1)} %collective-permute-done.3.below_ref) | copy-start | bytes 884740
  71.9 0.7 copy-start.1
  74.7 6.9 %collective-permute-start.5 = (f32[4,96,128]{2,1,0:T(8,128)}, f32[4,96,128]{2,1,0:T(8,128)S(1)}, u32[]{:S(2)}, u32[]{:S(2)}) collective-permute-start(f32[4,96,128]{2,1,0:T(8,128)} %get-tuple-element.12), channel_id=1, source_target_pairs={{0,1},{1,0},{2,3},{3,2},{4,5},{5,4},{6,7},{7,6},{8,9},{9,8},{10,11... | collective-permute-start | bytes 589832 | tf_op jit(solution)/shard_map/ppermute | solution.py:447
  81.5 0.7 copy-start.6

commit v2 on v0

v2 whole, which is shorter than its diff:
```python
import functools
import math

import jax
import jax.numpy as jnp
import numpy as np
from jax import lax
from jax.experimental import pallas as pl
from jax.experimental.pallas import tpu as pltpu
from jax.sharding import Mesh
from jax.sharding import PartitionSpec as P

object_rate = 0.02
probe_rate = 0.3

LANES = 128
f32 = jnp.float32
bf16 = jnp.bfloat16
VMEM = pl.BlockSpec(memory_space=pltpu.VMEM)
SMEM = pl.BlockSpec(memory_space=pltpu.SMEM)
ROWS = ("pair", "core")


def matrices(width):
    half = width // 2
    k = np.arange(half)
    angle = (k[:, None] * k[None, :] % half) * (2.0 * math.pi / half)
    cosine = np.cos(angle) / math.sqrt(width)
    sine = np.sin(angle) / math.sqrt(width)
    right = np.zeros((2, LANES, 2, LANES))
    right[0, :half, 0, :half] = cosine
    right[0, :half, 1, :half] = -sine
    right[1, :half, 0, :half] = sine
    right[1, :half, 1, :half] = cosine
    right = right.reshape(2 * LANES, 2 * LANES)
    left = np.block([[cosine, sine], [-sine, cosine]])

    def halves(matrix):
        high = matrix.astype(np.float32).astype(bf16)
        low = (matrix - high.astype(np.float64)).astype(np.float32).astype(bf16)
        return high, low

    right_high, right_low = halves(right)
    left_high, left_low = halves(left)
    turn = k * (2.0 * math.pi / width)
    turns = np.stack([np.cos(turn), np.sin(turn)]).astype(np.float32)
    lane_turns = np.zeros((2, 8, LANES), np.float32)
    lane_turns[:, :, :half] = turns[:, None, :]
    row_turns = np.broadcast_to(turns[:, :, None], (2, half, LANES)).copy()
    return (
        np.concatenate([right_high, right_high, right_low], 0),
        np.concatenate([left_high, left_high, left_low], 1),
        lane_turns,
        row_turns,
    )


def sorters(width):
    half = width // 2
    columns = np.zeros((width, 2 * LANES), np.float32)
    rows = np.zeros((width, width), np.float32)
    for i in range(half):
        for j in range(2):
            columns[2 * i + j, j * LANES + i] = 1
            rows[j * half + i, 2 * i + j] = 1
    return columns.astype(bf16), rows.astype(bf16)


def times(a_real, a_imag, b_real, b_imag):
    return (a_real * b_real - a_imag * b_imag, a_real * b_imag + a_imag * b_real)


def times_conj(a_real, a_imag, b_real, b_imag):
    return (a_real * b_real + a_imag * b_imag, a_real * b_imag - a_imag * b_real)


def halves_of(value):
    high = value.astype(bf16)
    return high, (value - high.astype(f32)).astype(bf16)


def lane_ids(rows):
    return lax.broadcasted_iota(jnp.int32, (rows, LANES), 1)


def packed(planes, half):
    lane = lane_ids(planes[0].shape[0])
    rest = LANES - half
    return [
        jnp.where(lane < half, planes[j], pltpu.roll(planes[3], (half - rest * j) % LANES, 1))
        for j in range(3)
    ]


def last_of(parts, half):
    lane = lane_ids(parts[0].shape[0])
    rest = LANES - half
    out = pltpu.roll(parts[0], rest, 1)
    for j in range(1, 3):
        out = jnp.where(lane < rest * j, out, pltpu.roll(parts[j], (rest * j + rest) % LANES, 1))
    return out


def prepare_kernel(probe_ref, trans_ref, measured_ref, columns_ref, rows_ref, wave_out, trans_out, measured_out):
    width = probe_ref.shape[1]
    half = width // 2
    lane = lane_ids(width)
    for j in range(2):
        head = probe_ref[j, :, :LANES]
        tail = jnp.concatenate(
            [probe_ref[j, :, LANES:], jnp.zeros((width, 2 * LANES - width), f32)], 1
        )
        rest = LANES - half
        wave_out[j, :, :LANES] = jnp.where(lane < half, head, 0.0)
        wave_out[j, :, LANES:] = jnp.where(
            lane < rest, pltpu.roll(head, rest, 1), pltpu.roll(tail, rest, 1)
        )
    for source, target in ((trans_ref, trans_out), (measured_ref, measured_out)):
        for j in range(source.shape[0]):
            left = source[j]
            total = jnp.zeros((width, 2 * LANES), f32)
            for part in range(3):
                piece = left.astype(bf16)
                left = left - piece.astype(f32)
                moved = jnp.dot(piece, columns_ref[...], preferred_element_type=f32)
                total = total + jnp.dot(
                    rows_ref[...], moved.astype(bf16), preferred_element_type=f32
                )
            target[j] = total


def position_kernel(
    paired,
    cores,
    offsets_ref,
    counts_ref,
    *refs,
):
    sides = 2 if paired else 3
    tiles = refs[: 3 * sides]
    (
        wave_ref,
        trans_ref,
        measured_ref,
        right_ref,
        left_ref,
        lane_turn_ref,
        row_turn_ref,
        top_out,
        middle_out,
        bottom_out,
        probe_out,
        obj,
        acc,
        window,
        carried,
        data,
        out_right,
        mid,
        out_left,
    ) = refs[3 * sides :]
    slots = measured_ref.shape[0]
    width = wave_ref.shape[1]
    half = width // 2
    tile = obj.shape[2] // 3
    total = slots * width
    step = 16
    column_of = lax.axis_index("col")

    pad = jnp.zeros((tile, LANES - tile), f32)
    for row in range(3):
        rows = slice(row * tile, (row + 1) * tile)
        for side in range(sides):
            if paired:
                place = 1 if side == 0 else 2 - 2 * column_of
            else:
                place = (1, 0, 2)[side]
            for plane in range(4):
                value = tiles[row * sides + side][plane // 2, plane % 2]
                obj[plane, place, rows, :] = jnp.concatenate([value, pad], 1)
        if paired:
            for plane in range(4):
                obj[plane, 2 * column_of, rows, :] = jnp.zeros((tile, LANES), f32)

    shift = tile - half
    corners = [
        (offsets_ref[0, 0, slot, 0] + shift, offsets_ref[0, 0, slot, 1] + shift)
        for slot in range(slots)
    ]
    chunk = half
    lane = lane_ids(chunk)
    for slot in range(slots):
        row, column = corners[slot]
        back = lax.rem(LANES - column, LANES)
        inside = lane < tile - column
        for plane in range(4):
            for start in range(0, width, chunk):
                source = pl.ds(row + start, chunk)
                target = pl.ds(slot * width + start, chunk)
                for j in range(2):
                    window[plane, j, target, :] = jnp.where(
                        inside,
                        pltpu.roll(obj[plane, j, source, :], back, 1),
                        pltpu.roll(obj[plane, j + 1, source, :], tile - column, 1),
                    )
    acc[...] = jnp.zeros(acc.shape, f32)

    lane_turn = [jnp.broadcast_to(lane_turn_ref[j, :1, :], (step, LANES)) for j in range(2)]
    span = 2 * LANES

    def put(block, start, a, b):
        rows = pl.ds(block * total + start, step)
        for j, value in enumerate((a, b)):
            high, low = halves_of(value)
            data[rows, j * LANES : (j + 1) * LANES] = high
            data[rows, span + j * LANES : span + (j + 1) * LANES] = low

    def multiply_right():
        left = jnp.concatenate([data[...], data[:, :span]], 1)
        out_right[...] = jnp.dot(left, right_ref[...], preferred_element_type=f32)

    def put_mid(slot, block, j, start, a, b):
        for part, value in enumerate((a, b)):
            high, low = halves_of(value)
            columns = slice(j * LANES, (j + 1) * LANES)
            mid[slot, block, pl.ds(part * half + start, step), columns] = high
            mid[slot, block, pl.ds((2 + part) * half + start, step), columns] = low

    def multiply_left():
        for slot in range(slots):
            for block in range(2):
                right = jnp.concatenate([mid[slot, block], mid[slot, block, :width]], 0)
                out_left[slot, block] = jnp.dot(
                    left_ref[...], right, preferred_element_type=f32
                )

    def get_right(block, start):
        rows = pl.ds(block * total + start, step)
        return out_right[rows, :LANES], out_right[rows, LANES:]

    def get_left(slot, block, j, start):
        columns = slice(j * LANES, (j + 1) * LANES)
        return (
            out_left[slot, block, pl.ds(start, step), columns],
            out_left[slot, block, pl.ds(half + start, step), columns],
        )

    def forward(source):
        for slot in range(slots):
            for row in range(0, width, step):
                (a0, b0), (a1, b1) = source(slot, row)
                start = slot * width + row
                put(0, start, a0 + a1, b0 + b1)
                put(1, start, *times_conj(*lane_turn, a0 - a1, b0 - b1))
        multiply_right()
        for slot in range(slots):
            for row in range(0, half, step):
                turn = row_turn_ref[0, pl.ds(row, step), :], row_turn_ref[1, pl.ds(row, step), :]
                for j in range(2):
                    a0, b0 = get_right(j, slot * width + row)
                    a1, b1 = get_right(j, slot * width + half + row)
                    put_mid(slot, 0, j, row, a0 + a1, b0 + b1)
                    put_mid(slot, 1, j, row, *times_conj(*turn, a0 - a1, b0 - b1))
        multiply_left()

    def inverse(source):
        for slot in range(slots):
            for row in range(0, width, step):
                for j, (a, b) in enumerate(source(slot, row)):
                    put(j, slot * width + row, a, b)
        multiply_right()
        for slot in range(slots):
            for row in range(0, width, step):
                a0, b0 = get_right(0, slot * width + row)
                a1, b1 = times_conj(*lane_turn, *get_right(1, slot * width + row))
                put_mid(slot, row // half, 0, row % half, a0 + a1, b0 + b1)
                put_mid(slot, row // half, 1, row % half, a0 - a1, b0 - b1)
        multiply_left()

    def frequency(slot, row, j):
        return get_left(slot, row // half, j, row % half)

    def natural(slot, row, j):
        b0, a0 = get_left(slot, 0, j, row)
        turn = row_turn_ref[0, pl.ds(row, step), :], row_turn_ref[1, pl.ds(row, step), :]
        b1, a1 = times_conj(*turn, *get_left(slot, 1, j, row))
        return (a0 + a1, b0 + b1), (a0 - a1, b0 - b1)

    def at(ref, first, row, j):
        rows = pl.ds(row, step)
        columns = slice(j * LANES, (j + 1) * LANES)
        return ref[first, rows, columns], ref[first + 1, rows, columns]

    def seen(first, slot, row, j):
        rows = pl.ds(slot * width + row, step)
        return window[first, j, rows, :], window[first + 1, j, rows, :]

    def keep(ref, first, slot, row, j, real, imag):
        rows = pl.ds(slot * width + row, step)
        ref[first, j, rows, :] = real
        ref[first + 1, j, rows, :] = imag

    def entry(slot, row):
        return [times(*at(wave_ref, 0, row, j), *seen(0, slot, row, j)) for j in range(2)]

    def propagate(slot, row):
        out = []
        for j in range(2):
            real, imag = times(*at(trans_ref, 0, row, j), *frequency(slot, row, j))
            out.append((imag, real))
        return out

    def residual(slot, row):
        out = []
        for j in range(2):
            real, imag = frequency(slot, row, j)
            columns = slice(j * LANES, (j + 1) * LANES)
            factor = real * real + imag * imag - measured_ref[slot, pl.ds(row, step), columns]
            out.append((factor * imag, factor * real))
        return out

    def propagate_back(slot, row):
        out = []
        for j in range(2):
            real, imag = times_conj(*at(trans_ref, 0, row, j), *frequency(slot, row, j))
            out.append((imag, real))
        return out

    def each_natural(handle):
        for slot in range(slots):
            for row in range(0, half, step):
                for j in range(2):
                    top, bottom = natural(slot, row, j)
                    handle(slot, row, j, *top)
                    handle(slot, half + row, j, *bottom)

    forward(entry)
    inverse(propagate)

    def leave(slot, row, j, real, imag):
        keep(carried, 0, slot, row, j, real, imag)
        keep(carried, 2, slot, row, j, *times(real, imag, *seen(2, slot, row, j)))

    each_natural(leave)

    def leaving(slot, row):
        rows = pl.ds(slot * width + row, step)
        return [(carried[2, j, rows, :], carried[3, j, rows, :]) for j in range(2)]

    forward(leaving)
    inverse(residual)

    def before(slot, row, j, real, imag):
        rows = pl.ds(slot * width + row, step)
        keep(
            carried, 2, slot, row, j, *times_conj(*seen(2, slot, row, j), real, imag)
        )
        keep(
            window,
            2,
            slot,
            row,
            j,
            *times_conj(carried[0, j, rows, :], carried[1, j, rows, :], real, imag),
        )

    each_natural(before)
    forward(leaving)
    inverse(propagate_back)

    live = [(slot < counts_ref[0, 0]).astype(f32) for slot in range(slots)]
    core = lax.axis_index("core")
    share = width // cores
    for row in range(0, half, step):
        sums = [[None] * 4 for side in range(2)]
        for j in range(2):
            for slot in range(slots):
                for side, (real, imag) in enumerate(natural(slot, row, j)):
                    place = side * half + row
                    term = times_conj(*seen(0, slot, place, j), real, imag)
                    keep(
                        window,
                        0,
                        slot,
                        place,
                        j,
                        *times_conj(*at(wave_ref, 0, place, j), real, imag),
                    )
                    for part in range(2):
                        value = live[slot] * term[part]
                        old = sums[side][2 * part + j]
                        sums[side][2 * part + j] = value if old is None else old + value
        for side in range(2):
            place = side * half + row
            which = lax.rem(place // share + core, cores)
            for j, block in enumerate(packed(sums[side], half)):
                probe_out[which, j, pl.ds(place % share, step), :] = block

    for slot in range(slots):
        row, column = corners[slot]
        inside = lane >= column
        over = column + LANES - tile
        for plane in range(4):
            for start in range(0, width, chunk):
                rows = pl.ds(slot * width + start, chunk)
                target = pl.ds(row + start, chunk)
                first, second = (live[slot] * window[plane, j, rows, :] for j in range(2))
                pieces = [jnp.where(inside, pltpu.roll(second, column, 1), pltpu.roll(first, over, 1))]
                if paired:
                    value = live[slot] * window[plane, 1 - column_of, rows, :]
                    value = pltpu.roll(value, jnp.where(column_of == 0, over, column), 1)
                    pieces.append(jnp.where(inside.astype(jnp.int32) == column_of, value, 0.0))
                else:
                    pieces.append(jnp.where(inside, pltpu.roll(first, column, 1), 0.0))
                    pieces.append(jnp.where(inside, 0.0, pltpu.roll(second, over, 1)))
                for side, piece in enumerate(pieces):
                    acc[plane, side, target, :] = acc[plane, side, target, :] + piece
    for row, out in enumerate((top_out, middle_out, bottom_out)):
        rows = slice(row * tile, (row + 1) * tile)
        for side in range(sides):
            planes = [acc[plane, side, rows, :] for plane in range(4)]
            for j, block in enumerate(packed(planes, tile)):
                k = 3 * side + j
                out[:, k * LANES : (k + 1) * LANES] = block


def fold_kernel(middle_ref, below_ref, above_ref, *outs):
    columns = outs[0].shape[1]
    for side, out in enumerate(outs):
        part = slice(side * columns, (side + 1) * columns)
        out[...] = middle_ref[:, part] + below_ref[:, part] + above_ref[:, part]


def update_kernel(object_ref, *refs):
    out_ref = refs[-1]
    tile = object_ref.shape[2]
    total = refs[0][...]
    for ref in refs[1:-1]:
        total = total + ref[...]
    parts = [total[:, j * LANES : (j + 1) * LANES] for j in range(3)]
    parts.append(last_of(parts, tile))
    for plane in range(4):
        out_ref[plane // 2, plane % 2] = (
            object_ref[plane // 2, plane % 2] - object_rate * parts[plane][:, :tile]
        )


def probe_kernel(rate, cores, probe_ref, *refs):
    out_ref = refs[-1]
    width = probe_ref.shape[1]
    half = width // 2
    share = width // cores
    lane = lane_ids(share)
    for k in range(cores):
        ref = refs[k]
        start = share * lax.rem(lax.axis_index("core") + k, cores)
        rows = pl.ds(pl.multiple_of(start, 8), share)
        parts = [ref[j] for j in range(3)]
        parts.append(last_of(parts, half))
        for j in range(2):
            head, tail = parts[2 * j], pltpu.roll(parts[2 * j + 1], half, 1)
            out_ref[j, rows, :LANES] = probe_ref[j, rows, :LANES] - rate * jnp.where(
                lane < half, head, tail
            )
            out_ref[j, rows, LANES:] = (
                probe_ref[j, rows, LANES:] - rate * tail[:, : width - LANES]
            )


def passed_along(x, axis, by):
    peers = lax.axis_size(axis)
    pairs = [(i, i + by) for i in range(peers) if 0 <= i + by < peers]
    return lax.ppermute(x, axis, pairs)


def all_sum(x, group):
    count = math.prod(lax.axis_size(axis) for axis in group)
    shape = x.shape
    x = x.reshape(-1, 2, LANES)
    pairs = x.shape[0]
    piece = -(-pairs // count)
    if piece * count > pairs:
        x = jnp.pad(x, ((0, piece * count - pairs), (0, 0), (0, 0)))
    x = x.reshape(count, piece, 2, LANES)
    x = lax.all_to_all(x, group, 0, 0, tiled=True)
    x = jnp.broadcast_to(jnp.sum(x, 0)[None], x.shape)
    x = lax.all_to_all(x, group, 0, 0, tiled=True)
    return x.reshape(count * piece, 2, LANES)[:pairs].reshape(shape)


def shards(object_slices, probe, propagator_phase, measured, offsets, counts):
    tile = object_slices.shape[-1]
    width = probe.shape[-1]
    slots = measured.shape[2]
    cores = lax.axis_size("core")
    cols_count = lax.axis_size("col")
    devices = lax.axis_size(ROWS) * cols_count
    paired = cols_count == 2
    params = pltpu.CompilerParams(vmem_limit_bytes=60 * 1024 * 1024)

    def shape(*dims, kind=f32):
        return jax.ShapeDtypeStruct(dims, kind)

    cells = object_slices
    if paired:
        beside = [lax.ppermute(cells, "col", [(0, 1), (1, 0)])]
    else:
        beside = [passed_along(cells, "col", 1), passed_along(cells, "col", -1)]
    middle = [cells] + beside
    above = [passed_along(x, ROWS, 1) for x in middle]
    below = [passed_along(x, ROWS, -1) for x in middle]

    columns, rows = sorters(width)
    wave, trans, intensities = pl.pallas_call(
        prepare_kernel,
        out_shape=[
            shape(2, width, 2 * LANES),
            shape(2, width, 2 * LANES),
            shape(slots, width, 2 * LANES),
        ],
        in_specs=[VMEM] * 5,
        out_specs=[VMEM] * 3,
    )(
        probe,
        jnp.stack([jnp.cos(propagator_phase), jnp.sin(propagator_phase)]),
        measured[0, 0],
        columns,
        rows,
    )

    total = slots * width
    sides = len(middle)
    strip = shape(tile, sides * 3 * LANES)
    scratch = [
        pltpu.VMEM((4, 3, 3 * tile, LANES), f32),
        pltpu.VMEM((4, sides, 3 * tile, LANES), f32),
        pltpu.VMEM((4, 2, total, LANES), f32),
        pltpu.VMEM((4, 2, total, LANES), f32),
        pltpu.VMEM((2 * total, 4 * LANES), bf16),
        pltpu.VMEM((2 * total, 2 * LANES), f32),
        pltpu.VMEM((slots, 2, 2 * width, 2 * LANES), bf16),
        pltpu.VMEM((slots, 2, width, 2 * LANES), f32),
    ]
    top, center, bottom, terms = pl.pallas_call(
        functools.partial(position_kernel, paired, cores),
        out_shape=[strip, strip, strip, shape(cores, 3, width // cores, LANES)],
        in_specs=[SMEM, SMEM] + [VMEM] * (3 * sides + 7),
        out_specs=[VMEM] * 4,
        scratch_shapes=scratch,
        compiler_params=params,
    )(offsets, counts, *above, *middle, *below, wave, trans, intensities, *matrices(width))

    if cores == 2:
        swap = [(0, 1), (1, 0)]
        mine = all_sum(terms[0] + lax.ppermute(terms[1], "core", swap), ("pair", "col"))
        sums = [mine, lax.ppermute(mine, "core", swap)]
    else:
        sums = [all_sum(terms[0], ("pair", "col"))]
    from_below = passed_along(top, ROWS, -1)
    from_above = passed_along(bottom, ROWS, 1)
    share = shape(tile, 3 * LANES)
    parts = pl.pallas_call(
        fold_kernel,
        out_shape=[share] * sides,
        in_specs=[VMEM] * 3,
        out_specs=[VMEM] * sides,
    )(center, from_below, from_above)
    if paired:
        received = [lax.ppermute(parts[1], "col", [(0, 1), (1, 0)])]
    else:
        received = [passed_along(parts[1], "col", -1), passed_along(parts[2], "col", 1)]
    object_out = pl.pallas_call(
        update_kernel,
        out_shape=shape(*object_slices.shape),
        in_specs=[VMEM] * (2 + len(received)),
        out_specs=VMEM,
    )(object_slices, parts[0], *received)
    probe_out = pl.pallas_call(
        functools.partial(probe_kernel, probe_rate / (slots * devices), cores),
        out_shape=shape(*probe.shape),
        in_specs=[VMEM] * (1 + cores),
        out_specs=VMEM,
    )(probe, *sums)
    return (object_out, probe_out)


def solution(mesh):
    rows, cols = mesh.devices.shape
    cores = 2 if rows % 2 == 0 else 1
    finer = Mesh(mesh.devices.reshape(rows // cores, cores, cols), ROWS + ("col",))
    return jax.shard_map(
        shards,
        mesh=finer,
        in_specs=(
            P(None, None, ROWS, "col"),
            P(),
            P(),
            P(ROWS, "col", None, None, None),
            P(ROWS, "col", None, None),
            P(ROWS, "col"),
        ),
        out_specs=(P(None, None, ROWS, "col"), P()),
        check_vma=False,
    )
```

time: 288 us -> 72.1 us (0.25)
  waiting for transfers between devices: 137 us -> 10.8 us
  matrix products: 66.4 us -> 0 us
  Pallas kernels: 0 us -> 22.1 us
  between operations: 23 us -> 1.48 us
  local copies, waits for them, and re-layouts: 27.2 us -> 6.26 us
  starting transfers between devices: 21.9 us -> 29.4 us
  other arithmetic: 8.57 us -> 1.51 us
    psum x1 -> x0, waiting for transfers between devices: 113 us -> none  [shards(): total = lax.psum(wave_gradient, ('row', 'col'))]
    dot_general x48 -> x0, matrix products: 66.4 us -> none  [the longest x24 35 us: on_left(): return jnp.einsum('jk,...kl->...jl', matrix, value, precision=highest)]
    pallas_call x0 -> x5, Pallas kernels: none -> 22.1 us  [the longest x1 13.2 us: shards(): pl.pallas_call(functools.partial(position_kernel, paired, cores), out_sha...]
    dynamic_update_slice x2 -> x0, local copies, waits for them, and re-layouts: 15.6 us -> none  [shards(): lax.dynamic_update_slice(grad_pad, previous + position_weight * object_te...]
    ppermute x4 -> x6, waiting for transfers between devices: 11.7 us -> 0.02 us  [passed_along(): return lax.ppermute(x, axis, pairs)]
    all_to_all x0 -> x2, starting transfers between devices: none -> 9.88 us  [all_sum(): x = lax.all_to_all(x, group, 0, 0, tiled=True)]
    ppermute x4, waiting for transfers between devices: 12.6 us -> 3.07 us  [the longest x1 1.28 us: shards(): received = [lax.ppermute(parts[1], 'col', [(0, 1), (1, 0)])]]
    all_to_all x0 -> x2, waiting for transfers between devices: none -> 7.71 us  [all_sum(): x = lax.all_to_all(x, group, 0, 0, tiled=True)]
  transfers between devices with their start and end apart: 9 -> 12, of which waited for: 5 -> 5; matrix products, arithmetic and copies ran while one was open for 3% -> 4% of each run, Pallas kernels for 0% -> 10%
where the time goes in v2:
time: 72.1 us; the launch traced here: 71.5 us
  starting transfers between devices  29.4 us (41%)
  Pallas kernels  22.1 us (31%)
  waiting for transfers between devices  10.8 us (15%)
  local copies, waits for them, and re-layouts  6.26 us (9%)
  other arithmetic  1.51 us (2%)
  between operations  1.48 us (2%)
    pallas_call x1, Pallas kernels, shards(): pl.pallas_call(functools.partial(position_kernel, paired, cores), out_sha...  13.2 us
    ppermute x6, starting transfers between devices, passed_along(): return lax.ppermute(x, axis, pairs)  13 us
    all_to_all x2, starting transfers between devices, all_sum(): x = lax.all_to_all(x, group, 0, 0, tiled=True)  9.88 us
    all_to_all x2, waiting for transfers between devices, all_sum(): x = lax.all_to_all(x, group, 0, 0, tiled=True)  7.71 us
    pallas_call x1, Pallas kernels, shards(): pl.pallas_call(prepare_kernel, out_shape=[shape(2, width, 2 * LANES), sha...  3.09 us
    ppermute x1, starting transfers between devices, shards(): beside = [lax.ppermute(cells, 'col', [(0, 1), (1, 0)])]  3.06 us
    unnamed x26, local copies, waits for them, and re-layouts  2.96 us
    pallas_call x1, Pallas kernels, shards(): pl.pallas_call(functools.partial(probe_kernel, probe_rate / (slots * devi...  2.1 us
  transfers between devices with their start and end apart: 12, of which 5 were waited for; matrix products, arithmetic and copies ran while one was open for 4% of the time, Pallas kernels for 10%

profile of v2, /device:TPU:0, one launch (start us, length us, event | category | flops | bytes accessed | tf_op | source)
XLA Modules:
  0.0 71.5 jit_solution(2356407199091495833)
XLA Ops:
  0.6 3.1 %collective-permute-start.1 = (f32[2,2,96,96]{3,2,1,0:T(8,128)}, f32[2,2,96,96]{3,2,1,0:T(8,128)S(1)}, u32[]{:S(2)}, u32[]{:S(2)}) collective-permute-start(f32[2,2,96,96]{3,2,1,0:T(8,128)} %object_ref.1), channel_id=1, source_target_pairs={{0,1},{1,0},{2,3},{3,2},{4,5},{5,4},{6,7},{7,6},{8,9},{9,8},{10,11... | collective-permute-start | bytes 442376 | tf_op jit(solution)/shard_map/ppermute | solution.py:506
  3.7 1.3 %collective-permute-start.3 = (f32[2,2,96,96]{3,2,1,0:T(8,128)}, f32[2,2,96,96]{3,2,1,0:T(8,128)S(1)}, u32[]{:S(2)}, u32[]{:S(2)}) collective-permute-start(f32[2,2,96,96]{3,2,1,0:T(8,128)} %object_ref.1), channel_id=1, source_target_pairs={{2,0},{4,2},{6,4},{8,6},{10,8},{12,10},{14,12},{16,14},{18,16},{20... | collective-permute-start | bytes 442376 | tf_op jit(solution)/shard_map/ppermute | solution.py:473
  5.0 3.0 %collective-permute-start = (f32[2,2,96,96]{3,2,1,0:T(8,128)}, f32[2,2,96,96]{3,2,1,0:T(8,128)S(1)}, u32[]{:S(2)}, u32[]{:S(2)}) collective-permute-start(f32[2,2,96,96]{3,2,1,0:T(8,128)} %object_ref.1), channel_id=1, source_target_pairs={{0,2},{2,4},{4,6},{6,8},{8,10},{10,12},{12,14},{14,16},{16,18},{18... | collective-permute-start | bytes 442376 | tf_op jit(solution)/shard_map/ppermute | solution.py:473
  8.0 0.8 %collective-permute-done.1.refs_3_ = f32[2,2,96,96]{3,2,1,0:T(8,128)S(1)} collective-permute-done((f32[2,2,96,96]{3,2,1,0:T(8,128)}, f32[2,2,96,96]{3,2,1,0:T(8,128)S(1)}, u32[]{:S(2)}, u32[]{:S(2)}) %collective-permute-start.1) | collective-permute-done | bytes 147488 | tf_op jit(solution)/shard_map/ppermute | solution.py:506
  8.8 1.3 %collective-permute-start.4 = (f32[2,2,96,96]{3,2,1,0:T(8,128)S(1)}, f32[2,2,96,96]{3,2,1,0:T(8,128)S(1)}, u32[]{:S(2)}, u32[]{:S(2)}) collective-permute-start(f32[2,2,96,96]{3,2,1,0:T(8,128)S(1)} %collective-permute-done.1.refs_3_), channel_id=1, source_target_pairs={{2,0},{4,2},{6,4},{8,6},{10,8},{12,10},{14,12},{16,14},{18,16},{20... | collective-permute-start | bytes 442376 | tf_op jit(solution)/shard_map/ppermute | solution.py:473
  10.1 3.0 %collective-permute-start.2 = (f32[2,2,96,96]{3,2,1,0:T(8,128)S(1)}, f32[2,2,96,96]{3,2,1,0:T(8,128)S(1)}, u32[]{:S(2)}, u32[]{:S(2)}) collective-permute-start(f32[2,2,96,96]{3,2,1,0:T(8,128)S(1)} %collective-permute-done.1.refs_3_), channel_id=1, source_target_pairs={{0,2},{2,4},{4,6},{6,8},{8,10},{10,12},{12,14},{14,16},{16,18},{18... | collective-permute-start | bytes 442376 | tf_op jit(solution)/shard_map/ppermute | solution.py:473
  13.1 1.6 %cosine_bitcast_fusion = (f32[1,192,192]{2,1,0:T(8,128)S(1)}, f32[1,192,192]{2,1,0:T(8,128)S(1)}) fusion(f32[192,192]{1,0:T(8,128)} %param.14), kind=kLoop, calls=%fused_computation.2 | loop fusion | bytes 442368 | tf_op jit(solution)/shard_map/stack | solution.py:525
  14.8 0.0 copy-done.4
  15.4 0.8 %pad_maximum_fusion.trans_ref = f32[2,192,192]{2,1,0:T(8,128)} fusion(f32[1,192,192]{2,1,0:T(8,128)S(1)} %get-tuple-element.21, f32[1,192,192]{2,1,0:T(8,128)S(1)} %get-tuple-element.20), kind=kLoop, calls=%fused_computation | loop fusion | flops 73728 | bytes 589824 | tf_op jit(solution)/shard_map/stack | solution.py:525
  16.2 3.1 %shard_map.131 = (f32[2,192,256]{2,1,0:T(8,128)}, f32[2,192,256]{2,1,0:T(8,128)}, f32[2,192,256]{2,1,0:T(8,128)}) custom-call(f32[2,192,192]{2,1,0:T(8,128)} %probe_ref.3, f32[2,192,192]{2,1,0:T(8,128)} %pad_maximum_fusion.trans_ref, f32[2,192,192]{2,1,0:T(8,128)} %bitcast.13, bf16[192,256]{1,0:T(8,128)(2,1)} %constant.14.clone.columns_ref, ...), custom_call_target="tpu_custom_call" | custom-call | tf_op jit(solution)/shard_map/pallas_call | solution.py:514
  19.3 0.0 collective-permute-done.3.refs_4_
  19.3 0.0 collective-permute-done.refs_0_
  19.3 0.0 copy-start.6
  19.3 0.0 collective-permute-done.4.refs_5_
  19.3 0.0 collective-permute-done.2.refs_1_
  19.3 0.0 copy-start.8
  19.3 0.6 copy-done.5
  20.0 0.1 copy-done.6
  20.0 0.1 copy-done.7
  20.1 0.1 copy-done.8
  20.2 13.2 %shard_map.132 = (f32[96,768]{1,0:T(8,128)}, f32[96,768]{1,0:T(8,128)}, f32[96,768]{1,0:T(8,128)}, f32[2,3,96,128]{3,2,1,0:T(8,128)}) custom-call(s32[1,1,2,2]{3,2,1,0:T(2,128)} %offsets_ref.1, s32[1,1]{1,0:T(1,128)S(6)} %copy.14.counts_ref, f32[2,2,96,96]{3,2,1,0:T(8,128)} %copy-done.6, f32[2,2,96,96]{3,2,1,0:T(8,128)} %copy-done.8, ...), custom_call_target="tpu_custom_call" | custom-call | tf_op jit(solution)/shard_map/pallas_call | solution.py:544
  33.3 1.0 %slice_bitcast_fusion = f32[3,96,128]{2,1,0:T(8,128)S(1)} fusion(f32[2,3,96,128]{3,2,1,0:T(8,128)} %get-tuple-element.19), kind=kLoop, calls=%fused_computation.4 | loop fusion | bytes 294912 | tf_op jit(solution)/shard_map/squeeze | solution.py:555
  34.3 0.0 copy-start.12
  34.4 1.6 %collective-permute-start.8 = (f32[3,96,128]{2,1,0:T(8,128)S(1)}, f32[3,96,128]{2,1,0:T(8,128)S(1)}, u32[]{:S(2)}, u32[]{:S(2)}) collective-permute-start(f32[3,96,128]{2,1,0:T(8,128)S(1)} %slice_bitcast_fusion), channel_id=1, source_target_pairs={{0,2},{2,0},{1,3},{3,1},{4,6},{6,4},{5,7},{7,5},{8,10},{10,8},{9,1... | collective-permute-start | bytes 442376 | tf_op jit(solution)/shard_map/ppermute | solution.py:555
  36.0 1.0 %collective-permute-done.8 = f32[3,96,128]{2,1,0:T(8,128)S(1)} collective-permute-done((f32[3,96,128]{2,1,0:T(8,128)S(1)}, f32[3,96,128]{2,1,0:T(8,128)S(1)}, u32[]{:S(2)}, u32[]{:S(2)}) %collective-permute-start.8) | collective-permute-done | bytes 147488 | tf_op jit(solution)/shard_map/ppermute | solution.py:555
  37.0 0.7 bitcast_add_fusion
  37.7 6.4 %all-to-all-start = ((f32[16,9,2,128]{3,2,1,0:T(2,128)}), f32[16,9,2,128]{3,2,1,0:T(2,128)S(1)}, u32[]{:S(2)}, u32[]{:S(2)}) async-start(f32[16,9,2,128]{3,2,1,0:T(2,128)} %bitcast.5), calls=%async_computation | async-start | bytes 294912 | tf_op jit(solution)/shard_map/all_to_all | solution.py:485
  44.1 1.3 %collective-permute-start.5 = (f32[96,768]{1,0:T(8,128)S(1)}, f32[96,768]{1,0:T(8,128)S(1)}, u32[]{:S(2)}, u32[]{:S(2)}) collective-permute-start(f32[96,768]{1,0:T(8,128)S(1)} %copy-done.12), channel_id=1, source_target_pairs={{2,0},{4,2},{6,4},{8,6},{10,8},{12,10},{14,12},{16,14},{18,16},{20... | collective-permute-start | bytes 884744 | tf_op jit(solution)/shard_map/ppermute | solution.py:473
  45.4 3.0 %collective-permute-start.6 = (f32[96,768]{1,0:T(8,128)S(1)}, f32[96,768]{1,0:T(8,128)S(1)}, u32[]{:S(2)}, u32[]{:S(2)}) collective-permute-start(f32[96,768]{1,0:T(8,128)S(1)} %copy-done.11), channel_id=1, source_target_pairs={{0,2},{2,4},{4,6},{6,8},{8,10},{10,12},{12,14},{14,16},{16,18},{18... | collective-permute-start | bytes 884744 | tf_op jit(solution)/shard_map/ppermute | solution.py:473
  48.5 3.8 %all-to-all-done = f32[16,9,2,128]{3,2,1,0:T(2,128)S(1)} async-done(((f32[16,9,2,128]{3,2,1,0:T(2,128)}), f32[16,9,2,128]{3,2,1,0:T(2,128)S(1)}, u32[]{:S(2)}, u32[]{:S(2)}) %all-to-all-start) | async-done | bytes 147488 | tf_op jit(solution)/shard_map/all_to_all | solution.py:485
  52.2 0.1 reduce_sum.9
  52.3 0.7 broadcast_in_dim.2
  53.0 3.5 %all-to-all-start.1 = ((f32[16,9,2,128]{3,2,1,0:T(2,128)}), f32[16,9,2,128]{3,2,1,0:T(2,128)S(1)}, u32[]{:S(2)}, u32[]{:S(2)}) async-start(f32[16,9,2,128]{3,2,1,0:T(2,128)} %broadcast_in_dim.2), calls=%async_computation.1 | async-start | bytes 294912 | tf_op jit(solution)/shard_map/all_to_all | solution.py:487
  56.5 0.0 collective-permute-done.5.below_ref
  56.5 0.0 copy-start.1
  56.5 0.0 collective-permute-done.6.above_ref
  56.6 0.7 copy-done.1
  57.3 0.1 copy-done.2
  57.4 1.9 %shard_map.133 = (f32[96,384]{1,0:T(8,128)}, f32[96,384]{1,0:T(8,128)}) custom-call(f32[96,768]{1,0:T(8,128)} %get-tuple-element.14.middle_ref, f32[96,768]{1,0:T(8,128)} %copy-done.1, f32[96,768]{1,0:T(8,128)} %copy-done.2), custom_call_target="tpu_custom_call" | custom-call | tf_op jit(solution)/shard_map/pallas_call | solution.py:562
  59.2 1.8 %collective-permute-start.7 = (f32[96,384]{1,0:T(8,128)}, f32[96,384]{1,0:T(8,128)S(1)}, u32[]{:S(2)}, u32[]{:S(2)}) collective-permute-start(f32[96,384]{1,0:T(8,128)} %get-tuple-element.18), channel_id=1, source_target_pairs={{0,1},{1,0},{2,3},{3,2},{4,5},{5,4},{6,7},{7,6},{8,9},{9,8},{10,11... | collective-permute-start | bytes 442376 | tf_op jit(solution)/shard_map/ppermute | solution.py:569
  61.0 3.9 %all-to-all-done.1 = f32[16,9,2,128]{3,2,1,0:T(2,128)S(1)} async-done(((f32[16,9,2,128]{3,2,1,0:T(2,128)}), f32[16,9,2,128]{3,2,1,0:T(2,128)S(1)}, u32[]{:S(2)}, u32[]{:S(2)}) %all-to-all-start.1) | async-done | bytes 147488 | tf_op jit(solution)/shard_map/all_to_all | solution.py:487
  65.0 0.0 collective-permute-start.9
  65.0 1.3 %collective-permute-done.7.refs_1_ = f32[96,384]{1,0:T(8,128)S(1)} collective-permute-done((f32[96,384]{1,0:T(8,128)}, f32[96,384]{1,0:T(8,128)S(1)}, u32[]{:S(2)}, u32[]{:S(2)}) %collective-permute-start.7) | collective-permute-done | bytes 147488 | tf_op jit(solution)/shard_map/ppermute | solution.py:569
  66.2 0.7 copy-done.9
  66.9 1.9 %shard_map.134 = f32[2,2,96,96]{3,2,1,0:T(8,128)} custom-call(f32[2,2,96,96]{3,2,1,0:T(8,128)} %object_ref.1, f32[96,384]{1,0:T(8,128)} %get-tuple-element.17.refs_0_, f32[96,384]{1,0:T(8,128)} %copy-done.9), custom_call_target="tpu_custom_call" | custom-call | tf_op jit(solution)/shard_map/pallas_call | solution.py:572
  68.8 0.0 collective-permute-done.9.refs_1_
  68.8 0.6 copy-done.10
  69.4 2.1 %shard_map.135 = f32[2,192,192]{2,1,0:T(8,128)} custom-call(f32[2,192,192]{2,1,0:T(8,128)} %probe_ref.3, f32[3,96,128]{2,1,0:T(8,128)} %bitcast.12, f32[3,96,128]{2,1,0:T(8,128)} %copy-done.10), custom_call_target="tpu_custom_call" | custom-call | tf_op jit(solution)/shard_map/pallas_call | solution.py:578
  (13 shorter events, 0.0 us)
Async XLA Ops:
  0.6 8.2 %collective-permute-start.1 = (f32[2,2,96,96]{3,2,1,0:T(8,128)}, f32[2,2,96,96]{3,2,1,0:T(8,128)S(1)}, u32[]{:S(2)}, u32[]{:S(2)}) collective-permute-start(f32[2,2,96,96]{3,2,1,0:T(8,128)} %object_ref.1), channel_id=1, source_target_pairs={{0,1},{1,0},{2,3},{3,2},{4,5},{5,4},{6,7},{7,6},{8,9},{9,8},{10,11... | collective-permute-start | bytes 442376 | tf_op jit(solution)/shard_map/ppermute | solution.py:506
  3.7 15.6 %collective-permute-start.3 = (f32[2,2,96,96]{3,2,1,0:T(8,128)}, f32[2,2,96,96]{3,2,1,0:T(8,128)S(1)}, u32[]{:S(2)}, u32[]{:S(2)}) collective-permute-start(f32[2,2,96,96]{3,2,1,0:T(8,128)} %object_ref.1), channel_id=1, source_target_pairs={{2,0},{4,2},{6,4},{8,6},{10,8},{12,10},{14,12},{16,14},{18,16},{20... | collective-permute-start | bytes 442376 | tf_op jit(solution)/shard_map/ppermute | solution.py:473
  5.0 14.3 %collective-permute-start = (f32[2,2,96,96]{3,2,1,0:T(8,128)}, f32[2,2,96,96]{3,2,1,0:T(8,128)S(1)}, u32[]{:S(2)}, u32[]{:S(2)}) collective-permute-start(f32[2,2,96,96]{3,2,1,0:T(8,128)} %object_ref.1), channel_id=1, source_target_pairs={{0,2},{2,4},{4,6},{6,8},{8,10},{10,12},{12,14},{14,16},{16,18},{18... | collective-permute-start | bytes 442376 | tf_op jit(solution)/shard_map/ppermute | solution.py:473
  8.8 6.0 %copy-start.4 = (f32[2,2,96,96]{3,2,1,0:T(8,128)}, f32[2,2,96,96]{3,2,1,0:T(8,128)S(1)}, u32[]{:S(2)}) copy-start(f32[2,2,96,96]{3,2,1,0:T(8,128)S(1)} %collective-permute-done.1.refs_3_) | copy-start | bytes 442372
  8.8 10.5 %collective-permute-start.4 = (f32[2,2,96,96]{3,2,1,0:T(8,128)S(1)}, f32[2,2,96,96]{3,2,1,0:T(8,128)S(1)}, u32[]{:S(2)}, u32[]{:S(2)}) collective-permute-start(f32[2,2,96,96]{3,2,1,0:T(8,128)S(1)} %collective-permute-done.1.refs_3_), channel_id=1, source_target_pairs={{2,0},{4,2},{6,4},{8,6},{10,8},{12,10},{14,12},{16,14},{18,16},{20... | collective-permute-start | bytes 442376 | tf_op jit(solution)/shard_map/ppermute | solution.py:473
  10.1 9.2 %collective-permute-start.2 = (f32[2,2,96,96]{3,2,1,0:T(8,128)S(1)}, f32[2,2,96,96]{3,2,1,0:T(8,128)S(1)}, u32[]{:S(2)}, u32[]{:S(2)}) collective-permute-start(f32[2,2,96,96]{3,2,1,0:T(8,128)S(1)} %collective-permute-done.1.refs_3_), channel_id=1, source_target_pairs={{0,2},{2,4},{4,6},{6,8},{8,10},{10,12},{12,14},{14,16},{16,18},{18... | collective-permute-start | bytes 442376 | tf_op jit(solution)/shard_map/ppermute | solution.py:473
  19.3 0.7 copy-start.5
  19.3 0.7 %copy-start.6 = (f32[2,2,96,96]{3,2,1,0:T(8,128)}, f32[2,2,96,96]{3,2,1,0:T(8,128)S(1)}, u32[]{:S(2)}) copy-start(f32[2,2,96,96]{3,2,1,0:T(8,128)S(1)} %collective-permute-done.refs_0_) | copy-start | bytes 442372
  19.3 0.8 %copy-start.7 = (f32[2,2,96,96]{3,2,1,0:T(8,128)}, f32[2,2,96,96]{3,2,1,0:T(8,128)S(1)}, u32[]{:S(2)}) copy-start(f32[2,2,96,96]{3,2,1,0:T(8,128)S(1)} %collective-permute-done.4.refs_5_) | copy-start | bytes 442372
  19.3 0.8 %copy-start.8 = (f32[2,2,96,96]{3,2,1,0:T(8,128)}, f32[2,2,96,96]{3,2,1,0:T(8,128)S(1)}, u32[]{:S(2)}) copy-start(f32[2,2,96,96]{3,2,1,0:T(8,128)S(1)} %collective-permute-done.2.refs_1_) | copy-start | bytes 442372
  33.3 3.7 %copy-start.3 = (f32[2,3,96,128]{3,2,1,0:T(8,128)S(1)}, f32[2,3,96,128]{3,2,1,0:T(8,128)}, u32[]{:S(2)}) copy-start(f32[2,3,96,128]{3,2,1,0:T(8,128)} %get-tuple-element.19) | copy-start | bytes 884740
  34.3 9.7 %copy-start.12 = (f32[96,768]{1,0:T(8,128)S(1)}, f32[96,768]{1,0:T(8,128)}, u32[]{:S(2)}) copy-start(f32[96,768]{1,0:T(8,128)} %get-tuple-element.15) | copy-start | bytes 884740
  34.4 11.0 %copy-start.11 = (f32[96,768]{1,0:T(8,128)S(1)}, f32[96,768]{1,0:T(8,128)}, u32[]{:S(2)}) copy-start(f32[96,768]{1,0:T(8,128)} %get-tuple-element.16) | copy-start | bytes 884740
  34.4 2.7 %collective-permute-start.8 = (f32[3,96,128]{2,1,0:T(8,128)S(1)}, f32[3,96,128]{2,1,0:T(8,128)S(1)}, u32[]{:S(2)}, u32[]{:S(2)}) collective-permute-start(f32[3,96,128]{2,1,0:T(8,128)S(1)} %slice_bitcast_fusion), channel_id=1, source_target_pairs={{0,2},{2,0},{1,3},{3,1},{4,6},{6,4},{5,7},{7,5},{8,10},{10,8},{9,1... | collective-permute-start | bytes 442376 | tf_op jit(solution)/shard_map/ppermute | solution.py:555
  37.7 14.5 %all-to-all-start = ((f32[16,9,2,128]{3,2,1,0:T(2,128)}), f32[16,9,2,128]{3,2,1,0:T(2,128)S(1)}, u32[]{:S(2)}, u32[]{:S(2)}) async-start(f32[16,9,2,128]{3,2,1,0:T(2,128)} %bitcast.5), calls=%async_computation | async-start | bytes 294912 | tf_op jit(solution)/shard_map/all_to_all | solution.py:485
  44.1 12.4 %collective-permute-start.5 = (f32[96,768]{1,0:T(8,128)S(1)}, f32[96,768]{1,0:T(8,128)S(1)}, u32[]{:S(2)}, u32[]{:S(2)}) collective-permute-start(f32[96,768]{1,0:T(8,128)S(1)} %copy-done.12), channel_id=1, source_target_pairs={{2,0},{4,2},{6,4},{8,6},{10,8},{12,10},{14,12},{16,14},{18,16},{20... | collective-permute-start | bytes 884744 | tf_op jit(solution)/shard_map/ppermute | solution.py:473
  45.4 11.2 %collective-permute-start.6 = (f32[96,768]{1,0:T(8,128)S(1)}, f32[96,768]{1,0:T(8,128)S(1)}, u32[]{:S(2)}, u32[]{:S(2)}) collective-permute-start(f32[96,768]{1,0:T(8,128)S(1)} %copy-done.11), channel_id=1, source_target_pairs={{0,2},{2,4},{4,6},{6,8},{8,10},{10,12},{12,14},{14,16},{16,18},{18... | collective-permute-start | bytes 884744 | tf_op jit(solution)/shard_map/ppermute | solution.py:473
  53.0 11.9 %all-to-all-start.1 = ((f32[16,9,2,128]{3,2,1,0:T(2,128)}), f32[16,9,2,128]{3,2,1,0:T(2,128)S(1)}, u32[]{:S(2)}, u32[]{:S(2)}) async-start(f32[16,9,2,128]{3,2,1,0:T(2,128)} %broadcast_in_dim.2), calls=%async_computation.1 | async-start | bytes 294912 | tf_op jit(solution)/shard_map/all_to_all | solution.py:487
  56.5 0.7 %copy-start.1 = (f32[96,768]{1,0:T(8,128)}, f32[96,768]{1,0:T(8,128)S(1)}, u32[]{:S(2)}) copy-start(f32[96,768]{1,0:T(8,128)S(1)} %collective-permute-done.5.below_ref) | copy-start | bytes 884740
  56.6 0.8 %copy-start.2 = (f32[96,768]{1,0:T(8,128)}, f32[96,768]{1,0:T(8,128)S(1)}, u32[]{:S(2)}) copy-start(f32[96,768]{1,0:T(8,128)S(1)} %collective-permute-done.6.above_ref) | copy-start | bytes 884740
  59.2 7.0 %collective-permute-start.7 = (f32[96,384]{1,0:T(8,128)}, f32[96,384]{1,0:T(8,128)S(1)}, u32[]{:S(2)}, u32[]{:S(2)}) collective-permute-start(f32[96,384]{1,0:T(8,128)} %get-tuple-element.18), channel_id=1, source_target_pairs={{0,1},{1,0},{2,3},{3,2},{4,5},{5,4},{6,7},{7,6},{8,9},{9,8},{10,11... | collective-permute-start | bytes 442376 | tf_op jit(solution)/shard_map/ppermute | solution.py:569
  65.0 3.8 %copy-start = (f32[16,9,2,128]{3,2,1,0:T(2,128)}, f32[16,9,2,128]{3,2,1,0:T(2,128)S(1)}, u32[]{:S(2)}) copy-start(f32[16,9,2,128]{3,2,1,0:T(2,128)S(1)} %all-to-all-done.1) | copy-start | bytes 442372
  65.0 3.8 %collective-permute-start.9 = (f32[3,96,128]{2,1,0:T(8,128)S(1)}, f32[3,96,128]{2,1,0:T(8,128)S(1)}, u32[]{:S(2)}, u32[]{:S(2)}) collective-permute-start(f32[3,96,128]{2,1,0:T(8,128)S(1)} %bitcast.11), channel_id=1, source_target_pairs={{0,2},{2,0},{1,3},{3,1},{4,6},{6,4},{5,7},{7,5},{8,10},{10,8},{9,1... | collective-permute-start | bytes 442376 | tf_op jit(solution)/shard_map/ppermute | solution.py:556
  66.2 0.7 copy-start.9
  68.8 0.7 copy-start.10

commit v3 on v2

--- a/solution.py
+++ b/solution.py
@@ -101,7 +101,17 @@
     return out
 
 
-def prepare_kernel(probe_ref, trans_ref, measured_ref, columns_ref, rows_ref, wave_out, trans_out, measured_out):
+def prepare_kernel(
+    probe_ref,
+    cosine_ref,
+    sine_ref,
+    measured_ref,
+    columns_ref,
+    rows_ref,
+    wave_out,
+    trans_out,
+    measured_out,
+):
     width = probe_ref.shape[1]
     half = width // 2
     lane = lane_ids(width)
@@ -115,18 +125,22 @@
         wave_out[j, :, LANES:] = jnp.where(
             lane < rest, pltpu.roll(head, rest, 1), pltpu.roll(tail, rest, 1)
         )
-    for source, target in ((trans_ref, trans_out), (measured_ref, measured_out)):
-        for j in range(source.shape[0]):
-            left = source[j]
-            total = jnp.zeros((width, 2 * LANES), f32)
-            for part in range(3):
-                piece = left.astype(bf16)
-                left = left - piece.astype(f32)
-                moved = jnp.dot(piece, columns_ref[...], preferred_element_type=f32)
-                total = total + jnp.dot(
-                    rows_ref[...], moved.astype(bf16), preferred_element_type=f32
-                )
-            target[j] = total
+    planes = [(cosine_ref[...], trans_out, 0), (sine_ref[...], trans_out, 1)]
+    for slot in range(measured_out.shape[0]):
+        planes.append((measured_ref[0, 0, slot], measured_out, slot))
+    for left, target, j in planes:
+        total = jnp.zeros((width, 2 * LANES), f32)
+        for part in range(3):
+            piece = left.astype(bf16)
+            left = left - piece.astype(f32)
+            moved = jnp.dot(piece, columns_ref[...], preferred_element_type=f32)
+            total = total + jnp.dot(rows_ref[...], moved.astype(bf16), preferred_element_type=f32)
+        target[j] = total
+
+
+def row_places(cores):
+    core = lax.axis_index("core") if cores == 2 else 1
+    return 1, 2 - 2 * core, 2 * core
 
 
 def position_kernel(
@@ -146,10 +160,12 @@
         left_ref,
         lane_turn_ref,
         row_turn_ref,
-        top_out,
-        middle_out,
-        bottom_out,
-        probe_out,
+        own_out,
+        near_out,
+        far_out,
+    ) = refs[3 * sides : 3 * sides + 10]
+    terms_out = refs[3 * sides + 10 : 3 * sides + 10 + cores]
+    (
         obj,
         acc,
         window,
@@ -158,7 +174,8 @@
         out_right,
         mid,
         out_left,
-    ) = refs[3 * sides :]
+        terms,
+    ) = refs[3 * sides + 10 + cores :]
     slots = measured_ref.shape[0]
     width = wave_ref.shape[1]
     half = width // 2
@@ -166,10 +183,11 @@
     total = slots * width
     step = 16
     column_of = lax.axis_index("col")
+    row_starts = [pl.multiple_of(place * tile, 8) for place in row_places(cores)]
 
     pad = jnp.zeros((tile, LANES - tile), f32)
     for row in range(3):
-        rows = slice(row * tile, (row + 1) * tile)
+        rows = pl.ds(row_starts[row], tile)
         for side in range(sides):
             if paired:
                 place = 1 if side == 0 else 2 - 2 * column_of
@@ -208,34 +226,34 @@
     lane_turn = [jnp.broadcast_to(lane_turn_ref[j, :1, :], (step, LANES)) for j in range(2)]
     span = 2 * LANES
 
-    def put(block, start, a, b):
-        rows = pl.ds(block * total + start, step)
-        for j, value in enumerate((a, b)):
-            high, low = halves_of(value)
-            data[rows, j * LANES : (j + 1) * LANES] = high
-            data[rows, span + j * LANES : span + (j + 1) * LANES] = low
+    def put(slot, block, row, a, b):
+        rows = pl.ds((2 * slot + block) * width + row, step)
+        high, low = halves_of(jnp.concatenate([a, b], 1))
+        data[rows, :span] = high
+        data[rows, span:] = low
 
     def multiply_right():
-        left = jnp.concatenate([data[...], data[:, :span]], 1)
-        out_right[...] = jnp.dot(left, right_ref[...], preferred_element_type=f32)
-
-    def put_mid(slot, block, j, start, a, b):
-        for part, value in enumerate((a, b)):
-            high, low = halves_of(value)
-            columns = slice(j * LANES, (j + 1) * LANES)
-            mid[slot, block, pl.ds(part * half + start, step), columns] = high
-            mid[slot, block, pl.ds((2 + part) * half + start, step), columns] = low
+        for slot in range(slots):
+            rows = slice(2 * slot * width, 2 * (slot + 1) * width)
+            left = jnp.concatenate([data[rows, :], data[rows, :span]], 1)
+            out_right[rows, :] = jnp.dot(left, right_ref[...], preferred_element_type=f32)
+
+    def put_mid(slot, block, start, first, second):
+        for part in range(2):
+            high, low = halves_of(jnp.concatenate([first[part], second[part]], 1))
+            mid[slot, block, pl.ds(part * half + start, step), :] = high
+            mid[slot, block, pl.ds((2 + part) * half + start, step), :] = low
+            mid[slot, block, pl.ds((4 + part) * half + start, step), :] = high
 
     def multiply_left():
         for slot in range(slots):
             for block in range(2):
-                right = jnp.concatenate([mid[slot, block], mid[slot, block, :width]], 0)
                 out_left[slot, block] = jnp.dot(
-                    left_ref[...], right, preferred_element_type=f32
+                    left_ref[...], mid[slot, block], preferred_element_type=f32
                 )
 
-    def get_right(block, start):
-        rows = pl.ds(block * total + start, step)
+    def get_right(slot, block, row):
+        rows = pl.ds((2 * slot + block) * width + row, step)
         return out_right[rows, :LANES], out_right[rows, LANES:]
 
     def get_left(slot, block, j, start):
@@ -249,32 +267,33 @@
         for slot in range(slots):
             for row in range(0, width, step):
                 (a0, b0), (a1, b1) = source(slot, row)
-                start = slot * width + row
-                put(0, start, a0 + a1, b0 + b1)
-                put(1, start, *times_conj(*lane_turn, a0 - a1, b0 - b1))
+                put(slot, 0, row, a0 + a1, b0 + b1)
+                put(slot, 1, row, *times_conj(*lane_turn, a0 - a1, b0 - b1))
         multiply_right()
         for slot in range(slots):
             for row in range(0, half, step):
                 turn = row_turn_ref[0, pl.ds(row, step), :], row_turn_ref[1, pl.ds(row, step), :]
+                even, odd = [], []
                 for j in range(2):
-                    a0, b0 = get_right(j, slot * width + row)
-                    a1, b1 = get_right(j, slot * width + half + row)
-                    put_mid(slot, 0, j, row, a0 + a1, b0 + b1)
-                    put_mid(slot, 1, j, row, *times_conj(*turn, a0 - a1, b0 - b1))
+                    a0, b0 = get_right(slot, j, row)
+                    a1, b1 = get_right(slot, j, half + row)
+                    even.append((a0 + a1, b0 + b1))
+                    odd.append(times_conj(*turn, a0 - a1, b0 - b1))
+                put_mid(slot, 0, row, *even)
+                put_mid(slot, 1, row, *odd)
         multiply_left()
 
     def inverse(source):
         for slot in range(slots):
             for row in range(0, width, step):
                 for j, (a, b) in enumerate(source(slot, row)):
-                    put(j, slot * width + row, a, b)
+                    put(slot, j, row, a, b)
         multiply_right()
         for slot in range(slots):
             for row in range(0, width, step):
-                a0, b0 = get_right(0, slot * width + row)
-                a1, b1 = times_conj(*lane_turn, *get_right(1, slot * width + row))
-                put_mid(slot, row // half, 0, row % half, a0 + a1, b0 + b1)
-                put_mid(slot, row // half, 1, row % half, a0 - a1, b0 - b1)
+                a0, b0 = get_right(slot, 0, row)
+                a1, b1 = times_conj(*lane_turn, *get_right(slot, 1, row))
+                put_mid(slot, row // half, row % half, (a0 + a1, b0 + b1), (a0 - a1, b0 - b1))
         multiply_left()
 
     def frequency(slot, row, j):
@@ -394,7 +413,9 @@
             place = side * half + row
             which = lax.rem(place // share + core, cores)
             for j, block in enumerate(packed(sums[side], half)):
-                probe_out[which, j, pl.ds(place % share, step), :] = block
+                terms[which, j, pl.ds(place % share, step), :] = block
+    for k, out in enumerate(terms_out):
+        out[...] = terms[k]
 
     for slot in range(slots):
         row, column = corners[slot]
@@ -415,8 +436,8 @@
                     pieces.append(jnp.where(inside, 0.0, pltpu.roll(second, over, 1)))
                 for side, piece in enumerate(pieces):
                     acc[plane, side, target, :] = acc[plane, side, target, :] + piece
-    for row, out in enumerate((top_out, middle_out, bottom_out)):
-        rows = slice(row * tile, (row + 1) * tile)
+    for start, out in zip(row_starts, (own_out, near_out, far_out)):
+        rows = pl.ds(start, tile)
         for side in range(sides):
             planes = [acc[plane, side, rows, :] for plane in range(4)]
             for j, block in enumerate(packed(planes, tile)):
@@ -424,45 +445,41 @@
                 out[:, k * LANES : (k + 1) * LANES] = block
 
 
-def fold_kernel(middle_ref, below_ref, above_ref, *outs):
+def fold_kernel(own_ref, near_ref, far_ref, *outs):
     columns = outs[0].shape[1]
     for side, out in enumerate(outs):
         part = slice(side * columns, (side + 1) * columns)
-        out[...] = middle_ref[:, part] + below_ref[:, part] + above_ref[:, part]
-
-
-def update_kernel(object_ref, *refs):
-    out_ref = refs[-1]
+        out[...] = own_ref[:, part] + near_ref[:, part] + far_ref[:, part]
+
+
+def update_kernel(rate, cores, object_ref, probe_ref, *refs):
+    object_out, probe_out = refs[-2:]
+    sums = refs[:cores]
     tile = object_ref.shape[2]
-    total = refs[0][...]
-    for ref in refs[1:-1]:
+    total = refs[cores][...]
+    for ref in refs[cores + 1 : -2]:
         total = total + ref[...]
     parts = [total[:, j * LANES : (j + 1) * LANES] for j in range(3)]
     parts.append(last_of(parts, tile))
     for plane in range(4):
-        out_ref[plane // 2, plane % 2] = (
+        object_out[plane // 2, plane % 2] = (
             object_ref[plane // 2, plane % 2] - object_rate * parts[plane][:, :tile]
         )
-
-
-def probe_kernel(rate, cores, probe_ref, *refs):
-    out_ref = refs[-1]
     width = probe_ref.shape[1]
     half = width // 2
     share = width // cores
     lane = lane_ids(share)
-    for k in range(cores):
-        ref = refs[k]
+    for k, ref in enumerate(sums):
         start = share * lax.rem(lax.axis_index("core") + k, cores)
         rows = pl.ds(pl.multiple_of(start, 8), share)
         parts = [ref[j] for j in range(3)]
         parts.append(last_of(parts, half))
         for j in range(2):
             head, tail = parts[2 * j], pltpu.roll(parts[2 * j + 1], half, 1)
-            out_ref[j, rows, :LANES] = probe_ref[j, rows, :LANES] - rate * jnp.where(
+            probe_out[j, rows, :LANES] = probe_ref[j, rows, :LANES] - rate * jnp.where(
                 lane < half, head, tail
             )
-            out_ref[j, rows, LANES:] = (
+            probe_out[j, rows, LANES:] = (
                 probe_ref[j, rows, LANES:] - rate * tail[:, : width - LANES]
             )
 
@@ -471,6 +488,20 @@
     peers = lax.axis_size(axis)
     pairs = [(i, i + by) for i in range(peers) if 0 <= i + by < peers]
     return lax.ppermute(x, axis, pairs)
+
+
+def from_near(x, cores):
+    if cores == 2:
+        return lax.ppermute(x, "core", [(0, 1), (1, 0)])
+    return passed_along(x, ROWS, 1)
+
+
+def from_far(x, cores):
+    if cores == 2:
+        ends = range(1, lax.axis_size(ROWS) - 1, 2)
+        pairs = [(i, i + 1) for i in ends] + [(i + 1, i) for i in ends]
+        return lax.ppermute(x, ROWS, pairs)
+    return passed_along(x, ROWS, -1)
 
 
 def all_sum(x, group):
@@ -506,9 +537,9 @@
         beside = [lax.ppermute(cells, "col", [(0, 1), (1, 0)])]
     else:
         beside = [passed_along(cells, "col", 1), passed_along(cells, "col", -1)]
-    middle = [cells] + beside
-    above = [passed_along(x, ROWS, 1) for x in middle]
-    below = [passed_along(x, ROWS, -1) for x in middle]
+    own = [cells] + beside
+    near = [from_near(x, cores) for x in own]
+    far = [from_far(x, cores) for x in own]
 
     columns, rows = sorters(width)
     wave, trans, intensities = pl.pallas_call(
@@ -518,18 +549,19 @@
             shape(2, width, 2 * LANES),
             shape(slots, width, 2 * LANES),
         ],
-        in_specs=[VMEM] * 5,
+        in_specs=[VMEM] * 6,
         out_specs=[VMEM] * 3,
     )(
         probe,
-        jnp.stack([jnp.cos(propagator_phase), jnp.sin(propagator_phase)]),
-        measured[0, 0],
+        jnp.cos(propagator_phase),
+        jnp.sin(propagator_phase),
+        measured,
         columns,
         rows,
     )
 
     total = slots * width
-    sides = len(middle)
+    sides = len(own)
     strip = shape(tile, sides * 3 * LANES)
     scratch = [
         pltpu.VMEM((4, 3, 3 * tile, LANES), f32),
@@ -538,50 +570,48 @@
         pltpu.VMEM((4, 2, total, LANES), f32),
         pltpu.VMEM((2 * total, 4 * LANES), bf16),
         pltpu.VMEM((2 * total, 2 * LANES), f32),
-        pltpu.VMEM((slots, 2, 2 * width, 2 * LANES), bf16),
+        pltpu.VMEM((slots, 2, 3 * width, 2 * LANES), bf16),
         pltpu.VMEM((slots, 2, width, 2 * LANES), f32),
     ]
-    top, center, bottom, terms = pl.pallas_call(
+    term = shape(3, width // cores, LANES)
+    scratch.append(pltpu.VMEM((cores,) + term.shape, f32))
+    strips = pl.pallas_call(
         functools.partial(position_kernel, paired, cores),
-        out_shape=[strip, strip, strip, shape(cores, 3, width // cores, LANES)],
+        out_shape=[strip] * 3 + [term] * cores,
         in_specs=[SMEM, SMEM] + [VMEM] * (3 * sides + 7),
-        out_specs=[VMEM] * 4,
+        out_specs=[VMEM] * (3 + cores),
         scratch_shapes=scratch,
         compiler_params=params,
-    )(offsets, counts, *above, *middle, *below, wave, trans, intensities, *matrices(width))
+    )(offsets, counts, *own, *near, *far, wave, trans, intensities, *matrices(width))
+    own_strip, near_strip, far_strip = strips[:3]
+    terms = strips[3:]
 
     if cores == 2:
-        swap = [(0, 1), (1, 0)]
-        mine = all_sum(terms[0] + lax.ppermute(terms[1], "core", swap), ("pair", "col"))
-        sums = [mine, lax.ppermute(mine, "core", swap)]
+        mine = all_sum(terms[0] + from_near(terms[1], cores), ("pair", "col"))
+        sums = [mine, from_near(mine, cores)]
     else:
         sums = [all_sum(terms[0], ("pair", "col"))]
-    from_below = passed_along(top, ROWS, -1)
-    from_above = passed_along(bottom, ROWS, 1)
+    if cores == 1:
+        near_strip, far_strip = passed_along(near_strip, ROWS, -1), passed_along(far_strip, ROWS, 1)
+    else:
+        near_strip, far_strip = from_near(near_strip, cores), from_far(far_strip, cores)
     share = shape(tile, 3 * LANES)
     parts = pl.pallas_call(
         fold_kernel,
         out_shape=[share] * sides,
         in_specs=[VMEM] * 3,
         out_specs=[VMEM] * sides,
-    )(center, from_below, from_above)
+    )(own_strip, near_strip, far_strip)
     if paired:
         received = [lax.ppermute(parts[1], "col", [(0, 1), (1, 0)])]
     else:
         received = [passed_along(parts[1], "col", -1), passed_along(parts[2], "col", 1)]
-    object_out = pl.pallas_call(
-        update_kernel,
-        out_shape=shape(*object_slices.shape),
-        in_specs=[VMEM] * (2 + len(received)),
-        out_specs=VMEM,
-    )(object_slices, parts[0], *received)
-    probe_out = pl.pallas_call(
-        functools.partial(probe_kernel, probe_rate / (slots * devices), cores),
-        out_shape=shape(*probe.shape),
-        in_specs=[VMEM] * (1 + cores),
-        out_specs=VMEM,
-    )(probe, *sums)
-    return (object_out, probe_out)
+    return pl.pallas_call(
+        functools.partial(update_kernel, probe_rate / (slots * devices), cores),
+        out_shape=[shape(*object_slices.shape), shape(*probe.shape)],
+        in_specs=[VMEM] * (3 + cores + len(received)),
+        out_specs=[VMEM] * 2,
+    )(object_slices, probe, *sums, parts[0], *received)
 
 
 def solution(mesh):

time: 72.1 us -> 62.4 us (0.87)
  starting transfers between devices: 29.4 us -> 22.6 us
  Pallas kernels: 22.1 us -> 16.4 us
  waiting for transfers between devices: 10.8 us -> 14.3 us
  local copies, waits for them, and re-layouts: 6.26 us -> 5.39 us
    ppermute x8, starting transfers between devices: 14.6 us -> 8.23 us  [the longest x5 6.23 us: from_near(): return lax.ppermute(x, 'core', [(0, 1), (1, 0)])]
    pallas_call x1, Pallas kernels: 13.2 us -> 9.15 us  [shards(): pl.pallas_call(functools.partial(position_kernel, paired, cores), out_sha...]
    all_to_all x2, waiting for transfers between devices: 7.71 us -> 10.6 us  [all_sum(): x = lax.all_to_all(x, group, 0, 0, tiled=True)]
    sin x0 -> x1, local copies, waits for them, and re-layouts: none -> 2.38 us  [shards(): jnp.sin(propagator_phase)]
    pallas_call x2 -> x1, Pallas kernels: 3.96 us -> 2.31 us  [shards(): pl.pallas_call(functools.partial(update_kernel, probe_rate / (slots * dev...]
    another operation x1 -> x0, local copies, waits for them, and re-layouts: 1.61 us -> none  [shards(): jnp.stack([jnp.cos(propagator_phase), jnp.sin(propagator_phase)])]
    ppermute x8, waiting for transfers between devices: 1.03 us -> 2.06 us  [the longest x5 2.05 us: from_near(): return lax.ppermute(x, 'core', [(0, 1), (1, 0)])]
    squeeze x1 -> x0, local copies, waits for them, and re-layouts: 0.99 us -> none  [shards(): terms[1]]
  transfers between devices with their start and end apart: 12 -> 12, of which waited for: 5 -> 6; matrix products, arithmetic and copies ran while one was open for 4% -> 5% of each run, Pallas kernels for 10% -> 8%
where the time goes in v3:
time: 62.4 us; the launch traced here: 61.9 us
  starting transfers between devices  22.6 us (36%)
  Pallas kernels  16.4 us (26%)
  waiting for transfers between devices  14.3 us (23%)
  local copies, waits for them, and re-layouts  5.39 us (9%)
  other arithmetic  1.72 us (3%)
  between operations  1.44 us (2%)
    all_to_all x2, waiting for transfers between devices, all_sum(): x = lax.all_to_all(x, group, 0, 0, tiled=True)  10.6 us
    all_to_all x2, starting transfers between devices, all_sum(): x = lax.all_to_all(x, group, 0, 0, tiled=True)  9.54 us
    pallas_call x1, Pallas kernels, shards(): pl.pallas_call(functools.partial(position_kernel, paired, cores), out_sha...  9.15 us
    ppermute x5, starting transfers between devices, from_near(): return lax.ppermute(x, 'core', [(0, 1), (1, 0)])  6.23 us
    pallas_call x1, Pallas kernels, shards(): pl.pallas_call(prepare_kernel, out_shape=[shape(2, width, 2 * LANES), sha...  3.07 us
    ppermute x1, starting transfers between devices, shards(): beside = [lax.ppermute(cells, 'col', [(0, 1), (1, 0)])]  3.06 us
    sin x1, local copies, waits for them, and re-layouts, shards(): jnp.sin(propagator_phase)  2.38 us
    unnamed x24, local copies, waits for them, and re-layouts  2.31 us
  transfers between devices with their start and end apart: 12, of which 6 were waited for; matrix products, arithmetic and copies ran while one was open for 5% of the time, Pallas kernels for 8%

profile of v3, /device:TPU:0, one launch (start us, length us, event | category | flops | bytes accessed | tf_op | source)
XLA Modules:
  0.0 61.9 jit_solution(1177184056782987196)
XLA Ops:
  0.6 3.1 %collective-permute-start = (f32[2,2,96,96]{3,2,1,0:T(8,128)}, f32[2,2,96,96]{3,2,1,0:T(8,128)S(1)}, u32[]{:S(2)}, u32[]{:S(2)}) collective-permute-start(f32[2,2,96,96]{3,2,1,0:T(8,128)} %object_ref.1), channel_id=1, source_target_pairs={{0,1},{1,0},{2,3},{3,2},{4,5},{5,4},{6,7},{7,6},{8,9},{9,8},{10,11... | collective-permute-start | bytes 442376 | tf_op jit(solution)/shard_map/ppermute | solution.py:537
  3.7 0.7 %collective-permute-start.3 = (f32[2,2,96,96]{3,2,1,0:T(8,128)}, f32[2,2,96,96]{3,2,1,0:T(8,128)S(1)}, u32[]{:S(2)}, u32[]{:S(2)}) collective-permute-start(f32[2,2,96,96]{3,2,1,0:T(8,128)} %object_ref.1), channel_id=1, source_target_pairs={{2,4},{6,8},{10,12},{14,16},{18,20},{22,24},{26,28},{4,2},{8,6},{1... | collective-permute-start | bytes 442376 | tf_op jit(solution)/shard_map/ppermute | solution.py:503
  4.4 2.9 %collective-permute-start.1 = (f32[2,2,96,96]{3,2,1,0:T(8,128)}, f32[2,2,96,96]{3,2,1,0:T(8,128)S(1)}, u32[]{:S(2)}, u32[]{:S(2)}) collective-permute-start(f32[2,2,96,96]{3,2,1,0:T(8,128)} %object_ref.1), channel_id=1, source_target_pairs={{0,2},{2,0},{1,3},{3,1},{4,6},{6,4},{5,7},{7,5},{8,10},{10,8},{9,1... | collective-permute-start | bytes 442376 | tf_op jit(solution)/shard_map/ppermute | solution.py:495
  7.9 0.9 %collective-permute-done.refs_1_ = f32[2,2,96,96]{3,2,1,0:T(8,128)S(1)} collective-permute-done((f32[2,2,96,96]{3,2,1,0:T(8,128)}, f32[2,2,96,96]{3,2,1,0:T(8,128)S(1)}, u32[]{:S(2)}, u32[]{:S(2)}) %collective-permute-start) | collective-permute-done | bytes 147488 | tf_op jit(solution)/shard_map/ppermute | solution.py:537
  8.8 0.7 %collective-permute-start.4 = (f32[2,2,96,96]{3,2,1,0:T(8,128)S(1)}, f32[2,2,96,96]{3,2,1,0:T(8,128)S(1)}, u32[]{:S(2)}, u32[]{:S(2)}) collective-permute-start(f32[2,2,96,96]{3,2,1,0:T(8,128)S(1)} %collective-permute-done.refs_1_), channel_id=1, source_target_pairs={{2,4},{6,8},{10,12},{14,16},{18,20},{22,24},{26,28},{4,2},{8,6},{1... | collective-permute-start | bytes 442376 | tf_op jit(solution)/shard_map/ppermute | solution.py:503
  9.5 3.1 %collective-permute-start.2 = (f32[2,2,96,96]{3,2,1,0:T(8,128)S(1)}, f32[2,2,96,96]{3,2,1,0:T(8,128)S(1)}, u32[]{:S(2)}, u32[]{:S(2)}) collective-permute-start(f32[2,2,96,96]{3,2,1,0:T(8,128)S(1)} %collective-permute-done.refs_1_), channel_id=1, source_target_pairs={{0,2},{2,0},{1,3},{3,1},{4,6},{6,4},{5,7},{7,5},{8,10},{10,8},{9,1... | collective-permute-start | bytes 442376 | tf_op jit(solution)/shard_map/ppermute | solution.py:495
  12.6 2.4 %fusion = (f32[192,192]{1,0:T(8,128)}, f32[192,192]{1,0:T(8,128)}) fusion(f32[192,192]{1,0:T(8,128)} %param.14), kind=kLoop, calls=%fused_computation | loop fusion | bytes 442368 | tf_op jit(solution)/shard_map/sin | solution.py:557
  15.0 0.0 copy-done.3
  15.0 3.1 %shard_map.131 = (f32[2,192,256]{2,1,0:T(8,128)}, f32[2,192,256]{2,1,0:T(8,128)}, f32[2,192,256]{2,1,0:T(8,128)}) custom-call(f32[2,192,192]{2,1,0:T(8,128)} %probe_ref.3, f32[192,192]{1,0:T(8,128)} %get-tuple-element.23.cosine_ref, f32[192,192]{1,0:T(8,128)} %get-tuple-element.22.sine_ref, f32[1,1,2,192,192]{4,3,2,1,0:T(8,128)} %measured_ref.1, ...), custom_call_target="tpu_custom_call" | custom-call | tf_op jit(solution)/shard_map/pallas_call | solution.py:545
  18.1 0.0 collective-permute-done.3.refs_4_
  18.1 0.0 collective-permute-done.1.refs_2_
  18.1 0.0 copy-start.5
  18.1 0.0 collective-permute-done.4.refs_5_
  18.1 0.0 copy-start.6
  18.1 0.0 collective-permute-done.2.refs_3_
  18.1 0.0 copy-start.7
  18.1 0.6 %copy-done.4 = f32[2,2,96,96]{3,2,1,0:T(8,128)} copy-done((f32[2,2,96,96]{3,2,1,0:T(8,128)}, f32[2,2,96,96]{3,2,1,0:T(8,128)S(1)}, u32[]{:S(2)}) %copy-start.4) | copy-done | bytes 147480
  18.7 0.1 copy-done.5
  18.8 0.1 copy-done.6
  18.9 0.1 copy-done.7
  19.0 9.2 %shard_map.132 = (f32[96,768]{1,0:T(8,128)}, f32[96,768]{1,0:T(8,128)}, f32[96,768]{1,0:T(8,128)}, f32[3,96,128]{2,1,0:T(8,128)}, f32[3,96,128]{2,1,0:T(8,128)}) custom-call(s32[1,1,2,2]{3,2,1,0:T(2,128)} %offsets_ref.1, s32[1,1]{1,0:T(1,128)S(6)} %copy.14.counts_ref, f32[2,2,96,96]{3,2,1,0:T(8,128)} %object_ref.1, f32[2,2,96,96]{3,2,1,0:T(8,128)} %copy-done.3, ...), custom_call_target="tpu_custom_call" | custom-call | tf_op jit(solution)/shard_map/pallas_call | solution.py:578
  28.1 0.1 collective-permute-start.5
  28.2 1.5 %collective-permute-done.5 = f32[3,96,128]{2,1,0:T(8,128)S(1)} collective-permute-done((f32[3,96,128]{2,1,0:T(8,128)}, f32[3,96,128]{2,1,0:T(8,128)S(1)}, u32[]{:S(2)}, u32[]{:S(2)}) %collective-permute-start.5) | collective-permute-done | bytes 147488 | tf_op jit(solution)/shard_map/ppermute | solution.py:495
  29.7 1.7 %add.3 = f32[3,96,128]{2,1,0:T(8,128)} add(f32[3,96,128]{2,1,0:T(8,128)} %get-tuple-element.15, f32[3,96,128]{2,1,0:T(8,128)S(1)} %collective-permute-done.5) | non-fusion elementwise | flops 36864 | bytes 442368 | tf_op jit(solution)/shard_map/add | solution.py:590
  31.4 6.0 %all-to-all-start = ((f32[16,9,2,128]{3,2,1,0:T(2,128)}), f32[16,9,2,128]{3,2,1,0:T(2,128)S(1)}, u32[]{:S(2)}, u32[]{:S(2)}) async-start(f32[16,9,2,128]{3,2,1,0:T(2,128)} %bitcast), calls=%async_computation | async-start | bytes 294912 | tf_op jit(solution)/shard_map/all_to_all | solution.py:516
  37.4 0.0 copy-done.11
  37.4 0.1 collective-permute-start.7
  37.5 0.0 copy-done.10
  37.5 0.7 %collective-permute-start.8 = (f32[96,768]{1,0:T(8,128)S(1)}, f32[96,768]{1,0:T(8,128)S(1)}, u32[]{:S(2)}, u32[]{:S(2)}) collective-permute-start(f32[96,768]{1,0:T(8,128)S(1)} %copy-done.10), channel_id=1, source_target_pairs={{2,4},{6,8},{10,12},{14,16},{18,20},{22,24},{26,28},{4,2},{8,6},{1... | collective-permute-start | bytes 884744 | tf_op jit(solution)/shard_map/ppermute | solution.py:503
  38.2 7.2 %all-to-all-done = f32[16,9,2,128]{3,2,1,0:T(2,128)S(1)} async-done(((f32[16,9,2,128]{3,2,1,0:T(2,128)}), f32[16,9,2,128]{3,2,1,0:T(2,128)S(1)}, u32[]{:S(2)}, u32[]{:S(2)}) %all-to-all-start) | async-done | bytes 147488 | tf_op jit(solution)/shard_map/all_to_all | solution.py:516
  45.4 0.1 reduce_sum.9
  45.4 0.7 %broadcast_in_dim.2 = f32[16,9,2,128]{3,2,1,0:T(2,128)} broadcast(f32[9,2,128]{2,1,0:T(2,128)S(1)} %reduce_sum.9), dimensions={1,2,3} | broadcast | bytes 156672 | tf_op jit(solution)/shard_map/broadcast_in_dim | solution.py:517
  46.1 3.5 %all-to-all-start.1 = ((f32[16,9,2,128]{3,2,1,0:T(2,128)}), f32[16,9,2,128]{3,2,1,0:T(2,128)S(1)}, u32[]{:S(2)}, u32[]{:S(2)}) async-start(f32[16,9,2,128]{3,2,1,0:T(2,128)} %broadcast_in_dim.2), calls=%async_computation.1 | async-start | bytes 294912 | tf_op jit(solution)/shard_map/all_to_all | solution.py:518
  49.6 0.0 collective-permute-done.7.near_ref
  49.6 0.0 copy-start.1
  49.7 0.0 collective-permute-done.8.far_ref
  49.7 0.0 copy-start.2
  49.7 0.7 %copy-done.1 = f32[96,768]{1,0:T(8,128)} copy-done((f32[96,768]{1,0:T(8,128)}, f32[96,768]{1,0:T(8,128)S(1)}, u32[]{:S(2)}) %copy-start.1) | copy-done | bytes 294936
  50.4 0.1 copy-done.2
  50.5 1.9 %shard_map.133 = (f32[96,384]{1,0:T(8,128)}, f32[96,384]{1,0:T(8,128)}) custom-call(f32[96,768]{1,0:T(8,128)} %get-tuple-element.17.own_ref, f32[96,768]{1,0:T(8,128)} %copy-done.1, f32[96,768]{1,0:T(8,128)} %copy-done.2), custom_call_target="tpu_custom_call" | custom-call | tf_op jit(solution)/shard_map/pallas_call | solution.py:599
  52.3 1.8 %collective-permute-start.9 = (f32[96,384]{1,0:T(8,128)}, f32[96,384]{1,0:T(8,128)S(1)}, u32[]{:S(2)}, u32[]{:S(2)}) collective-permute-start(f32[96,384]{1,0:T(8,128)} %get-tuple-element.21), channel_id=1, source_target_pairs={{0,1},{1,0},{2,3},{3,2},{4,5},{5,4},{6,7},{7,6},{8,9},{9,8},{10,11... | collective-permute-start | bytes 442376 | tf_op jit(solution)/shard_map/ppermute | solution.py:606
  54.1 3.4 %all-to-all-done.1 = f32[16,9,2,128]{3,2,1,0:T(2,128)S(1)} async-done(((f32[16,9,2,128]{3,2,1,0:T(2,128)}), f32[16,9,2,128]{3,2,1,0:T(2,128)S(1)}, u32[]{:S(2)}, u32[]{:S(2)}) %all-to-all-start.1) | async-done | bytes 147488 | tf_op jit(solution)/shard_map/all_to_all | solution.py:518
  57.6 0.0 collective-permute-start.6
  57.6 0.8 %collective-permute-done.9.refs_3_ = f32[96,384]{1,0:T(8,128)S(1)} collective-permute-done((f32[96,384]{1,0:T(8,128)}, f32[96,384]{1,0:T(8,128)S(1)}, u32[]{:S(2)}, u32[]{:S(2)}) %collective-permute-start.9) | collective-permute-done | bytes 147488 | tf_op jit(solution)/shard_map/ppermute | solution.py:606
  58.4 0.6 collective-permute-done.6.refs_1_
  59.0 0.1 copy-done.8
  59.0 0.6 copy-done.9
  59.6 2.3 %shard_map.134 = (f32[2,2,96,96]{3,2,1,0:T(8,128)}, f32[2,192,192]{2,1,0:T(8,128)}) custom-call(f32[2,2,96,96]{3,2,1,0:T(8,128)} %object_ref.1, f32[2,192,192]{2,1,0:T(8,128)} %probe_ref.3, f32[3,96,128]{2,1,0:T(8,128)} %bitcast.3, f32[3,96,128]{2,1,0:T(8,128)} %copy-done.9, f32[96,384]{1,0:T(8,128)} %get-tuple-element.20.refs_2_, f32[96,384]{1,0:T(8,128)} %copy-done.8), custom_call_target="tpu_custom_call" | custom-call | tf_op jit(solution)/shard_map/pallas_call | solution.py:609
  (8 shorter events, 0.0 us)
Async XLA Ops:
  0.6 8.2 %collective-permute-start = (f32[2,2,96,96]{3,2,1,0:T(8,128)}, f32[2,2,96,96]{3,2,1,0:T(8,128)S(1)}, u32[]{:S(2)}, u32[]{:S(2)}) collective-permute-start(f32[2,2,96,96]{3,2,1,0:T(8,128)} %object_ref.1), channel_id=1, source_target_pairs={{0,1},{1,0},{2,3},{3,2},{4,5},{5,4},{6,7},{7,6},{8,9},{9,8},{10,11... | collective-permute-start | bytes 442376 | tf_op jit(solution)/shard_map/ppermute | solution.py:537
  3.7 14.4 %collective-permute-start.3 = (f32[2,2,96,96]{3,2,1,0:T(8,128)}, f32[2,2,96,96]{3,2,1,0:T(8,128)S(1)}, u32[]{:S(2)}, u32[]{:S(2)}) collective-permute-start(f32[2,2,96,96]{3,2,1,0:T(8,128)} %object_ref.1), channel_id=1, source_target_pairs={{2,4},{6,8},{10,12},{14,16},{18,20},{22,24},{26,28},{4,2},{8,6},{1... | collective-permute-start | bytes 442376 | tf_op jit(solution)/shard_map/ppermute | solution.py:503
  4.4 13.7 %collective-permute-start.1 = (f32[2,2,96,96]{3,2,1,0:T(8,128)}, f32[2,2,96,96]{3,2,1,0:T(8,128)S(1)}, u32[]{:S(2)}, u32[]{:S(2)}) collective-permute-start(f32[2,2,96,96]{3,2,1,0:T(8,128)} %object_ref.1), channel_id=1, source_target_pairs={{0,2},{2,0},{1,3},{3,1},{4,6},{6,4},{5,7},{7,5},{8,10},{10,8},{9,1... | collective-permute-start | bytes 442376 | tf_op jit(solution)/shard_map/ppermute | solution.py:495
  8.8 6.2 %copy-start.3 = (f32[2,2,96,96]{3,2,1,0:T(8,128)}, f32[2,2,96,96]{3,2,1,0:T(8,128)S(1)}, u32[]{:S(2)}) copy-start(f32[2,2,96,96]{3,2,1,0:T(8,128)S(1)} %collective-permute-done.refs_1_) | copy-start | bytes 442372
  8.8 9.3 %collective-permute-start.4 = (f32[2,2,96,96]{3,2,1,0:T(8,128)S(1)}, f32[2,2,96,96]{3,2,1,0:T(8,128)S(1)}, u32[]{:S(2)}, u32[]{:S(2)}) collective-permute-start(f32[2,2,96,96]{3,2,1,0:T(8,128)S(1)} %collective-permute-done.refs_1_), channel_id=1, source_target_pairs={{2,4},{6,8},{10,12},{14,16},{18,20},{22,24},{26,28},{4,2},{8,6},{1... | collective-permute-start | bytes 442376 | tf_op jit(solution)/shard_map/ppermute | solution.py:503
  9.5 8.6 %collective-permute-start.2 = (f32[2,2,96,96]{3,2,1,0:T(8,128)S(1)}, f32[2,2,96,96]{3,2,1,0:T(8,128)S(1)}, u32[]{:S(2)}, u32[]{:S(2)}) collective-permute-start(f32[2,2,96,96]{3,2,1,0:T(8,128)S(1)} %collective-permute-done.refs_1_), channel_id=1, source_target_pairs={{0,2},{2,0},{1,3},{3,1},{4,6},{6,4},{5,7},{7,5},{8,10},{10,8},{9,1... | collective-permute-start | bytes 442376 | tf_op jit(solution)/shard_map/ppermute | solution.py:495
  18.1 0.7 %copy-start.4 = (f32[2,2,96,96]{3,2,1,0:T(8,128)}, f32[2,2,96,96]{3,2,1,0:T(8,128)S(1)}, u32[]{:S(2)}) copy-start(f32[2,2,96,96]{3,2,1,0:T(8,128)S(1)} %collective-permute-done.3.refs_4_) | copy-start | bytes 442372
  18.1 0.7 %copy-start.5 = (f32[2,2,96,96]{3,2,1,0:T(8,128)}, f32[2,2,96,96]{3,2,1,0:T(8,128)S(1)}, u32[]{:S(2)}) copy-start(f32[2,2,96,96]{3,2,1,0:T(8,128)S(1)} %collective-permute-done.1.refs_2_) | copy-start | bytes 442372
  18.1 0.8 %copy-start.6 = (f32[2,2,96,96]{3,2,1,0:T(8,128)}, f32[2,2,96,96]{3,2,1,0:T(8,128)S(1)}, u32[]{:S(2)}) copy-start(f32[2,2,96,96]{3,2,1,0:T(8,128)S(1)} %collective-permute-done.4.refs_5_) | copy-start | bytes 442372
  18.1 0.9 %copy-start.7 = (f32[2,2,96,96]{3,2,1,0:T(8,128)}, f32[2,2,96,96]{3,2,1,0:T(8,128)S(1)}, u32[]{:S(2)}) copy-start(f32[2,2,96,96]{3,2,1,0:T(8,128)S(1)} %collective-permute-done.2.refs_3_) | copy-start | bytes 442372
  28.1 1.6 %collective-permute-start.5 = (f32[3,96,128]{2,1,0:T(8,128)}, f32[3,96,128]{2,1,0:T(8,128)S(1)}, u32[]{:S(2)}, u32[]{:S(2)}) collective-permute-start(f32[3,96,128]{2,1,0:T(8,128)} %get-tuple-element.16), channel_id=1, source_target_pairs={{0,2},{2,0},{1,3},{3,1},{4,6},{6,4},{5,7},{7,5},{8,10},{10,8},{9,1... | collective-permute-start | bytes 442376 | tf_op jit(solution)/shard_map/ppermute | solution.py:495
  29.7 7.7 %copy-start.11 = (f32[96,768]{1,0:T(8,128)S(1)}, f32[96,768]{1,0:T(8,128)}, u32[]{:S(2)}) copy-start(f32[96,768]{1,0:T(8,128)} %get-tuple-element.18) | copy-start | bytes 884740
  29.7 7.8 %copy-start.10 = (f32[96,768]{1,0:T(8,128)S(1)}, f32[96,768]{1,0:T(8,128)}, u32[]{:S(2)}) copy-start(f32[96,768]{1,0:T(8,128)} %get-tuple-element.19) | copy-start | bytes 884740
  31.4 14.0 %all-to-all-start = ((f32[16,9,2,128]{3,2,1,0:T(2,128)}), f32[16,9,2,128]{3,2,1,0:T(2,128)S(1)}, u32[]{:S(2)}, u32[]{:S(2)}) async-start(f32[16,9,2,128]{3,2,1,0:T(2,128)} %bitcast), calls=%async_computation | async-start | bytes 294912 | tf_op jit(solution)/shard_map/all_to_all | solution.py:516
  37.4 12.2 %collective-permute-start.7 = (f32[96,768]{1,0:T(8,128)S(1)}, f32[96,768]{1,0:T(8,128)S(1)}, u32[]{:S(2)}, u32[]{:S(2)}) collective-permute-start(f32[96,768]{1,0:T(8,128)S(1)} %copy-done.11), channel_id=1, source_target_pairs={{0,2},{2,0},{1,3},{3,1},{4,6},{6,4},{5,7},{7,5},{8,10},{10,8},{9,1... | collective-permute-start | bytes 884744 | tf_op jit(solution)/shard_map/ppermute | solution.py:495
  37.5 12.2 %collective-permute-start.8 = (f32[96,768]{1,0:T(8,128)S(1)}, f32[96,768]{1,0:T(8,128)S(1)}, u32[]{:S(2)}, u32[]{:S(2)}) collective-permute-start(f32[96,768]{1,0:T(8,128)S(1)} %copy-done.10), channel_id=1, source_target_pairs={{2,4},{6,8},{10,12},{14,16},{18,20},{22,24},{26,28},{4,2},{8,6},{1... | collective-permute-start | bytes 884744 | tf_op jit(solution)/shard_map/ppermute | solution.py:503
  46.1 11.5 %all-to-all-start.1 = ((f32[16,9,2,128]{3,2,1,0:T(2,128)}), f32[16,9,2,128]{3,2,1,0:T(2,128)S(1)}, u32[]{:S(2)}, u32[]{:S(2)}) async-start(f32[16,9,2,128]{3,2,1,0:T(2,128)} %broadcast_in_dim.2), calls=%async_computation.1 | async-start | bytes 294912 | tf_op jit(solution)/shard_map/all_to_all | solution.py:518
  49.6 0.7 %copy-start.1 = (f32[96,768]{1,0:T(8,128)}, f32[96,768]{1,0:T(8,128)S(1)}, u32[]{:S(2)}) copy-start(f32[96,768]{1,0:T(8,128)S(1)} %collective-permute-done.7.near_ref) | copy-start | bytes 884740
  49.7 0.8 %copy-start.2 = (f32[96,768]{1,0:T(8,128)}, f32[96,768]{1,0:T(8,128)S(1)}, u32[]{:S(2)}) copy-start(f32[96,768]{1,0:T(8,128)S(1)} %collective-permute-done.8.far_ref) | copy-start | bytes 884740
  52.3 6.0 %collective-permute-start.9 = (f32[96,384]{1,0:T(8,128)}, f32[96,384]{1,0:T(8,128)S(1)}, u32[]{:S(2)}, u32[]{:S(2)}) collective-permute-start(f32[96,384]{1,0:T(8,128)} %get-tuple-element.21), channel_id=1, source_target_pairs={{0,1},{1,0},{2,3},{3,2},{4,5},{5,4},{6,7},{7,6},{8,9},{9,8},{10,11... | collective-permute-start | bytes 442376 | tf_op jit(solution)/shard_map/ppermute | solution.py:606
  57.6 1.4 %copy-start = (f32[16,9,2,128]{3,2,1,0:T(2,128)}, f32[16,9,2,128]{3,2,1,0:T(2,128)S(1)}, u32[]{:S(2)}) copy-start(f32[16,9,2,128]{3,2,1,0:T(2,128)S(1)} %all-to-all-done.1) | copy-start | bytes 442372
  57.6 1.4 %collective-permute-start.6 = (f32[3,96,128]{2,1,0:T(8,128)S(1)}, f32[3,96,128]{2,1,0:T(8,128)S(1)}, u32[]{:S(2)}, u32[]{:S(2)}) collective-permute-start(f32[3,96,128]{2,1,0:T(8,128)S(1)} %bitcast.2), channel_id=1, source_target_pairs={{0,2},{2,0},{1,3},{3,1},{4,6},{6,4},{5,7},{7,5},{8,10},{10,8},{9,1... | collective-permute-start | bytes 442376 | tf_op jit(solution)/shard_map/ppermute | solution.py:495
  58.4 0.7 %copy-start.8 = (f32[96,384]{1,0:T(8,128)}, f32[96,384]{1,0:T(8,128)S(1)}, u32[]{:S(2)}) copy-start(f32[96,384]{1,0:T(8,128)S(1)} %collective-permute-done.9.refs_3_) | copy-start | bytes 442372
  58.9 0.7 %copy-start.9 = (f32[3,96,128]{2,1,0:T(8,128)}, f32[3,96,128]{2,1,0:T(8,128)S(1)}, u32[]{:S(2)}) copy-start(f32[3,96,128]{2,1,0:T(8,128)S(1)} %collective-permute-done.6.refs_1_) | copy-start | bytes 442372

commit v4 on v3

--- a/solution.py
+++ b/solution.py
@@ -170,18 +170,18 @@
         acc,
         window,
         carried,
-        data,
-        out_right,
-        mid,
-        out_left,
         terms,
-    ) = refs[3 * sides + 10 + cores :]
+    ) = refs[3 * sides + 10 + cores : 3 * sides + 15 + cores]
     slots = measured_ref.shape[0]
+    work = refs[3 * sides + 15 + cores :]
+    data, out_right, mid, out_left = (work[k * slots : (k + 1) * slots] for k in range(4))
     width = wave_ref.shape[1]
     half = width // 2
     tile = obj.shape[2] // 3
     total = slots * width
     step = 16
+    part_rows = half // 2
+    lag = 2
     column_of = lax.axis_index("col")
     row_starts = [pl.multiple_of(place * tile, 8) for place in row_places(cores)]
 
@@ -227,82 +227,91 @@
     span = 2 * LANES
 
     def put(slot, block, row, a, b):
-        rows = pl.ds((2 * slot + block) * width + row, step)
+        rows = pl.ds(block * width + row, step)
         high, low = halves_of(jnp.concatenate([a, b], 1))
-        data[rows, :span] = high
-        data[rows, span:] = low
-
-    def multiply_right():
-        for slot in range(slots):
-            rows = slice(2 * slot * width, 2 * (slot + 1) * width)
-            left = jnp.concatenate([data[rows, :], data[rows, :span]], 1)
-            out_right[rows, :] = jnp.dot(left, right_ref[...], preferred_element_type=f32)
+        data[slot][rows, :span] = high
+        data[slot][rows, span:] = low
+
+    def multiply_right(slot):
+        for start in range(0, 2 * width, width):
+            rows = slice(start, start + width)
+            left = jnp.concatenate([data[slot][rows, :], data[slot][rows, :span]], 1)
+            out_right[slot][rows, :] = jnp.dot(
+                left, right_ref[...], preferred_element_type=f32
+            )
+            yield
 
     def put_mid(slot, block, start, first, second):
         for part in range(2):
             high, low = halves_of(jnp.concatenate([first[part], second[part]], 1))
-            mid[slot, block, pl.ds(part * half + start, step), :] = high
-            mid[slot, block, pl.ds((2 + part) * half + start, step), :] = low
-            mid[slot, block, pl.ds((4 + part) * half + start, step), :] = high
-
-    def multiply_left():
-        for slot in range(slots):
-            for block in range(2):
-                out_left[slot, block] = jnp.dot(
-                    left_ref[...], mid[slot, block], preferred_element_type=f32
-                )
+            mid[slot][block, pl.ds(part * half + start, step), :] = high
+            mid[slot][block, pl.ds((2 + part) * half + start, step), :] = low
+            mid[slot][block, pl.ds((4 + part) * half + start, step), :] = high
+
+    def multiply_left(slot):
+        for block in range(2):
+            out_left[slot][block] = jnp.dot(
+                left_ref[...], mid[slot][block], preferred_element_type=f32
+            )
+            yield
 
     def get_right(slot, block, row):
-        rows = pl.ds((2 * slot + block) * width + row, step)
-        return out_right[rows, :LANES], out_right[rows, LANES:]
+        rows = pl.ds(block * width + row, step)
+        return out_right[slot][rows, :LANES], out_right[slot][rows, LANES:]
 
     def get_left(slot, block, j, start):
         columns = slice(j * LANES, (j + 1) * LANES)
         return (
-            out_left[slot, block, pl.ds(start, step), columns],
-            out_left[slot, block, pl.ds(half + start, step), columns],
+            out_left[slot][block, pl.ds(start, step), columns],
+            out_left[slot][block, pl.ds(half + start, step), columns],
         )
 
-    def forward(source):
-        for slot in range(slots):
-            for row in range(0, width, step):
-                (a0, b0), (a1, b1) = source(slot, row)
-                put(slot, 0, row, a0 + a1, b0 + b1)
-                put(slot, 1, row, *times_conj(*lane_turn, a0 - a1, b0 - b1))
-        multiply_right()
-        for slot in range(slots):
-            for row in range(0, half, step):
-                turn = row_turn_ref[0, pl.ds(row, step), :], row_turn_ref[1, pl.ds(row, step), :]
-                even, odd = [], []
-                for j in range(2):
-                    a0, b0 = get_right(slot, j, row)
-                    a1, b1 = get_right(slot, j, half + row)
-                    even.append((a0 + a1, b0 + b1))
-                    odd.append(times_conj(*turn, a0 - a1, b0 - b1))
-                put_mid(slot, 0, row, *even)
-                put_mid(slot, 1, row, *odd)
-        multiply_left()
-
-    def inverse(source):
-        for slot in range(slots):
-            for row in range(0, width, step):
-                for j, (a, b) in enumerate(source(slot, row)):
-                    put(slot, j, row, a, b)
-        multiply_right()
-        for slot in range(slots):
-            for row in range(0, width, step):
-                a0, b0 = get_right(slot, 0, row)
-                a1, b1 = times_conj(*lane_turn, *get_right(slot, 1, row))
-                put_mid(slot, row // half, row % half, (a0 + a1, b0 + b1), (a0 - a1, b0 - b1))
-        multiply_left()
+    def row_turn(row):
+        return row_turn_ref[0, pl.ds(row, step), :], row_turn_ref[1, pl.ds(row, step), :]
+
+    def forward(slot, source):
+        for row in range(0, half, step):
+            for side, ((a0, b0), (a1, b1)) in enumerate(source(slot, row)):
+                place = side * half + row
+                put(slot, 0, place, a0 + a1, b0 + b1)
+                put(slot, 1, place, *times_conj(*lane_turn, a0 - a1, b0 - b1))
+            if row % part_rows == part_rows - step:
+                yield
+        yield from multiply_right(slot)
+        for row in range(0, half, step):
+            even, odd = [], []
+            for j in range(2):
+                a0, b0 = get_right(slot, j, row)
+                a1, b1 = get_right(slot, j, half + row)
+                even.append((a0 + a1, b0 + b1))
+                odd.append(times_conj(*row_turn(row), a0 - a1, b0 - b1))
+            put_mid(slot, 0, row, *even)
+            put_mid(slot, 1, row, *odd)
+            if row % part_rows == part_rows - step:
+                yield
+        yield from multiply_left(slot)
+
+    def inverse(slot, source):
+        for row in range(0, width, step):
+            for j, (a, b) in enumerate(source(slot, row)):
+                put(slot, j, row, a, b)
+            if row % (2 * part_rows) == 2 * part_rows - step:
+                yield
+        yield from multiply_right(slot)
+        for row in range(0, width, step):
+            a0, b0 = get_right(slot, 0, row)
+            a1, b1 = times_conj(*lane_turn, *get_right(slot, 1, row))
+            put_mid(slot, row // half, row % half, (a0 + a1, b0 + b1), (a0 - a1, b0 - b1))
+            if row % (2 * part_rows) == 2 * part_rows - step:
+                yield
+        yield from multiply_left(slot)
 
     def frequency(slot, row, j):
         return get_left(slot, row // half, j, row % half)
 
     def natural(slot, row, j):
         b0, a0 = get_left(slot, 0, j, row)
-        turn = row_turn_ref[0, pl.ds(row, step), :], row_turn_ref[1, pl.ds(row, step), :]
-        b1, a1 = times_conj(*turn, *get_left(slot, 1, j, row))
+        b1, a1 = times_conj(*row_turn(row), *get_left(slot, 1, j, row))
         return (a0 + a1, b0 + b1), (a0 - a1, b0 - b1)
 
     def at(ref, first, row, j):
@@ -310,9 +319,9 @@
         columns = slice(j * LANES, (j + 1) * LANES)
         return ref[first, rows, columns], ref[first + 1, rows, columns]
 
-    def seen(first, slot, row, j):
+    def seen(ref, first, slot, row, j):
         rows = pl.ds(slot * width + row, step)
-        return window[first, j, rows, :], window[first + 1, j, rows, :]
+        return ref[first, j, rows, :], ref[first + 1, j, rows, :]
 
     def keep(ref, first, slot, row, j, real, imag):
         rows = pl.ds(slot * width + row, step)
@@ -320,72 +329,73 @@
         ref[first + 1, j, rows, :] = imag
 
     def entry(slot, row):
-        return [times(*at(wave_ref, 0, row, j), *seen(0, slot, row, j)) for j in range(2)]
-
-    def propagate(slot, row):
-        out = []
-        for j in range(2):
-            real, imag = times(*at(trans_ref, 0, row, j), *frequency(slot, row, j))
-            out.append((imag, real))
-        return out
-
-    def residual(slot, row):
-        out = []
-        for j in range(2):
-            real, imag = frequency(slot, row, j)
-            columns = slice(j * LANES, (j + 1) * LANES)
-            factor = real * real + imag * imag - measured_ref[slot, pl.ds(row, step), columns]
-            out.append((factor * imag, factor * real))
-        return out
-
-    def propagate_back(slot, row):
-        out = []
-        for j in range(2):
-            real, imag = times_conj(*at(trans_ref, 0, row, j), *frequency(slot, row, j))
-            out.append((imag, real))
-        return out
-
-    def each_natural(handle):
-        for slot in range(slots):
-            for row in range(0, half, step):
-                for j in range(2):
-                    top, bottom = natural(slot, row, j)
-                    handle(slot, row, j, *top)
-                    handle(slot, half + row, j, *bottom)
-
-    forward(entry)
-    inverse(propagate)
-
+        return [
+            [times(*at(wave_ref, 0, place, j), *seen(window, 0, slot, place, j)) for j in range(2)]
+            for place in (row, half + row)
+        ]
+
+    def from_natural(handle):
+        def source(slot, row):
+            pairs = [natural(slot, row, j) for j in range(2)]
+            return [
+                [handle(slot, side * half + row, j, *pairs[j][side]) for j in range(2)]
+                for side in range(2)
+            ]
+
+        return source
+
+    def from_frequency(handle):
+        def source(slot, row):
+            out = []
+            for j in range(2):
+                real, imag = handle(slot, row, j, *frequency(slot, row, j))
+                out.append((imag, real))
+            return out
+
+        return source
+
+    @from_frequency
+    def propagate(slot, row, j, real, imag):
+        return times(*at(trans_ref, 0, row, j), real, imag)
+
+    @from_natural
     def leave(slot, row, j, real, imag):
         keep(carried, 0, slot, row, j, real, imag)
-        keep(carried, 2, slot, row, j, *times(real, imag, *seen(2, slot, row, j)))
-
-    each_natural(leave)
-
-    def leaving(slot, row):
-        rows = pl.ds(slot * width + row, step)
-        return [(carried[2, j, rows, :], carried[3, j, rows, :]) for j in range(2)]
-
-    forward(leaving)
-    inverse(residual)
-
+        return times(real, imag, *seen(window, 2, slot, row, j))
+
+    @from_frequency
+    def residual(slot, row, j, real, imag):
+        columns = slice(j * LANES, (j + 1) * LANES)
+        factor = real * real + imag * imag - measured_ref[slot, pl.ds(row, step), columns]
+        return factor * real, factor * imag
+
+    @from_natural
     def before(slot, row, j, real, imag):
-        rows = pl.ds(slot * width + row, step)
-        keep(
-            carried, 2, slot, row, j, *times_conj(*seen(2, slot, row, j), real, imag)
-        )
-        keep(
-            window,
-            2,
-            slot,
-            row,
-            j,
-            *times_conj(carried[0, j, rows, :], carried[1, j, rows, :], real, imag),
-        )
-
-    each_natural(before)
-    forward(leaving)
-    inverse(propagate_back)
+        inner = times_conj(*seen(window, 2, slot, row, j), real, imag)
+        second = times_conj(*seen(carried, 0, slot, row, j), real, imag)
+        keep(window, 2, slot, row, j, *second)
+        return inner
+
+    @from_frequency
+    def propagate_back(slot, row, j, real, imag):
+        return times_conj(*at(trans_ref, 0, row, j), real, imag)
+
+    def stages(slot):
+        yield from forward(slot, entry)
+        yield from inverse(slot, propagate)
+        yield from forward(slot, leave)
+        yield from inverse(slot, residual)
+        yield from forward(slot, before)
+        yield from inverse(slot, propagate_back)
+
+    running = [stages(slot) for slot in range(slots)]
+    turn = 0
+    while any(x is not None for x in running):
+        for slot in range(slots):
+            if running[slot] is not None and turn >= slot * lag:
+                if next(running[slot], "end") == "end":
+                    running[slot] = None
+        turn += 1
 
     live = [(slot < counts_ref[0, 0]).astype(f32) for slot in range(slots)]
     core = lax.axis_index("core")
@@ -396,7 +406,7 @@
             for slot in range(slots):
                 for side, (real, imag) in enumerate(natural(slot, row, j)):
                     place = side * half + row
-                    term = times_conj(*seen(0, slot, place, j), real, imag)
+                    term = times_conj(*seen(window, 0, slot, place, j), real, imag)
                     keep(
                         window,
                         0,
@@ -527,7 +537,8 @@
     cols_count = lax.axis_size("col")
     devices = lax.axis_size(ROWS) * cols_count
     paired = cols_count == 2
-    params = pltpu.CompilerParams(vmem_limit_bytes=60 * 1024 * 1024)
+    large = pltpu.CompilerParams(vmem_limit_bytes=18 * 1024 * 1024)
+    small = pltpu.CompilerParams(vmem_limit_bytes=6 * 1024 * 1024)
 
     def shape(*dims, kind=f32):
         return jax.ShapeDtypeStruct(dims, kind)
@@ -551,6 +562,7 @@
         ],
         in_specs=[VMEM] * 6,
         out_specs=[VMEM] * 3,
+        compiler_params=small,
     )(
         probe,
         jnp.cos(propagator_phase),
@@ -567,21 +579,21 @@
         pltpu.VMEM((4, 3, 3 * tile, LANES), f32),
         pltpu.VMEM((4, sides, 3 * tile, LANES), f32),
         pltpu.VMEM((4, 2, total, LANES), f32),
-        pltpu.VMEM((4, 2, total, LANES), f32),
-        pltpu.VMEM((2 * total, 4 * LANES), bf16),
-        pltpu.VMEM((2 * total, 2 * LANES), f32),
-        pltpu.VMEM((slots, 2, 3 * width, 2 * LANES), bf16),
-        pltpu.VMEM((slots, 2, width, 2 * LANES), f32),
+        pltpu.VMEM((2, 2, total, LANES), f32),
+        pltpu.VMEM((cores, 3, width // cores, LANES), f32),
     ]
+    scratch += [pltpu.VMEM((2 * width, 4 * LANES), bf16)] * slots
+    scratch += [pltpu.VMEM((2 * width, 2 * LANES), f32)] * slots
+    scratch += [pltpu.VMEM((2, 3 * width, 2 * LANES), bf16)] * slots
+    scratch += [pltpu.VMEM((2, width, 2 * LANES), f32)] * slots
     term = shape(3, width // cores, LANES)
-    scratch.append(pltpu.VMEM((cores,) + term.shape, f32))
     strips = pl.pallas_call(
         functools.partial(position_kernel, paired, cores),
         out_shape=[strip] * 3 + [term] * cores,
         in_specs=[SMEM, SMEM] + [VMEM] * (3 * sides + 7),
         out_specs=[VMEM] * (3 + cores),
         scratch_shapes=scratch,
-        compiler_params=params,
+        compiler_params=large,
     )(offsets, counts, *own, *near, *far, wave, trans, intensities, *matrices(width))
     own_strip, near_strip, far_strip = strips[:3]
     terms = strips[3:]
@@ -601,6 +613,7 @@
         out_shape=[share] * sides,
         in_specs=[VMEM] * 3,
         out_specs=[VMEM] * sides,
+        compiler_params=small,
     )(own_strip, near_strip, far_strip)
     if paired:
         received = [lax.ppermute(parts[1], "col", [(0, 1), (1, 0)])]
@@ -611,6 +624,7 @@
         out_shape=[shape(*object_slices.shape), shape(*probe.shape)],
         in_specs=[VMEM] * (3 + cores + len(received)),
         out_specs=[VMEM] * 2,
+        compiler_params=small,
     )(object_slices, probe, *sums, parts[0], *received)
 
 

time: 62.4 us -> 56.3 us (0.902)
  Pallas kernels: 16.4 us -> 8.7 us
  starting transfers between devices: 22.6 us -> 24.6 us
  waiting for transfers between devices: 14.3 us -> 16.3 us
  local copies, waits for them, and re-layouts: 5.39 us -> 4.03 us
  other arithmetic: 1.72 us -> 0.74 us
    pallas_call x1, Pallas kernels: 9.15 us -> 6.61 us  [shards(): pl.pallas_call(functools.partial(position_kernel, paired, cores), out_sha...]
    all_to_all x2, waiting for transfers between devices: 10.6 us -> 13.1 us  [all_sum(): x = lax.all_to_all(x, group, 0, 0, tiled=True)]
    pallas_call x1, Pallas kernels: 3.07 us -> 0.98 us  [shards(): pl.pallas_call(prepare_kernel, out_shape=[shape(2, width, 2 * LANES), sha...]
    pallas_call x1, Pallas kernels: 1.88 us -> 0.05 us  [shards(): pl.pallas_call(fold_kernel, out_shape=[share] * sides, in_specs=[VMEM] *...]
    pallas_call x1, Pallas kernels: 2.31 us -> 1.06 us  [shards(): pl.pallas_call(functools.partial(update_kernel, probe_rate / (slots * dev...]
    all_to_all x2, starting transfers between devices: 9.54 us -> 10.6 us  [all_sum(): x = lax.all_to_all(x, group, 0, 0, tiled=True)]
    add x1, other arithmetic: 1.66 us -> 0.68 us  [shards(): mine = all_sum(terms[0] + from_near(terms[1], cores), ('pair', 'col'))]
    ppermute x5, starting transfers between devices: 6.23 us -> 7.08 us  [from_near(): return lax.ppermute(x, 'core', [(0, 1), (1, 0)])]
  transfers between devices with their start and end apart: 12 -> 12, of which waited for: 6 -> 5; matrix products, arithmetic and copies ran while one was open for 5% -> 4% of each run, Pallas kernels for 8% -> 2%
where the time goes in v4:
time: 56.3 us; the launch traced here: 55.9 us
  starting transfers between devices  24.6 us (44%)
  waiting for transfers between devices  16.3 us (29%)
  Pallas kernels  8.7 us (15%)
  local copies, waits for them, and re-layouts  4.03 us (7%)
  between operations  1.49 us (3%)
  other arithmetic  0.74 us (1%)
    all_to_all x2, waiting for transfers between devices, all_sum(): x = lax.all_to_all(x, group, 0, 0, tiled=True)  13.1 us
    all_to_all x2, starting transfers between devices, all_sum(): x = lax.all_to_all(x, group, 0, 0, tiled=True)  10.6 us
    ppermute x5, starting transfers between devices, from_near(): return lax.ppermute(x, 'core', [(0, 1), (1, 0)])  7.08 us
    pallas_call x1, Pallas kernels, shards(): pl.pallas_call(functools.partial(position_kernel, paired, cores), out_sha...  6.61 us
    ppermute x1, starting transfers between devices, shards(): beside = [lax.ppermute(cells, 'col', [(0, 1), (1, 0)])]  3.06 us
    ppermute x5, waiting for transfers between devices, from_near(): return lax.ppermute(x, 'core', [(0, 1), (1, 0)])  2.38 us
    ppermute x3, starting transfers between devices, from_far(): return lax.ppermute(x, ROWS, pairs)  2 us
    ppermute x1, starting transfers between devices, shards(): received = [lax.ppermute(parts[1], 'col', [(0, 1), (1, 0)])]  1.87 us
  transfers between devices with their start and end apart: 12, of which 5 were waited for; matrix products, arithmetic and copies ran while one was open for 4% of the time, Pallas kernels for 2%

profile of v4, /device:TPU:0, one launch (start us, length us, event | category | flops | bytes accessed | tf_op | source)
XLA Modules:
  0.0 55.9 jit_solution(11345546439197193682)
XLA Ops:
  0.6 0.0 copy-start
  0.6 3.1 %collective-permute-start = (f32[2,2,96,96]{3,2,1,0:T(8,128)}, f32[2,2,96,96]{3,2,1,0:T(8,128)S(1)}, u32[]{:S(2)}, u32[]{:S(2)}) collective-permute-start(f32[2,2,96,96]{3,2,1,0:T(8,128)} %object_ref.1), channel_id=1, source_target_pairs={{0,1},{1,0},{2,3},{3,2},{4,5},{5,4},{6,7},{7,6},{8,9},{9,8},{10,11... | collective-permute-start | bytes 442376 | tf_op jit(solution)/shard_map/ppermute | solution.py:548
  3.7 0.7 %collective-permute-start.3 = (f32[2,2,96,96]{3,2,1,0:T(8,128)}, f32[2,2,96,96]{3,2,1,0:T(8,128)S(1)}, u32[]{:S(2)}, u32[]{:S(2)}) collective-permute-start(f32[2,2,96,96]{3,2,1,0:T(8,128)} %object_ref.1), channel_id=1, source_target_pairs={{2,4},{6,8},{10,12},{14,16},{18,20},{22,24},{26,28},{4,2},{8,6},{1... | collective-permute-start | bytes 442376 | tf_op jit(solution)/shard_map/ppermute | solution.py:513
  4.4 2.9 %collective-permute-start.1 = (f32[2,2,96,96]{3,2,1,0:T(8,128)}, f32[2,2,96,96]{3,2,1,0:T(8,128)S(1)}, u32[]{:S(2)}, u32[]{:S(2)}) collective-permute-start(f32[2,2,96,96]{3,2,1,0:T(8,128)} %object_ref.1), channel_id=1, source_target_pairs={{0,2},{2,0},{1,3},{3,1},{4,6},{6,4},{5,7},{7,5},{8,10},{10,8},{9,1... | collective-permute-start | bytes 442376 | tf_op jit(solution)/shard_map/ppermute | solution.py:505
  7.9 0.0 copy-start.6
  7.9 0.0 copy-start.7
  8.0 0.9 %collective-permute-done.refs_1_ = f32[2,2,96,96]{3,2,1,0:T(8,128)S(1)} collective-permute-done((f32[2,2,96,96]{3,2,1,0:T(8,128)}, f32[2,2,96,96]{3,2,1,0:T(8,128)S(1)}, u32[]{:S(2)}, u32[]{:S(2)}) %collective-permute-start) | collective-permute-done | bytes 147488 | tf_op jit(solution)/shard_map/ppermute | solution.py:548
  8.8 0.7 %collective-permute-start.4 = (f32[2,2,96,96]{3,2,1,0:T(8,128)S(1)}, f32[2,2,96,96]{3,2,1,0:T(8,128)S(1)}, u32[]{:S(2)}, u32[]{:S(2)}) collective-permute-start(f32[2,2,96,96]{3,2,1,0:T(8,128)S(1)} %collective-permute-done.refs_1_), channel_id=1, source_target_pairs={{2,4},{6,8},{10,12},{14,16},{18,20},{22,24},{26,28},{4,2},{8,6},{1... | collective-permute-start | bytes 442376 | tf_op jit(solution)/shard_map/ppermute | solution.py:513
  9.5 3.1 %collective-permute-start.2 = (f32[2,2,96,96]{3,2,1,0:T(8,128)S(1)}, f32[2,2,96,96]{3,2,1,0:T(8,128)S(1)}, u32[]{:S(2)}, u32[]{:S(2)}) collective-permute-start(f32[2,2,96,96]{3,2,1,0:T(8,128)S(1)} %collective-permute-done.refs_1_), channel_id=1, source_target_pairs={{0,2},{2,0},{1,3},{3,1},{4,6},{6,4},{5,7},{7,5},{8,10},{10,8},{9,1... | collective-permute-start | bytes 442376 | tf_op jit(solution)/shard_map/ppermute | solution.py:505
  12.6 1.6 %fusion = (f32[192,192]{1,0:T(8,128)S(1)}, f32[192,192]{1,0:T(8,128)S(1)}) fusion(f32[192,192]{1,0:T(8,128)} %param.14), kind=kLoop, calls=%fused_computation | loop fusion | bytes 442368 | tf_op jit(solution)/shard_map/sin | solution.py:569
  14.2 0.0 copy-done
  14.2 0.0 copy-done.6
  14.2 0.0 copy-done.7
  14.3 0.0 copy-start.3
  14.3 1.0 %copy-done.3 = f32[1,1,2,192,192]{4,3,2,1,0:T(8,128)S(1)} copy-done((f32[1,1,2,192,192]{4,3,2,1,0:T(8,128)S(1)}, f32[1,1,2,192,192]{4,3,2,1,0:T(8,128)}, u32[]{:S(2)}) %copy-start.3) | copy-done | bytes 294936
  15.3 0.0 copy-start.1
  15.3 0.0 copy-start.8
  15.3 1.0 %shard_map.131 = (f32[2,192,256]{2,1,0:T(8,128)S(1)}, f32[2,192,256]{2,1,0:T(8,128)S(1)}, f32[2,192,256]{2,1,0:T(8,128)S(1)}) custom-call(f32[2,192,192]{2,1,0:T(8,128)S(1)} %copy-done, f32[192,192]{1,0:T(8,128)S(1)} %get-tuple-element.23.cosine_ref, f32[192,192]{1,0:T(8,128)S(1)} %get-tuple-element.22.sine_ref, f32[1,1,2,192,192]{4,3,2,1,0:T(8,128)S(1)} %copy-done.3, ...), custom_call_target="tpu_custom_call" | custom-call | tf_op jit(solution)/shard_map/pallas_call | solution.py:556
  16.3 0.0 collective-permute-done.3.refs_4_
  16.3 0.0 collective-permute-done.1.refs_2_
  16.3 0.0 collective-permute-done.4.refs_5_
  16.3 0.0 collective-permute-done.2.refs_3_
  16.3 0.0 copy-start.9
  16.3 0.0 copy-done.1
  16.3 0.0 copy-done.2
  16.4 0.1 copy-done.4
  16.4 0.0 copy-done.5
  16.4 0.0 copy-done.8
  16.4 0.6 %copy-done.9 = s32[1,1,2,2]{3,2,1,0:T(2,128)S(1)} copy-done((s32[1,1,2,2]{3,2,1,0:T(2,128)S(1)}, s32[1,1,2,2]{3,2,1,0:T(2,128)}, u32[]{:S(2)}) %copy-start.9) | copy-done | bytes 40
  17.0 6.6 %shard_map.132 = (f32[96,768]{1,0:T(8,128)S(1)}, f32[96,768]{1,0:T(8,128)S(1)}, f32[96,768]{1,0:T(8,128)S(1)}, f32[3,96,128]{2,1,0:T(8,128)S(1)}, f32[3,96,128]{2,1,0:T(8,128)S(1)}) custom-call(s32[1,1,2,2]{3,2,1,0:T(2,128)S(1)} %copy-done.9, s32[1,1]{1,0:T(1,128)S(6)} %copy.14.counts_ref, f32[2,2,96,96]{3,2,1,0:T(8,128)S(1)} %copy-done.1, ...), custom_call_target="tpu_custom_call" | custom-call | tf_op jit(solution)/shard_map/pallas_call | solution.py:590
  23.6 1.0 %collective-permute-start.5 = (f32[3,96,128]{2,1,0:T(8,128)S(1)}, f32[3,96,128]{2,1,0:T(8,128)S(1)}, u32[]{:S(2)}, u32[]{:S(2)}) collective-permute-start(f32[3,96,128]{2,1,0:T(8,128)S(1)} %get-tuple-element.16), channel_id=1, source_target_pairs={{0,2},{2,0},{1,3},{3,1},{4,6},{6,4},{5,7},{7,5},{8,10},{10,8},{9,1... | collective-permute-start | bytes 442376 | tf_op jit(solution)/shard_map/ppermute | solution.py:505
  24.6 1.0 %collective-permute-done.5 = f32[3,96,128]{2,1,0:T(8,128)S(1)} collective-permute-done((f32[3,96,128]{2,1,0:T(8,128)S(1)}, f32[3,96,128]{2,1,0:T(8,128)S(1)}, u32[]{:S(2)}, u32[]{:S(2)}) %collective-permute-start.5) | collective-permute-done | bytes 147488 | tf_op jit(solution)/shard_map/ppermute | solution.py:505
  25.6 0.7 %add.3 = f32[3,96,128]{2,1,0:T(8,128)} add(f32[3,96,128]{2,1,0:T(8,128)S(1)} %get-tuple-element.15, f32[3,96,128]{2,1,0:T(8,128)S(1)} %collective-permute-done.5) | non-fusion elementwise | flops 36864 | bytes 442368 | tf_op jit(solution)/shard_map/add | solution.py:602
  26.3 7.1 %all-to-all-start = ((f32[16,9,2,128]{3,2,1,0:T(2,128)}), f32[16,9,2,128]{3,2,1,0:T(2,128)S(1)}, u32[]{:S(2)}, u32[]{:S(2)}) async-start(f32[16,9,2,128]{3,2,1,0:T(2,128)} %bitcast), calls=%async_computation | async-start | bytes 294912 | tf_op jit(solution)/shard_map/all_to_all | solution.py:526
  33.4 0.1 collective-permute-start.7
  33.5 0.7 %collective-permute-start.8 = (f32[96,768]{1,0:T(8,128)S(1)}, f32[96,768]{1,0:T(8,128)S(1)}, u32[]{:S(2)}, u32[]{:S(2)}) collective-permute-start(f32[96,768]{1,0:T(8,128)S(1)} %get-tuple-element.19), channel_id=1, source_target_pairs={{2,4},{6,8},{10,12},{14,16},{18,20},{22,24},{26,28},{4,2},{8,6},{1... | collective-permute-start | bytes 884744 | tf_op jit(solution)/shard_map/ppermute | solution.py:513
  34.2 7.2 %all-to-all-done = f32[16,9,2,128]{3,2,1,0:T(2,128)S(1)} async-done(((f32[16,9,2,128]{3,2,1,0:T(2,128)}), f32[16,9,2,128]{3,2,1,0:T(2,128)S(1)}, u32[]{:S(2)}, u32[]{:S(2)}) %all-to-all-start) | async-done | bytes 147488 | tf_op jit(solution)/shard_map/all_to_all | solution.py:526
  41.3 0.1 reduce_sum.9
  41.4 0.7 %broadcast_in_dim.2 = f32[16,9,2,128]{3,2,1,0:T(2,128)} broadcast(f32[9,2,128]{2,1,0:T(2,128)S(1)} %reduce_sum.9), dimensions={1,2,3} | broadcast | bytes 156672 | tf_op jit(solution)/shard_map/broadcast_in_dim | solution.py:527
  42.1 3.5 %all-to-all-start.1 = ((f32[16,9,2,128]{3,2,1,0:T(2,128)}), f32[16,9,2,128]{3,2,1,0:T(2,128)S(1)}, u32[]{:S(2)}, u32[]{:S(2)}) async-start(f32[16,9,2,128]{3,2,1,0:T(2,128)} %broadcast_in_dim.2), calls=%async_computation.1 | async-start | bytes 294912 | tf_op jit(solution)/shard_map/all_to_all | solution.py:528
  45.6 0.0 collective-permute-done.7.near_ref
  45.6 0.0 collective-permute-done.8.far_ref
  45.7 1.9 %collective-permute-start.9 = (f32[96,384]{1,0:T(8,128)S(1)}, f32[96,384]{1,0:T(8,128)S(1)}, u32[]{:S(2)}, u32[]{:S(2)}) collective-permute-start(f32[96,384]{1,0:T(8,128)S(1)} %get-tuple-element.21), channel_id=1, source_target_pairs={{0,1},{1,0},{2,3},{3,2},{4,5},{5,4},{6,7},{7,6},{8,9},{9,8},{10,11... | collective-permute-start | bytes 442376 | tf_op jit(solution)/shard_map/ppermute | solution.py:619
  47.6 5.9 %all-to-all-done.1 = f32[16,9,2,128]{3,2,1,0:T(2,128)S(1)} async-done(((f32[16,9,2,128]{3,2,1,0:T(2,128)}), f32[16,9,2,128]{3,2,1,0:T(2,128)S(1)}, u32[]{:S(2)}, u32[]{:S(2)}) %all-to-all-start.1) | async-done | bytes 147488 | tf_op jit(solution)/shard_map/all_to_all | solution.py:528
  53.5 0.0 collective-permute-start.6
  53.5 0.0 collective-permute-done.9.refs_3_
  53.5 1.4 %collective-permute-done.6.refs_1_ = f32[3,96,128]{2,1,0:T(8,128)S(1)} collective-permute-done((f32[3,96,128]{2,1,0:T(8,128)S(1)}, f32[3,96,128]{2,1,0:T(8,128)S(1)}, u32[]{:S(2)}, u32[]{:S(2)}) %collective-permute-start.6) | collective-permute-done | bytes 147488 | tf_op jit(solution)/shard_map/ppermute | solution.py:505
  54.8 1.1 %shard_map.134 = (f32[2,2,96,96]{3,2,1,0:T(8,128)}, f32[2,192,192]{2,1,0:T(8,128)}) custom-call(f32[2,2,96,96]{3,2,1,0:T(8,128)S(1)} %copy-done.1, f32[2,192,192]{2,1,0:T(8,128)S(1)} %copy-done, f32[3,96,128]{2,1,0:T(8,128)S(1)} %bitcast.3, f32[3,96,128]{2,1,0:T(8,128)S(1)} %collective-permute-done.6.refs_1_, f32[96,384]{1,0:T(8,128)S(1)} %get-tuple-element.20.refs_2_, ...), custom_call_target="tpu_custom_call" | custom-call | tf_op jit(solution)/shard_map/pallas_call | solution.py:622
  (4 shorter events, 0.1 us)
Async XLA Ops:
  0.6 13.6 %copy-start = (f32[2,192,192]{2,1,0:T(8,128)S(1)}, f32[2,192,192]{2,1,0:T(8,128)}, u32[]{:S(2)}) copy-start(f32[2,192,192]{2,1,0:T(8,128)} %probe_ref.3) | copy-start | bytes 884740
  0.6 8.2 %collective-permute-start = (f32[2,2,96,96]{3,2,1,0:T(8,128)}, f32[2,2,96,96]{3,2,1,0:T(8,128)S(1)}, u32[]{:S(2)}, u32[]{:S(2)}) collective-permute-start(f32[2,2,96,96]{3,2,1,0:T(8,128)} %object_ref.1), channel_id=1, source_target_pairs={{0,1},{1,0},{2,3},{3,2},{4,5},{5,4},{6,7},{7,6},{8,9},{9,8},{10,11... | collective-permute-start | bytes 442376 | tf_op jit(solution)/shard_map/ppermute | solution.py:548
  3.7 12.6 %collective-permute-start.3 = (f32[2,2,96,96]{3,2,1,0:T(8,128)}, f32[2,2,96,96]{3,2,1,0:T(8,128)S(1)}, u32[]{:S(2)}, u32[]{:S(2)}) collective-permute-start(f32[2,2,96,96]{3,2,1,0:T(8,128)} %object_ref.1), channel_id=1, source_target_pairs={{2,4},{6,8},{10,12},{14,16},{18,20},{22,24},{26,28},{4,2},{8,6},{1... | collective-permute-start | bytes 442376 | tf_op jit(solution)/shard_map/ppermute | solution.py:513
  4.4 11.9 %collective-permute-start.1 = (f32[2,2,96,96]{3,2,1,0:T(8,128)}, f32[2,2,96,96]{3,2,1,0:T(8,128)S(1)}, u32[]{:S(2)}, u32[]{:S(2)}) collective-permute-start(f32[2,2,96,96]{3,2,1,0:T(8,128)} %object_ref.1), channel_id=1, source_target_pairs={{0,2},{2,0},{1,3},{3,1},{4,6},{6,4},{5,7},{7,5},{8,10},{10,8},{9,1... | collective-permute-start | bytes 442376 | tf_op jit(solution)/shard_map/ppermute | solution.py:505
  7.9 6.3 %copy-start.6 = (bf16[192,192]{1,0:T(8,128)(2,1)S(1)}, bf16[192,192]{1,0:T(8,128)(2,1)}, u32[]{:S(2)}) copy-start(bf16[192,192]{1,0:T(8,128)(2,1)} %constant.15.clone.rows_ref) | copy-start | bytes 221188
  7.9 6.3 %copy-start.7 = (bf16[192,256]{1,0:T(8,128)(2,1)S(1)}, bf16[192,256]{1,0:T(8,128)(2,1)}, u32[]{:S(2)}) copy-start(bf16[192,256]{1,0:T(8,128)(2,1)} %constant.14.clone.columns_ref) | copy-start | bytes 294916
  8.8 7.5 %collective-permute-start.4 = (f32[2,2,96,96]{3,2,1,0:T(8,128)S(1)}, f32[2,2,96,96]{3,2,1,0:T(8,128)S(1)}, u32[]{:S(2)}, u32[]{:S(2)}) collective-permute-start(f32[2,2,96,96]{3,2,1,0:T(8,128)S(1)} %collective-permute-done.refs_1_), channel_id=1, source_target_pairs={{2,4},{6,8},{10,12},{14,16},{18,20},{22,24},{26,28},{4,2},{8,6},{1... | collective-permute-start | bytes 442376 | tf_op jit(solution)/shard_map/ppermute | solution.py:513
  9.5 6.8 %collective-permute-start.2 = (f32[2,2,96,96]{3,2,1,0:T(8,128)S(1)}, f32[2,2,96,96]{3,2,1,0:T(8,128)S(1)}, u32[]{:S(2)}, u32[]{:S(2)}) collective-permute-start(f32[2,2,96,96]{3,2,1,0:T(8,128)S(1)} %collective-permute-done.refs_1_), channel_id=1, source_target_pairs={{0,2},{2,0},{1,3},{3,1},{4,6},{6,4},{5,7},{7,5},{8,10},{10,8},{9,1... | collective-permute-start | bytes 442376 | tf_op jit(solution)/shard_map/ppermute | solution.py:505
  14.3 1.0 %copy-start.3 = (f32[1,1,2,192,192]{4,3,2,1,0:T(8,128)S(1)}, f32[1,1,2,192,192]{4,3,2,1,0:T(8,128)}, u32[]{:S(2)}) copy-start(f32[1,1,2,192,192]{4,3,2,1,0:T(8,128)} %measured_ref.1) | copy-start | bytes 884740
  15.3 1.1 %copy-start.1 = (f32[2,2,96,96]{3,2,1,0:T(8,128)S(1)}, f32[2,2,96,96]{3,2,1,0:T(8,128)}, u32[]{:S(2)}) copy-start(f32[2,2,96,96]{3,2,1,0:T(8,128)} %object_ref.1) | copy-start | bytes 442372
  15.3 1.1 %copy-start.2 = (bf16[768,256]{1,0:T(8,128)(2,1)S(1)}, bf16[768,256]{1,0:T(8,128)(2,1)}, u32[]{:S(2)}) copy-start(bf16[768,256]{1,0:T(8,128)(2,1)} %constant.16.clone.refs_9_) | copy-start | bytes 1179652
  15.3 1.2 %copy-start.4 = (bf16[192,576]{1,0:T(8,128)(2,1)S(1)}, bf16[192,576]{1,0:T(8,128)(2,1)}, u32[]{:S(2)}) copy-start(bf16[192,576]{1,0:T(8,128)(2,1)} %constant.17.clone.refs_10_) | copy-start | bytes 663556
  15.3 1.2 %copy-start.5 = (f32[2,96,128]{2,1,0:T(8,128)S(1)}, f32[2,96,128]{2,1,0:T(8,128)}, u32[]{:S(2)}) copy-start(f32[2,96,128]{2,1,0:T(8,128)} %constant.19.clone.refs_12_) | copy-start | bytes 294916
  15.3 1.2 %copy-start.8 = (f32[2,8,128]{2,1,0:T(8,128)S(1)}, f32[2,8,128]{2,1,0:T(8,128)}, u32[]{:S(2)}) copy-start(f32[2,8,128]{2,1,0:T(8,128)} %constant.18.clone.refs_11_) | copy-start | bytes 24580
  16.3 0.7 %copy-start.9 = (s32[1,1,2,2]{3,2,1,0:T(2,128)S(1)}, s32[1,1,2,2]{3,2,1,0:T(2,128)}, u32[]{:S(2)}) copy-start(s32[1,1,2,2]{3,2,1,0:T(2,128)} %offsets_ref.1) | copy-start | bytes 52
  23.6 2.0 %collective-permute-start.5 = (f32[3,96,128]{2,1,0:T(8,128)S(1)}, f32[3,96,128]{2,1,0:T(8,128)S(1)}, u32[]{:S(2)}, u32[]{:S(2)}) collective-permute-start(f32[3,96,128]{2,1,0:T(8,128)S(1)} %get-tuple-element.16), channel_id=1, source_target_pairs={{0,2},{2,0},{1,3},{3,1},{4,6},{6,4},{5,7},{7,5},{8,10},{10,8},{9,1... | collective-permute-start | bytes 442376 | tf_op jit(solution)/shard_map/ppermute | solution.py:505
  26.3 15.0 %all-to-all-start = ((f32[16,9,2,128]{3,2,1,0:T(2,128)}), f32[16,9,2,128]{3,2,1,0:T(2,128)S(1)}, u32[]{:S(2)}, u32[]{:S(2)}) async-start(f32[16,9,2,128]{3,2,1,0:T(2,128)} %bitcast), calls=%async_computation | async-start | bytes 294912 | tf_op jit(solution)/shard_map/all_to_all | solution.py:526
  33.4 12.2 %collective-permute-start.7 = (f32[96,768]{1,0:T(8,128)S(1)}, f32[96,768]{1,0:T(8,128)S(1)}, u32[]{:S(2)}, u32[]{:S(2)}) collective-permute-start(f32[96,768]{1,0:T(8,128)S(1)} %get-tuple-element.18), channel_id=1, source_target_pairs={{0,2},{2,0},{1,3},{3,1},{4,6},{6,4},{5,7},{7,5},{8,10},{10,8},{9,1... | collective-permute-start | bytes 884744 | tf_op jit(solution)/shard_map/ppermute | solution.py:505
  33.5 12.2 %collective-permute-start.8 = (f32[96,768]{1,0:T(8,128)S(1)}, f32[96,768]{1,0:T(8,128)S(1)}, u32[]{:S(2)}, u32[]{:S(2)}) collective-permute-start(f32[96,768]{1,0:T(8,128)S(1)} %get-tuple-element.19), channel_id=1, source_target_pairs={{2,4},{6,8},{10,12},{14,16},{18,20},{22,24},{26,28},{4,2},{8,6},{1... | collective-permute-start | bytes 884744 | tf_op jit(solution)/shard_map/ppermute | solution.py:513
  42.1 11.4 %all-to-all-start.1 = ((f32[16,9,2,128]{3,2,1,0:T(2,128)}), f32[16,9,2,128]{3,2,1,0:T(2,128)S(1)}, u32[]{:S(2)}, u32[]{:S(2)}) async-start(f32[16,9,2,128]{3,2,1,0:T(2,128)} %broadcast_in_dim.2), calls=%async_computation.1 | async-start | bytes 294912 | tf_op jit(solution)/shard_map/all_to_all | solution.py:528
  45.7 7.8 %collective-permute-start.9 = (f32[96,384]{1,0:T(8,128)S(1)}, f32[96,384]{1,0:T(8,128)S(1)}, u32[]{:S(2)}, u32[]{:S(2)}) collective-permute-start(f32[96,384]{1,0:T(8,128)S(1)} %get-tuple-element.21), channel_id=1, source_target_pairs={{0,1},{1,0},{2,3},{3,2},{4,5},{5,4},{6,7},{7,6},{8,9},{9,8},{10,11... | collective-permute-start | bytes 442376 | tf_op jit(solution)/shard_map/ppermute | solution.py:619
  53.5 1.4 %collective-permute-start.6 = (f32[3,96,128]{2,1,0:T(8,128)S(1)}, f32[3,96,128]{2,1,0:T(8,128)S(1)}, u32[]{:S(2)}, u32[]{:S(2)}) collective-permute-start(f32[3,96,128]{2,1,0:T(8,128)S(1)} %bitcast.2), channel_id=1, source_target_pairs={{0,2},{2,0},{1,3},{3,1},{4,6},{6,4},{5,7},{7,5},{8,10},{10,8},{9,1... | collective-permute-start | bytes 442376 | tf_op jit(solution)/shard_map/ppermute | solution.py:505

commit v5 on v4

--- a/solution.py
+++ b/solution.py
@@ -18,6 +18,7 @@
 bf16 = jnp.bfloat16
 VMEM = pl.BlockSpec(memory_space=pltpu.VMEM)
 SMEM = pl.BlockSpec(memory_space=pltpu.SMEM)
+ANY = pl.BlockSpec(memory_space=pl.ANY)
 ROWS = ("pair", "core")
 
 
@@ -57,13 +58,17 @@
 
 def sorters(width):
     half = width // 2
-    columns = np.zeros((width, 2 * LANES), np.float32)
-    rows = np.zeros((width, width), np.float32)
-    for i in range(half):
-        for j in range(2):
-            columns[2 * i + j, j * LANES + i] = 1
-            rows[j * half + i, 2 * i + j] = 1
-    return columns.astype(bf16), rows.astype(bf16)
+
+    def ids(shape, axis):
+        return lax.broadcasted_iota(jnp.int32, shape, axis)
+
+    shape = (width, 2 * LANES)
+    source = ids(shape, 0)
+    columns = ids(shape, 1) == (source & 1) * LANES + (source >> 1)
+    shape = (width, width)
+    target = ids(shape, 0)
+    rows = ids(shape, 1) == jnp.where(target < half, 2 * target, 2 * (target - half) + 1)
+    return [jnp.where(x, 1.0, 0.0).astype(bf16) for x in (columns, rows)]
 
 
 def times(a_real, a_imag, b_real, b_imag):
@@ -101,17 +106,50 @@
     return out
 
 
+def cosine_and_sine(x):
+    turns = jnp.floor(x * (2.0 / math.pi) + 0.5)
+    rest = ((x - turns * 1.5703125) - turns * 4.837512969970703125e-4) - turns * 7.54978995489188e-8
+    square = rest * rest
+    sine = ((-1.9515295891e-4 * square + 8.3321608736e-3) * square - 1.6666654611e-1) * square
+    sine = sine * rest + rest
+    cosine = (2.443315711809948e-5 * square - 1.388731625493765e-3) * square + 4.166664568298827e-2
+    cosine = cosine * square * square - 0.5 * square + 1.0
+    quarter = turns.astype(jnp.int32) & 3
+    odd = (quarter & 1) == 1
+    return (
+        jnp.where(odd, sine, cosine) * jnp.where((quarter == 1) | (quarter == 2), -1.0, 1.0),
+        jnp.where(odd, cosine, sine) * jnp.where(quarter >= 2, -1.0, 1.0),
+    )
+
+
+def pack_kernel(object_ref, out_ref):
+    tile = object_ref.shape[2]
+    pad = jnp.zeros((tile, LANES - tile), f32)
+    planes = [
+        jnp.concatenate([object_ref[plane // 2, plane % 2], pad], 1) for plane in range(4)
+    ]
+    for j, block in enumerate(packed(planes, tile)):
+        out_ref[:, j * LANES : (j + 1) * LANES] = block
+
+
 def prepare_kernel(
+    offsets_ref,
+    counts_ref,
     probe_ref,
-    cosine_ref,
-    sine_ref,
+    phase_ref,
     measured_ref,
-    columns_ref,
-    rows_ref,
     wave_out,
     trans_out,
     measured_out,
+    places_out,
 ):
+    lanes = lax.broadcasted_iota(jnp.int32, places_out.shape, 1)
+    slots = measured_out.shape[0]
+    places = jnp.where(lanes == 2 * slots, counts_ref[0, 0], 0)
+    for slot in range(slots):
+        for axis in range(2):
+            places = jnp.where(lanes == 2 * slot + axis, offsets_ref[0, 0, slot, axis], places)
+    places_out[...] = places
     width = probe_ref.shape[1]
     half = width // 2
     lane = lane_ids(width)
@@ -125,17 +163,21 @@
         wave_out[j, :, LANES:] = jnp.where(
             lane < rest, pltpu.roll(head, rest, 1), pltpu.roll(tail, rest, 1)
         )
-    planes = [(cosine_ref[...], trans_out, 0), (sine_ref[...], trans_out, 1)]
-    for slot in range(measured_out.shape[0]):
-        planes.append((measured_ref[0, 0, slot], measured_out, slot))
-    for left, target, j in planes:
+    columns, rows = sorters(width)
+    planes = [phase_ref[...]] + [measured_ref[0, 0, j] for j in range(measured_out.shape[0])]
+    for j, left in enumerate(planes):
         total = jnp.zeros((width, 2 * LANES), f32)
         for part in range(3):
             piece = left.astype(bf16)
             left = left - piece.astype(f32)
-            moved = jnp.dot(piece, columns_ref[...], preferred_element_type=f32)
-            total = total + jnp.dot(rows_ref[...], moved.astype(bf16), preferred_element_type=f32)
-        target[j] = total
+            moved = jnp.dot(piece, columns, preferred_element_type=f32)
+            total = total + jnp.dot(rows, moved.astype(bf16), preferred_element_type=f32)
+        if j > 0:
+            measured_out[j - 1] = total
+            continue
+        used = lax.rem(lax.broadcasted_iota(jnp.int32, total.shape, 1), LANES) < half
+        for side, value in enumerate(cosine_and_sine(total)):
+            trans_out[side] = jnp.where(used, value, 0.0)
 
 
 def row_places(cores):
@@ -146,8 +188,7 @@
 def position_kernel(
     paired,
     cores,
-    offsets_ref,
-    counts_ref,
+    places_ref,
     *refs,
 ):
     sides = 2 if paired else 3
@@ -171,9 +212,13 @@
         window,
         carried,
         terms,
-    ) = refs[3 * sides + 10 + cores : 3 * sides + 15 + cores]
+        places,
+        arrived,
+    ) = refs[3 * sides + 10 + cores : 3 * sides + 17 + cores]
+    copy = pltpu.make_async_copy(places_ref, places, arrived)
+    copy.start()
     slots = measured_ref.shape[0]
-    work = refs[3 * sides + 15 + cores :]
+    work = refs[3 * sides + 17 + cores :]
     data, out_right, mid, out_left = (work[k * slots : (k + 1) * slots] for k in range(4))
     width = wave_ref.shape[1]
     half = width // 2
@@ -185,7 +230,6 @@
     column_of = lax.axis_index("col")
     row_starts = [pl.multiple_of(place * tile, 8) for place in row_places(cores)]
 
-    pad = jnp.zeros((tile, LANES - tile), f32)
     for row in range(3):
         rows = pl.ds(row_starts[row], tile)
         for side in range(sides):
@@ -193,16 +237,19 @@
                 place = 1 if side == 0 else 2 - 2 * column_of
             else:
                 place = (1, 0, 2)[side]
+            ref = tiles[row * sides + side]
+            parts = [ref[:, j * LANES : (j + 1) * LANES] for j in range(3)]
+            parts.append(last_of(parts, tile))
             for plane in range(4):
-                value = tiles[row * sides + side][plane // 2, plane % 2]
-                obj[plane, place, rows, :] = jnp.concatenate([value, pad], 1)
+                obj[plane, place, rows, :] = parts[plane]
         if paired:
             for plane in range(4):
                 obj[plane, 2 * column_of, rows, :] = jnp.zeros((tile, LANES), f32)
 
+    copy.wait()
     shift = tile - half
     corners = [
-        (offsets_ref[0, 0, slot, 0] + shift, offsets_ref[0, 0, slot, 1] + shift)
+        (places[0, 2 * slot] + shift, places[0, 2 * slot + 1] + shift)
         for slot in range(slots)
     ]
     chunk = half
@@ -397,7 +444,7 @@
                     running[slot] = None
         turn += 1
 
-    live = [(slot < counts_ref[0, 0]).astype(f32) for slot in range(slots)]
+    live = [(slot < places[0, 2 * slots]).astype(f32) for slot in range(slots)]
     core = lax.axis_index("core")
     share = width // cores
     for row in range(0, half, step):
@@ -514,6 +561,15 @@
     return passed_along(x, ROWS, -1)
 
 
+def from_far_beside(x):
+    ends = range(1, lax.axis_size(ROWS) - 1, 2)
+    pairs = []
+    for i in ends:
+        for j in range(2):
+            pairs += [(2 * i + j, 2 * i + 3 - j), (2 * i + 2 + j, 2 * i + 1 - j)]
+    return lax.ppermute(x, ROWS + ("col",), pairs)
+
+
 def all_sum(x, group):
     count = math.prod(lax.axis_size(axis) for axis in group)
     shape = x.shape
@@ -543,34 +599,38 @@
     def shape(*dims, kind=f32):
         return jax.ShapeDtypeStruct(dims, kind)
 
-    cells = object_slices
+    cells = pl.pallas_call(
+        pack_kernel,
+        out_shape=shape(tile, 3 * LANES),
+        in_specs=[VMEM],
+        out_specs=VMEM,
+        cost_estimate=pl.CostEstimate(flops=10**10, bytes_accessed=10**7, transcendentals=0),
+        compiler_params=small,
+    )(object_slices)
     if paired:
         beside = [lax.ppermute(cells, "col", [(0, 1), (1, 0)])]
     else:
         beside = [passed_along(cells, "col", 1), passed_along(cells, "col", -1)]
     own = [cells] + beside
     near = [from_near(x, cores) for x in own]
-    far = [from_far(x, cores) for x in own]
-
-    columns, rows = sorters(width)
-    wave, trans, intensities = pl.pallas_call(
+    if paired and cores == 2:
+        far = [from_far(cells, cores), from_far_beside(cells)]
+    else:
+        far = [from_far(x, cores) for x in own]
+
+    wave, trans, intensities, places = pl.pallas_call(
         prepare_kernel,
         out_shape=[
             shape(2, width, 2 * LANES),
             shape(2, width, 2 * LANES),
             shape(slots, width, 2 * LANES),
+            shape(8, LANES, kind=jnp.int32),
         ],
-        in_specs=[VMEM] * 6,
-        out_specs=[VMEM] * 3,
+        in_specs=[SMEM] * 2 + [VMEM] * 3,
+        out_specs=[VMEM] * 4,
+        cost_estimate=pl.CostEstimate(flops=10**10, bytes_accessed=10**7, transcendentals=0),
         compiler_params=small,
-    )(
-        probe,
-        jnp.cos(propagator_phase),
-        jnp.sin(propagator_phase),
-        measured,
-        columns,
-        rows,
-    )
+    )(offsets, counts, probe, propagator_phase, measured)
 
     total = slots * width
     sides = len(own)
@@ -581,6 +641,8 @@
         pltpu.VMEM((4, 2, total, LANES), f32),
         pltpu.VMEM((2, 2, total, LANES), f32),
         pltpu.VMEM((cores, 3, width // cores, LANES), f32),
+        pltpu.SMEM((8, LANES), jnp.int32),
+        pltpu.SemaphoreType.DMA,
     ]
     scratch += [pltpu.VMEM((2 * width, 4 * LANES), bf16)] * slots
     scratch += [pltpu.VMEM((2 * width, 2 * LANES), f32)] * slots
@@ -590,11 +652,11 @@
     strips = pl.pallas_call(
         functools.partial(position_kernel, paired, cores),
         out_shape=[strip] * 3 + [term] * cores,
-        in_specs=[SMEM, SMEM] + [VMEM] * (3 * sides + 7),
+        in_specs=[ANY] + [VMEM] * (3 * sides + 7),
         out_specs=[VMEM] * (3 + cores),
         scratch_shapes=scratch,
         compiler_params=large,
-    )(offsets, counts, *own, *near, *far, wave, trans, intensities, *matrices(width))
+    )(places, *own, *near, *far, wave, trans, intensities, *matrices(width))
     own_strip, near_strip, far_strip = strips[:3]
     terms = strips[3:]
 

time: 56.3 us -> 53.5 us (0.950)
  local copies, waits for them, and re-layouts: 4.03 us -> 1.72 us
  Pallas kernels: 8.7 us -> 9.53 us
  waiting for transfers between devices: 16.3 us -> 15.6 us
  starting transfers between devices: 24.6 us -> 24 us
    sin x1 -> x0, local copies, waits for them, and re-layouts: 1.61 us -> none  [shards(): jnp.sin(propagator_phase)]
    ppermute x1, waiting for transfers between devices: 0.86 us -> 0.01 us  [shards(): beside = [lax.ppermute(cells, 'col', [(0, 1), (1, 0)])]]
    ppermute x5, starting transfers between devices: 7.08 us -> 6.36 us  [from_near(): return lax.ppermute(x, 'core', [(0, 1), (1, 0)])]
    unnamed x20, local copies, waits for them, and re-layouts: 1.72 us -> 1.02 us
    ppermute x3 -> x2, starting transfers between devices: 2 us -> 1.34 us  [from_far(): return lax.ppermute(x, ROWS, pairs)]
    ppermute x0 -> x1, starting transfers between devices: none -> 0.66 us  [from_far_beside(): return lax.ppermute(x, ROWS + ('col',), pairs)]
    pallas_call x1, Pallas kernels: 0.98 us -> 1.64 us  [shards(): pl.pallas_call(prepare_kernel, out_shape=[shape(2, width, 2 * LANES), sha...]
  transfers between devices with their start and end apart: 12 -> 12, of which waited for: 5 -> 4; matrix products, arithmetic and copies ran while one was open for 4% -> 1% of each run, Pallas kernels for 2% -> 3%
where the time goes in v5:
time: 53.5 us; the launch traced here: 53.1 us
  starting transfers between devices  24 us (45%)
  waiting for transfers between devices  15.6 us (29%)
  Pallas kernels  9.53 us (18%)
  local copies, waits for them, and re-layouts  1.72 us (3%)
  between operations  1.54 us (3%)
  other arithmetic  0.74 us (1%)
    all_to_all x2, waiting for transfers between devices, all_sum(): x = lax.all_to_all(x, group, 0, 0, tiled=True)  13.2 us
    all_to_all x2, starting transfers between devices, all_sum(): x = lax.all_to_all(x, group, 0, 0, tiled=True)  10.7 us
    pallas_call x1, Pallas kernels, shards(): pl.pallas_call(functools.partial(position_kernel, paired, cores), out_sha...  6.69 us
    ppermute x5, starting transfers between devices, from_near(): return lax.ppermute(x, 'core', [(0, 1), (1, 0)])  6.36 us
    ppermute x1, starting transfers between devices, shards(): beside = [lax.ppermute(cells, 'col', [(0, 1), (1, 0)])]  3.06 us
    ppermute x5, waiting for transfers between devices, from_near(): return lax.ppermute(x, 'core', [(0, 1), (1, 0)])  2.38 us
    ppermute x1, starting transfers between devices, shards(): received = [lax.ppermute(parts[1], 'col', [(0, 1), (1, 0)])]  1.87 us
    pallas_call x1, Pallas kernels, shards(): pl.pallas_call(prepare_kernel, out_shape=[shape(2, width, 2 * LANES), sha...  1.64 us
  transfers between devices with their start and end apart: 12, of which 4 were waited for; matrix products, arithmetic and copies ran while one was open for 1% of the time, Pallas kernels for 3%

profile of v5, /device:TPU:0, one launch (start us, length us, event | category | flops | bytes accessed | tf_op | source)
XLA Modules:
  0.0 53.1 jit_solution(4843181501885133447)
XLA Ops:
  0.6 0.0 copy-start
  0.6 0.0 copy-start.3
  0.7 1.0 %copy-done.3 = f32[2,2,96,96]{3,2,1,0:T(8,128)S(1)} copy-done((f32[2,2,96,96]{3,2,1,0:T(8,128)S(1)}, f32[2,2,96,96]{3,2,1,0:T(8,128)}, u32[]{:S(2)}) %copy-start.3) | copy-done | bytes 147480
  1.6 0.1 shard_map.114.refs_0_
  1.7 0.0 copy-start.9
  1.7 3.1 %collective-permute-start = (f32[96,384]{1,0:T(8,128)S(1)}, f32[96,384]{1,0:T(8,128)S(1)}, u32[]{:S(2)}, u32[]{:S(2)}) collective-permute-start(f32[96,384]{1,0:T(8,128)S(1)} %shard_map.114.refs_0_), channel_id=1, source_target_pairs={{0,1},{1,0},{2,3},{3,2},{4,5},{5,4},{6,7},{7,6},{8,9},{9,8},{10,11... | collective-permute-start | bytes 442376 | tf_op jit(solution)/shard_map/ppermute | solution.py:611
  4.8 0.7 %collective-permute-start.4 = (f32[96,384]{1,0:T(8,128)S(1)}, f32[96,384]{1,0:T(8,128)S(1)}, u32[]{:S(2)}, u32[]{:S(2)}) collective-permute-start(f32[96,384]{1,0:T(8,128)S(1)} %shard_map.114.refs_0_), channel_id=1, source_target_pairs={{2,5},{4,3},{3,4},{5,2},{6,9},{8,7},{7,8},{9,6},{10,13},{12,11},{1... | collective-permute-start | bytes 442376 | tf_op jit(solution)/shard_map/ppermute | solution.py:570
  5.5 0.7 %collective-permute-start.3 = (f32[96,384]{1,0:T(8,128)S(1)}, f32[96,384]{1,0:T(8,128)S(1)}, u32[]{:S(2)}, u32[]{:S(2)}) collective-permute-start(f32[96,384]{1,0:T(8,128)S(1)} %shard_map.114.refs_0_), channel_id=1, source_target_pairs={{2,4},{6,8},{10,12},{14,16},{18,20},{22,24},{26,28},{4,2},{8,6},{1... | collective-permute-start | bytes 442376 | tf_op jit(solution)/shard_map/ppermute | solution.py:560
  6.1 4.2 %collective-permute-start.1 = (f32[96,384]{1,0:T(8,128)S(1)}, f32[96,384]{1,0:T(8,128)S(1)}, u32[]{:S(2)}, u32[]{:S(2)}) collective-permute-start(f32[96,384]{1,0:T(8,128)S(1)} %shard_map.114.refs_0_), channel_id=1, source_target_pairs={{0,2},{2,0},{1,3},{3,1},{4,6},{6,4},{5,7},{7,5},{8,10},{10,8},{9,1... | collective-permute-start | bytes 442376 | tf_op jit(solution)/shard_map/ppermute | solution.py:552
  11.0 0.0 copy-start.1
  11.0 0.0 copy-start.2
  11.0 0.0 copy-start.5
  11.0 0.0 collective-permute-done.refs_1_
  11.0 0.1 collective-permute-start.2
  11.1 0.0 copy-done
  11.1 0.0 copy-done.7
  11.1 0.0 copy-done.8
  11.1 0.0 copy-done.9
  11.1 0.0 copy-start.6
  11.1 1.6 %shard_map.113 = (f32[2,192,256]{2,1,0:T(8,128)S(1)}, f32[2,192,256]{2,1,0:T(8,128)S(1)}, f32[2,192,256]{2,1,0:T(8,128)S(1)}, s32[8,128]{1,0:T(8,128)S(1)}) custom-call(s32[1,1,2,2]{3,2,1,0:T(2,128)S(1)} %copy-done.9, s32[1,1]{1,0:T(1,128)S(6)} %copy.12.counts_ref, f32[2,192,192]{2,1,0:T(8,128)S(1)} %copy-done, f32[192,192]{1,0:T(8,128)S(1)} %copy-done.8, ...), custom_call_target="tpu_custom_call" | custom-call | flops 10000000000 | bytes 10000000 | tf_op jit(solution)/shard_map/pallas_call | solution.py:621
  12.8 0.0 collective-permute-done.4.refs_5_
  12.8 0.0 collective-permute-done.3.refs_4_
  12.8 0.0 collective-permute-done.1.refs_2_
  12.8 0.0 collective-permute-done.2.refs_3_
  12.8 0.0 copy-done.1
  12.8 0.0 copy-done.2
  12.8 0.0 copy-done.5
  12.8 0.0 copy-done.6
  12.9 6.7 %shard_map.115 = (f32[96,768]{1,0:T(8,128)S(1)}, f32[96,768]{1,0:T(8,128)S(1)}, f32[96,768]{1,0:T(8,128)S(1)}, f32[3,96,128]{2,1,0:T(8,128)S(1)}, f32[3,96,128]{2,1,0:T(8,128)S(1)}) custom-call(s32[8,128]{1,0:T(8,128)S(1)} %get-tuple-element.13.places_ref, f32[96,384]{1,0:T(8,128)S(1)} %shard_map.114.refs_0_, f32[96,384]{1,0:T(8,128)S(1)} %collective-permute-done.refs_1_, ...), custom_call_target="tpu_custom_call" | custom-call | tf_op jit(solution)/shard_map/pallas_call | solution.py:652
  19.6 2.0 %collective-permute-start.5 = (f32[3,96,128]{2,1,0:T(8,128)S(1)}, f32[3,96,128]{2,1,0:T(8,128)S(1)}, u32[]{:S(2)}, u32[]{:S(2)}) collective-permute-start(f32[3,96,128]{2,1,0:T(8,128)S(1)} %get-tuple-element.18), channel_id=1, source_target_pairs={{0,2},{2,0},{1,3},{3,1},{4,6},{6,4},{5,7},{7,5},{8,10},{10,8},{9,1... | collective-permute-start | bytes 442376 | tf_op jit(solution)/shard_map/ppermute | solution.py:552
  21.5 1.0 %collective-permute-done.5 = f32[3,96,128]{2,1,0:T(8,128)S(1)} collective-permute-done((f32[3,96,128]{2,1,0:T(8,128)S(1)}, f32[3,96,128]{2,1,0:T(8,128)S(1)}, u32[]{:S(2)}, u32[]{:S(2)}) %collective-permute-start.5) | collective-permute-done | bytes 147488 | tf_op jit(solution)/shard_map/ppermute | solution.py:552
  22.5 0.7 %add.3 = f32[3,96,128]{2,1,0:T(8,128)} add(f32[3,96,128]{2,1,0:T(8,128)S(1)} %get-tuple-element.17, f32[3,96,128]{2,1,0:T(8,128)S(1)} %collective-permute-done.5) | non-fusion elementwise | flops 36864 | bytes 442368 | tf_op jit(solution)/shard_map/add | solution.py:664
  23.2 7.2 %all-to-all-start = ((f32[16,9,2,128]{3,2,1,0:T(2,128)}), f32[16,9,2,128]{3,2,1,0:T(2,128)S(1)}, u32[]{:S(2)}, u32[]{:S(2)}) async-start(f32[16,9,2,128]{3,2,1,0:T(2,128)} %bitcast), calls=%async_computation | async-start | bytes 294912 | tf_op jit(solution)/shard_map/all_to_all | solution.py:582
  30.4 0.1 collective-permute-start.7
  30.5 0.7 %collective-permute-start.8 = (f32[96,768]{1,0:T(8,128)S(1)}, f32[96,768]{1,0:T(8,128)S(1)}, u32[]{:S(2)}, u32[]{:S(2)}) collective-permute-start(f32[96,768]{1,0:T(8,128)S(1)} %get-tuple-element.21), channel_id=1, source_target_pairs={{2,4},{6,8},{10,12},{14,16},{18,20},{22,24},{26,28},{4,2},{8,6},{1... | collective-permute-start | bytes 884744 | tf_op jit(solution)/shard_map/ppermute | solution.py:560
  31.2 7.3 %all-to-all-done = f32[16,9,2,128]{3,2,1,0:T(2,128)S(1)} async-done(((f32[16,9,2,128]{3,2,1,0:T(2,128)}), f32[16,9,2,128]{3,2,1,0:T(2,128)S(1)}, u32[]{:S(2)}, u32[]{:S(2)}) %all-to-all-start) | async-done | bytes 147488 | tf_op jit(solution)/shard_map/all_to_all | solution.py:582
  38.5 0.1 reduce_sum.9
  38.6 0.7 %broadcast_in_dim.2 = f32[16,9,2,128]{3,2,1,0:T(2,128)} broadcast(f32[9,2,128]{2,1,0:T(2,128)S(1)} %reduce_sum.9), dimensions={1,2,3} | broadcast | bytes 156672 | tf_op jit(solution)/shard_map/broadcast_in_dim | solution.py:583
  39.3 3.5 %all-to-all-start.1 = ((f32[16,9,2,128]{3,2,1,0:T(2,128)}), f32[16,9,2,128]{3,2,1,0:T(2,128)S(1)}, u32[]{:S(2)}, u32[]{:S(2)}) async-start(f32[16,9,2,128]{3,2,1,0:T(2,128)} %broadcast_in_dim.2), calls=%async_computation.1 | async-start | bytes 294912 | tf_op jit(solution)/shard_map/all_to_all | solution.py:584
  42.8 0.0 collective-permute-done.7.near_ref
  42.8 0.0 collective-permute-done.8.far_ref
  42.9 0.0 copy-start.4
  42.9 1.9 %collective-permute-start.9 = (f32[96,384]{1,0:T(8,128)S(1)}, f32[96,384]{1,0:T(8,128)S(1)}, u32[]{:S(2)}, u32[]{:S(2)}) collective-permute-start(f32[96,384]{1,0:T(8,128)S(1)} %get-tuple-element.23), channel_id=1, source_target_pairs={{0,1},{1,0},{2,3},{3,2},{4,5},{5,4},{6,7},{7,6},{8,9},{9,8},{10,11... | collective-permute-start | bytes 442376 | tf_op jit(solution)/shard_map/ppermute | solution.py:681
  44.8 5.9 %all-to-all-done.1 = f32[16,9,2,128]{3,2,1,0:T(2,128)S(1)} async-done(((f32[16,9,2,128]{3,2,1,0:T(2,128)}), f32[16,9,2,128]{3,2,1,0:T(2,128)S(1)}, u32[]{:S(2)}, u32[]{:S(2)}) %all-to-all-start.1) | async-done | bytes 147488 | tf_op jit(solution)/shard_map/all_to_all | solution.py:584
  50.7 0.0 collective-permute-start.6
  50.7 0.0 collective-permute-done.9.refs_3_
  50.7 1.4 %collective-permute-done.6.refs_1_ = f32[3,96,128]{2,1,0:T(8,128)S(1)} collective-permute-done((f32[3,96,128]{2,1,0:T(8,128)S(1)}, f32[3,96,128]{2,1,0:T(8,128)S(1)}, u32[]{:S(2)}, u32[]{:S(2)}) %collective-permute-start.6) | collective-permute-done | bytes 147488 | tf_op jit(solution)/shard_map/ppermute | solution.py:552
  52.0 1.1 %shard_map.117 = (f32[2,2,96,96]{3,2,1,0:T(8,128)}, f32[2,192,192]{2,1,0:T(8,128)}) custom-call(f32[2,2,96,96]{3,2,1,0:T(8,128)S(1)} %copy-done.4, f32[2,192,192]{2,1,0:T(8,128)S(1)} %copy-done, f32[3,96,128]{2,1,0:T(8,128)S(1)} %bitcast.3, f32[3,96,128]{2,1,0:T(8,128)S(1)} %collective-permute-done.6.refs_1_, f32[96,384]{1,0:T(8,128)S(1)} %get-tuple-element.22.refs_2_, ...), custom_call_target="tpu_custom_call" | custom-call | tf_op jit(solution)/shard_map/pallas_call | solution.py:684
  (4 shorter events, 0.1 us)
Async XLA Ops:
  0.6 10.5 %copy-start = (f32[2,192,192]{2,1,0:T(8,128)S(1)}, f32[2,192,192]{2,1,0:T(8,128)}, u32[]{:S(2)}) copy-start(f32[2,192,192]{2,1,0:T(8,128)} %probe_ref.3) | copy-start | bytes 884740
  0.6 1.0 %copy-start.3 = (f32[2,2,96,96]{3,2,1,0:T(8,128)S(1)}, f32[2,2,96,96]{3,2,1,0:T(8,128)}, u32[]{:S(2)}) copy-start(f32[2,2,96,96]{3,2,1,0:T(8,128)} %object_ref.3) | copy-start | bytes 442372
  1.6 9.5 %copy-start.7 = (f32[1,1,2,192,192]{4,3,2,1,0:T(8,128)S(1)}, f32[1,1,2,192,192]{4,3,2,1,0:T(8,128)}, u32[]{:S(2)}) copy-start(f32[1,1,2,192,192]{4,3,2,1,0:T(8,128)} %measured_ref.1) | copy-start | bytes 884740
  1.6 9.5 %copy-start.8 = (f32[192,192]{1,0:T(8,128)S(1)}, f32[192,192]{1,0:T(8,128)}, u32[]{:S(2)}) copy-start(f32[192,192]{1,0:T(8,128)} %phase_ref.1) | copy-start | bytes 442372
  1.7 9.4 %copy-start.9 = (s32[1,1,2,2]{3,2,1,0:T(2,128)S(1)}, s32[1,1,2,2]{3,2,1,0:T(2,128)}, u32[]{:S(2)}) copy-start(s32[1,1,2,2]{3,2,1,0:T(2,128)} %offsets_ref.1) | copy-start | bytes 52
  1.7 9.3 %collective-permute-start = (f32[96,384]{1,0:T(8,128)S(1)}, f32[96,384]{1,0:T(8,128)S(1)}, u32[]{:S(2)}, u32[]{:S(2)}) collective-permute-start(f32[96,384]{1,0:T(8,128)S(1)} %shard_map.114.refs_0_), channel_id=1, source_target_pairs={{0,1},{1,0},{2,3},{3,2},{4,5},{5,4},{6,7},{7,6},{8,9},{9,8},{10,11... | collective-permute-start | bytes 442376 | tf_op jit(solution)/shard_map/ppermute | solution.py:611
  4.8 8.0 %collective-permute-start.4 = (f32[96,384]{1,0:T(8,128)S(1)}, f32[96,384]{1,0:T(8,128)S(1)}, u32[]{:S(2)}, u32[]{:S(2)}) collective-permute-start(f32[96,384]{1,0:T(8,128)S(1)} %shard_map.114.refs_0_), channel_id=1, source_target_pairs={{2,5},{4,3},{3,4},{5,2},{6,9},{8,7},{7,8},{9,6},{10,13},{12,11},{1... | collective-permute-start | bytes 442376 | tf_op jit(solution)/shard_map/ppermute | solution.py:570
  5.5 7.3 %collective-permute-start.3 = (f32[96,384]{1,0:T(8,128)S(1)}, f32[96,384]{1,0:T(8,128)S(1)}, u32[]{:S(2)}, u32[]{:S(2)}) collective-permute-start(f32[96,384]{1,0:T(8,128)S(1)} %shard_map.114.refs_0_), channel_id=1, source_target_pairs={{2,4},{6,8},{10,12},{14,16},{18,20},{22,24},{26,28},{4,2},{8,6},{1... | collective-permute-start | bytes 442376 | tf_op jit(solution)/shard_map/ppermute | solution.py:560
  6.1 6.7 %collective-permute-start.1 = (f32[96,384]{1,0:T(8,128)S(1)}, f32[96,384]{1,0:T(8,128)S(1)}, u32[]{:S(2)}, u32[]{:S(2)}) collective-permute-start(f32[96,384]{1,0:T(8,128)S(1)} %shard_map.114.refs_0_), channel_id=1, source_target_pairs={{0,2},{2,0},{1,3},{3,1},{4,6},{6,4},{5,7},{7,5},{8,10},{10,8},{9,1... | collective-permute-start | bytes 442376 | tf_op jit(solution)/shard_map/ppermute | solution.py:552
  11.0 1.9 %copy-start.1 = (bf16[768,256]{1,0:T(8,128)(2,1)S(1)}, bf16[768,256]{1,0:T(8,128)(2,1)}, u32[]{:S(2)}) copy-start(bf16[768,256]{1,0:T(8,128)(2,1)} %constant.10.clone.refs_9_) | copy-start | bytes 1179652
  11.0 1.9 %copy-start.2 = (bf16[192,576]{1,0:T(8,128)(2,1)S(1)}, bf16[192,576]{1,0:T(8,128)(2,1)}, u32[]{:S(2)}) copy-start(bf16[192,576]{1,0:T(8,128)(2,1)} %constant.11.clone.refs_10_) | copy-start | bytes 663556
  11.0 1.9 %copy-start.5 = (f32[2,96,128]{2,1,0:T(8,128)S(1)}, f32[2,96,128]{2,1,0:T(8,128)}, u32[]{:S(2)}) copy-start(f32[2,96,128]{2,1,0:T(8,128)} %constant.13.clone.refs_12_) | copy-start | bytes 294916
  11.0 1.8 %collective-permute-start.2 = (f32[96,384]{1,0:T(8,128)S(1)}, f32[96,384]{1,0:T(8,128)S(1)}, u32[]{:S(2)}, u32[]{:S(2)}) collective-permute-start(f32[96,384]{1,0:T(8,128)S(1)} %collective-permute-done.refs_1_), channel_id=1, source_target_pairs={{0,2},{2,0},{1,3},{3,1},{4,6},{6,4},{5,7},{7,5},{8,10},{10,8},{9,1... | collective-permute-start | bytes 442376 | tf_op jit(solution)/shard_map/ppermute | solution.py:552
  11.1 1.7 %copy-start.6 = (f32[2,8,128]{2,1,0:T(8,128)S(1)}, f32[2,8,128]{2,1,0:T(8,128)}, u32[]{:S(2)}) copy-start(f32[2,8,128]{2,1,0:T(8,128)} %constant.12.clone.refs_11_) | copy-start | bytes 24580
  19.6 3.0 %collective-permute-start.5 = (f32[3,96,128]{2,1,0:T(8,128)S(1)}, f32[3,96,128]{2,1,0:T(8,128)S(1)}, u32[]{:S(2)}, u32[]{:S(2)}) collective-permute-start(f32[3,96,128]{2,1,0:T(8,128)S(1)} %get-tuple-element.18), channel_id=1, source_target_pairs={{0,2},{2,0},{1,3},{3,1},{4,6},{6,4},{5,7},{7,5},{8,10},{10,8},{9,1... | collective-permute-start | bytes 442376 | tf_op jit(solution)/shard_map/ppermute | solution.py:552
  23.2 15.3 %all-to-all-start = ((f32[16,9,2,128]{3,2,1,0:T(2,128)}), f32[16,9,2,128]{3,2,1,0:T(2,128)S(1)}, u32[]{:S(2)}, u32[]{:S(2)}) async-start(f32[16,9,2,128]{3,2,1,0:T(2,128)} %bitcast), calls=%async_computation | async-start | bytes 294912 | tf_op jit(solution)/shard_map/all_to_all | solution.py:582
  30.4 12.5 %collective-permute-start.7 = (f32[96,768]{1,0:T(8,128)S(1)}, f32[96,768]{1,0:T(8,128)S(1)}, u32[]{:S(2)}, u32[]{:S(2)}) collective-permute-start(f32[96,768]{1,0:T(8,128)S(1)} %get-tuple-element.20), channel_id=1, source_target_pairs={{0,2},{2,0},{1,3},{3,1},{4,6},{6,4},{5,7},{7,5},{8,10},{10,8},{9,1... | collective-permute-start | bytes 884744 | tf_op jit(solution)/shard_map/ppermute | solution.py:552
  30.5 12.3 %collective-permute-start.8 = (f32[96,768]{1,0:T(8,128)S(1)}, f32[96,768]{1,0:T(8,128)S(1)}, u32[]{:S(2)}, u32[]{:S(2)}) collective-permute-start(f32[96,768]{1,0:T(8,128)S(1)} %get-tuple-element.21), channel_id=1, source_target_pairs={{2,4},{6,8},{10,12},{14,16},{18,20},{22,24},{26,28},{4,2},{8,6},{1... | collective-permute-start | bytes 884744 | tf_op jit(solution)/shard_map/ppermute | solution.py:560
  39.3 11.4 %all-to-all-start.1 = ((f32[16,9,2,128]{3,2,1,0:T(2,128)}), f32[16,9,2,128]{3,2,1,0:T(2,128)S(1)}, u32[]{:S(2)}, u32[]{:S(2)}) async-start(f32[16,9,2,128]{3,2,1,0:T(2,128)} %broadcast_in_dim.2), calls=%async_computation.1 | async-start | bytes 294912 | tf_op jit(solution)/shard_map/all_to_all | solution.py:584
  42.9 9.2 %copy-start.4 = (f32[2,2,96,96]{3,2,1,0:T(8,128)S(1)}, f32[2,2,96,96]{3,2,1,0:T(8,128)}, u32[]{:S(2)}) copy-start(f32[2,2,96,96]{3,2,1,0:T(8,128)} %object_ref.3) | copy-start | bytes 442372
  42.9 7.7 %collective-permute-start.9 = (f32[96,384]{1,0:T(8,128)S(1)}, f32[96,384]{1,0:T(8,128)S(1)}, u32[]{:S(2)}, u32[]{:S(2)}) collective-permute-start(f32[96,384]{1,0:T(8,128)S(1)} %get-tuple-element.23), channel_id=1, source_target_pairs={{0,1},{1,0},{2,3},{3,2},{4,5},{5,4},{6,7},{7,6},{8,9},{9,8},{10,11... | collective-permute-start | bytes 442376 | tf_op jit(solution)/shard_map/ppermute | solution.py:681
  50.7 1.4 %collective-permute-start.6 = (f32[3,96,128]{2,1,0:T(8,128)S(1)}, f32[3,96,128]{2,1,0:T(8,128)S(1)}, u32[]{:S(2)}, u32[]{:S(2)}) collective-permute-start(f32[3,96,128]{2,1,0:T(8,128)S(1)} %bitcast.2), channel_id=1, source_target_pairs={{0,2},{2,0},{1,3},{3,1},{4,6},{6,4},{5,7},{7,5},{8,10},{10,8},{9,1... | collective-permute-start | bytes 442376 | tf_op jit(solution)/shard_map/ppermute | solution.py:552

commit v6 on v5

--- a/solution.py
+++ b/solution.py
@@ -17,7 +17,6 @@
 f32 = jnp.float32
 bf16 = jnp.bfloat16
 VMEM = pl.BlockSpec(memory_space=pltpu.VMEM)
-SMEM = pl.BlockSpec(memory_space=pltpu.SMEM)
 ANY = pl.BlockSpec(memory_space=pl.ANY)
 ROWS = ("pair", "core")
 
@@ -25,35 +24,29 @@
 def matrices(width):
     half = width // 2
     k = np.arange(half)
-    angle = (k[:, None] * k[None, :] % half) * (2.0 * math.pi / half)
-    cosine = np.cos(angle) / math.sqrt(width)
-    sine = np.sin(angle) / math.sqrt(width)
-    right = np.zeros((2, LANES, 2, LANES))
-    right[0, :half, 0, :half] = cosine
-    right[0, :half, 1, :half] = -sine
-    right[1, :half, 0, :half] = sine
-    right[1, :half, 1, :half] = cosine
-    right = right.reshape(2 * LANES, 2 * LANES)
-    left = np.block([[cosine, sine], [-sine, cosine]])
+    turns = [2 * k[:, None] * k[None, :], k[:, None] * (2 * k[None, :] + 1)]
+    turns.append(turns[1].T)
+    rights, lefts = [], []
 
     def halves(matrix):
         high = matrix.astype(np.float32).astype(bf16)
         low = (matrix - high.astype(np.float64)).astype(np.float32).astype(bf16)
         return high, low
 
-    right_high, right_low = halves(right)
-    left_high, left_low = halves(left)
-    turn = k * (2.0 * math.pi / width)
-    turns = np.stack([np.cos(turn), np.sin(turn)]).astype(np.float32)
-    lane_turns = np.zeros((2, 8, LANES), np.float32)
-    lane_turns[:, :, :half] = turns[:, None, :]
-    row_turns = np.broadcast_to(turns[:, :, None], (2, half, LANES)).copy()
-    return (
-        np.concatenate([right_high, right_high, right_low], 0),
-        np.concatenate([left_high, left_high, left_low], 1),
-        lane_turns,
-        row_turns,
-    )
+    for turn in turns:
+        angle = (turn % width) * (2.0 * math.pi / width)
+        cosine = np.cos(angle) / math.sqrt(width)
+        sine = np.sin(angle) / math.sqrt(width)
+        right = np.zeros((2, LANES, 2, LANES))
+        right[0, :half, 0, :half] = cosine
+        right[0, :half, 1, :half] = -sine
+        right[1, :half, 0, :half] = sine
+        right[1, :half, 1, :half] = cosine
+        high, low = halves(right.reshape(2 * LANES, 2 * LANES))
+        rights.append(np.stack([high, low]))
+        high, low = halves(np.block([[cosine.T, sine.T], [-sine.T, cosine.T]]))
+        lefts.append(np.concatenate([high, low], 0))
+    return np.stack(rights), np.stack(lefts)
 
 
 def sorters(width):
@@ -145,10 +138,11 @@
 ):
     lanes = lax.broadcasted_iota(jnp.int32, places_out.shape, 1)
     slots = measured_out.shape[0]
-    places = jnp.where(lanes == 2 * slots, counts_ref[0, 0], 0)
+    places = jnp.where(lanes == 2 * slots, counts_ref[...], 0)
     for slot in range(slots):
         for axis in range(2):
-            places = jnp.where(lanes == 2 * slot + axis, offsets_ref[0, 0, slot, axis], places)
+            value = offsets_ref[0, 0, slot : slot + 1, axis : axis + 1]
+            places = jnp.where(lanes == 2 * slot + axis, value, places)
     places_out[...] = places
     width = probe_ref.shape[1]
     half = width // 2
@@ -199,26 +193,20 @@
         measured_ref,
         right_ref,
         left_ref,
-        lane_turn_ref,
-        row_turn_ref,
-        own_out,
-        near_out,
-        far_out,
-    ) = refs[3 * sides : 3 * sides + 10]
-    terms_out = refs[3 * sides + 10 : 3 * sides + 10 + cores]
+        window,
+    ) = refs[3 * sides : 3 * sides + 6]
+    terms_out = refs[3 * sides + 6 : 3 * sides + 6 + cores]
     (
         obj,
-        acc,
-        window,
         carried,
         terms,
         places,
         arrived,
-    ) = refs[3 * sides + 10 + cores : 3 * sides + 17 + cores]
+    ) = refs[3 * sides + 6 + cores : 3 * sides + 11 + cores]
     copy = pltpu.make_async_copy(places_ref, places, arrived)
     copy.start()
     slots = measured_ref.shape[0]
-    work = refs[3 * sides + 17 + cores :]
+    work = refs[3 * sides + 11 + cores :]
     data, out_right, mid, out_left = (work[k * slots : (k + 1) * slots] for k in range(4))
     width = wave_ref.shape[1]
     half = width // 2
@@ -268,24 +256,20 @@
                         pltpu.roll(obj[plane, j, source, :], back, 1),
                         pltpu.roll(obj[plane, j + 1, source, :], tile - column, 1),
                     )
-    acc[...] = jnp.zeros(acc.shape, f32)
-
-    lane_turn = [jnp.broadcast_to(lane_turn_ref[j, :1, :], (step, LANES)) for j in range(2)]
     span = 2 * LANES
 
     def put(slot, block, row, a, b):
-        rows = pl.ds(block * width + row, step)
         high, low = halves_of(jnp.concatenate([a, b], 1))
-        data[slot][rows, :span] = high
-        data[slot][rows, span:] = low
-
-    def multiply_right(slot):
-        for start in range(0, 2 * width, width):
-            rows = slice(start, start + width)
-            left = jnp.concatenate([data[slot][rows, :], data[slot][rows, :span]], 1)
-            out_right[slot][rows, :] = jnp.dot(
-                left, right_ref[...], preferred_element_type=f32
-            )
+        data[slot][block, pl.ds(row, step), :] = high
+        data[slot][block, pl.ds(width + row, step), :] = low
+
+    def multiply_right(slot, odd):
+        for block in range(2):
+            rows = slice(block * width, (block + 1) * width)
+            left = data[slot][block]
+            out = jnp.dot(left, right_ref[odd * block, 0], preferred_element_type=f32)
+            low = jnp.dot(left[:width], right_ref[odd * block, 1], preferred_element_type=f32)
+            out_right[slot][rows, :] = out[:width] + (out[width:] + low)
             yield
 
     def put_mid(slot, block, start, first, second):
@@ -293,13 +277,15 @@
             high, low = halves_of(jnp.concatenate([first[part], second[part]], 1))
             mid[slot][block, pl.ds(part * half + start, step), :] = high
             mid[slot][block, pl.ds((2 + part) * half + start, step), :] = low
-            mid[slot][block, pl.ds((4 + part) * half + start, step), :] = high
-
-    def multiply_left(slot):
+
+    def multiply_left(slot, odd):
         for block in range(2):
-            out_left[slot][block] = jnp.dot(
-                left_ref[...], mid[slot][block], preferred_element_type=f32
-            )
+            both = left_ref[odd * block]
+            high = mid[slot][block, :width]
+            low = mid[slot][block, width:]
+            out = jnp.dot(both, high, preferred_element_type=f32)
+            rest = jnp.dot(both[:width], low, preferred_element_type=f32)
+            out_left[slot][block] = out[:width] + (out[width:] + rest)
             yield
 
     def get_right(slot, block, row):
@@ -313,30 +299,27 @@
             out_left[slot][block, pl.ds(half + start, step), columns],
         )
 
-    def row_turn(row):
-        return row_turn_ref[0, pl.ds(row, step), :], row_turn_ref[1, pl.ds(row, step), :]
-
     def forward(slot, source):
         for row in range(0, half, step):
             for side, ((a0, b0), (a1, b1)) in enumerate(source(slot, row)):
                 place = side * half + row
                 put(slot, 0, place, a0 + a1, b0 + b1)
-                put(slot, 1, place, *times_conj(*lane_turn, a0 - a1, b0 - b1))
+                put(slot, 1, place, a0 - a1, b0 - b1)
             if row % part_rows == part_rows - step:
                 yield
-        yield from multiply_right(slot)
+        yield from multiply_right(slot, 1)
         for row in range(0, half, step):
             even, odd = [], []
             for j in range(2):
                 a0, b0 = get_right(slot, j, row)
                 a1, b1 = get_right(slot, j, half + row)
                 even.append((a0 + a1, b0 + b1))
-                odd.append(times_conj(*row_turn(row), a0 - a1, b0 - b1))
+                odd.append((a0 - a1, b0 - b1))
             put_mid(slot, 0, row, *even)
             put_mid(slot, 1, row, *odd)
             if row % part_rows == part_rows - step:
                 yield
-        yield from multiply_left(slot)
+        yield from multiply_left(slot, 1)
 
     def inverse(slot, source):
         for row in range(0, width, step):
@@ -344,21 +327,21 @@
                 put(slot, j, row, a, b)
             if row % (2 * part_rows) == 2 * part_rows - step:
                 yield
-        yield from multiply_right(slot)
+        yield from multiply_right(slot, 2)
         for row in range(0, width, step):
             a0, b0 = get_right(slot, 0, row)
-            a1, b1 = times_conj(*lane_turn, *get_right(slot, 1, row))
+            a1, b1 = get_right(slot, 1, row)
             put_mid(slot, row // half, row % half, (a0 + a1, b0 + b1), (a0 - a1, b0 - b1))
             if row % (2 * part_rows) == 2 * part_rows - step:
                 yield
-        yield from multiply_left(slot)
+        yield from multiply_left(slot, 2)
 
     def frequency(slot, row, j):
         return get_left(slot, row // half, j, row % half)
 
     def natural(slot, row, j):
         b0, a0 = get_left(slot, 0, j, row)
-        b1, a1 = times_conj(*row_turn(row), *get_left(slot, 1, j, row))
+        b1, a1 = get_left(slot, 1, j, row)
         return (a0 + a1, b0 + b1), (a0 - a1, b0 - b1)
 
     def at(ref, first, row, j):
@@ -474,6 +457,26 @@
     for k, out in enumerate(terms_out):
         out[...] = terms[k]
 
+
+def place_kernel(paired, cores, places_ref, window, own_out, near_out, far_out, acc, places, arrived):
+    copy = pltpu.make_async_copy(places_ref, places, arrived)
+    copy.start()
+    acc[...] = jnp.zeros(acc.shape, f32)
+    sides = acc.shape[1]
+    tile = acc.shape[2] // 3
+    slots = window.shape[2] // (2 * tile)
+    width = window.shape[2] // slots
+    half = width // 2
+    column_of = lax.axis_index("col")
+    row_starts = [pl.multiple_of(place * tile, 8) for place in row_places(cores)]
+    copy.wait()
+    shift = tile - half
+    corners = [
+        (places[0, 2 * slot] + shift, places[0, 2 * slot + 1] + shift) for slot in range(slots)
+    ]
+    live = [(slot < places[0, 2 * slots]).astype(f32) for slot in range(slots)]
+    chunk = half
+    lane = lane_ids(chunk)
     for slot in range(slots):
         row, column = corners[slot]
         inside = lane >= column
@@ -626,7 +629,7 @@
             shape(slots, width, 2 * LANES),
             shape(8, LANES, kind=jnp.int32),
         ],
-        in_specs=[SMEM] * 2 + [VMEM] * 3,
+        in_specs=[VMEM] * 5,
         out_specs=[VMEM] * 4,
         cost_estimate=pl.CostEstimate(flops=10**10, bytes_accessed=10**7, transcendentals=0),
         compiler_params=small,
@@ -637,28 +640,36 @@
     strip = shape(tile, sides * 3 * LANES)
     scratch = [
         pltpu.VMEM((4, 3, 3 * tile, LANES), f32),
-        pltpu.VMEM((4, sides, 3 * tile, LANES), f32),
-        pltpu.VMEM((4, 2, total, LANES), f32),
         pltpu.VMEM((2, 2, total, LANES), f32),
         pltpu.VMEM((cores, 3, width // cores, LANES), f32),
         pltpu.SMEM((8, LANES), jnp.int32),
         pltpu.SemaphoreType.DMA,
     ]
-    scratch += [pltpu.VMEM((2 * width, 4 * LANES), bf16)] * slots
+    scratch += [pltpu.VMEM((2, 2 * width, 2 * LANES), bf16)] * slots
     scratch += [pltpu.VMEM((2 * width, 2 * LANES), f32)] * slots
-    scratch += [pltpu.VMEM((2, 3 * width, 2 * LANES), bf16)] * slots
+    scratch += [pltpu.VMEM((2, 2 * width, 2 * LANES), bf16)] * slots
     scratch += [pltpu.VMEM((2, width, 2 * LANES), f32)] * slots
     term = shape(3, width // cores, LANES)
-    strips = pl.pallas_call(
+    gradients, *terms = pl.pallas_call(
         functools.partial(position_kernel, paired, cores),
-        out_shape=[strip] * 3 + [term] * cores,
-        in_specs=[ANY] + [VMEM] * (3 * sides + 7),
-        out_specs=[VMEM] * (3 + cores),
+        out_shape=[shape(4, 2, total, LANES)] + [term] * cores,
+        in_specs=[ANY] + [VMEM] * (3 * sides + 5),
+        out_specs=[VMEM] * (1 + cores),
         scratch_shapes=scratch,
         compiler_params=large,
     )(places, *own, *near, *far, wave, trans, intensities, *matrices(width))
-    own_strip, near_strip, far_strip = strips[:3]
-    terms = strips[3:]
+    own_strip, near_strip, far_strip = pl.pallas_call(
+        functools.partial(place_kernel, paired, cores),
+        out_shape=[strip] * 3,
+        in_specs=[ANY, VMEM],
+        out_specs=[VMEM] * 3,
+        scratch_shapes=[
+            pltpu.VMEM((4, sides, 3 * tile, LANES), f32),
+            pltpu.SMEM((8, LANES), jnp.int32),
+            pltpu.SemaphoreType.DMA,
+        ],
+        compiler_params=small,
+    )(places, gradients)
 
     if cores == 2:
         mine = all_sum(terms[0] + from_near(terms[1], cores), ("pair", "col"))

time: 53.5 us -> 52.8 us (0.987)
  waiting for transfers between devices: 15.6 us -> 14.2 us
    pallas_call x0 -> x1, Pallas kernels: none -> 1.62 us  [shards(): pl.pallas_call(functools.partial(place_kernel, paired, cores), out_shape=...]
    all_to_all x2, waiting for transfers between devices: 13.2 us -> 11.6 us  [all_sum(): x = lax.all_to_all(x, group, 0, 0, tiled=True)]
    pallas_call x1, Pallas kernels: 6.69 us -> 6.01 us  [shards(): pl.pallas_call(functools.partial(position_kernel, paired, cores), out_sha...]
    pallas_call x1, Pallas kernels: 1.64 us -> 1.09 us  [shards(): pl.pallas_call(prepare_kernel, out_shape=[shape(2, width, 2 * LANES), sha...]
  transfers between devices with their start and end apart: 12 -> 12, of which waited for: 4 -> 5; matrix products, arithmetic and copies ran while one was open for 1% -> 1% of each run, Pallas kernels for 3% -> 5%
where the time goes in v6:
time: 52.8 us; the launch traced here: 52.4 us
  starting transfers between devices  24.3 us (46%)
  waiting for transfers between devices  14.2 us (27%)
  Pallas kernels  9.93 us (19%)
  local copies, waits for them, and re-layouts  1.71 us (3%)
  between operations  1.49 us (3%)
  other arithmetic  0.74 us (1%)
    all_to_all x2, waiting for transfers between devices, all_sum(): x = lax.all_to_all(x, group, 0, 0, tiled=True)  11.6 us
    all_to_all x2, starting transfers between devices, all_sum(): x = lax.all_to_all(x, group, 0, 0, tiled=True)  10.7 us
    ppermute x5, starting transfers between devices, from_near(): return lax.ppermute(x, 'core', [(0, 1), (1, 0)])  6.72 us
    pallas_call x1, Pallas kernels, shards(): pl.pallas_call(functools.partial(position_kernel, paired, cores), out_sha...  6.01 us
    ppermute x1, starting transfers between devices, shards(): beside = [lax.ppermute(cells, 'col', [(0, 1), (1, 0)])]  3.06 us
    ppermute x5, waiting for transfers between devices, from_near(): return lax.ppermute(x, 'core', [(0, 1), (1, 0)])  2.57 us
    ppermute x1, starting transfers between devices, shards(): received = [lax.ppermute(parts[1], 'col', [(0, 1), (1, 0)])]  1.87 us
    pallas_call x1, Pallas kernels, shards(): pl.pallas_call(functools.partial(place_kernel, paired, cores), out_shape=...  1.62 us
  transfers between devices with their start and end apart: 12, of which 5 were waited for; matrix products, arithmetic and copies ran while one was open for 1% of the time, Pallas kernels for 5%

profile of v6, /device:TPU:0, one launch (start us, length us, event | category | flops | bytes accessed | tf_op | source)
XLA Modules:
  0.0 52.4 jit_solution(7355237166294966581)
XLA Ops:
  0.6 0.0 copy-start.2
  0.6 0.0 copy-start.3
  0.7 1.0 %copy-done.3 = f32[2,2,96,96]{3,2,1,0:T(8,128)S(1)} copy-done((f32[2,2,96,96]{3,2,1,0:T(8,128)S(1)}, f32[2,2,96,96]{3,2,1,0:T(8,128)}, u32[]{:S(2)}) %copy-start.3) | copy-done | bytes 147480
  1.6 0.0 copy-start.5
  1.6 0.0 copy-start.6
  1.6 0.0 copy-start.7
  1.6 0.1 shard_map.96.refs_0_
  1.7 3.1 %collective-permute-start = (f32[96,384]{1,0:T(8,128)S(1)}, f32[96,384]{1,0:T(8,128)S(1)}, u32[]{:S(2)}, u32[]{:S(2)}) collective-permute-start(f32[96,384]{1,0:T(8,128)S(1)} %shard_map.96.refs_0_), channel_id=1, source_target_pairs={{0,1},{1,0},{2,3},{3,2},{4,5},{5,4},{6,7},{7,6},{8,9},{9,8},{10,11... | collective-permute-start | bytes 442376 | tf_op jit(solution)/shard_map/ppermute | solution.py:614
  4.8 0.7 %collective-permute-start.4 = (f32[96,384]{1,0:T(8,128)S(1)}, f32[96,384]{1,0:T(8,128)S(1)}, u32[]{:S(2)}, u32[]{:S(2)}) collective-permute-start(f32[96,384]{1,0:T(8,128)S(1)} %shard_map.96.refs_0_), channel_id=1, source_target_pairs={{2,5},{4,3},{3,4},{5,2},{6,9},{8,7},{7,8},{9,6},{10,13},{12,11},{1... | collective-permute-start | bytes 442376 | tf_op jit(solution)/shard_map/ppermute | solution.py:573
  5.5 0.7 %collective-permute-start.3 = (f32[96,384]{1,0:T(8,128)S(1)}, f32[96,384]{1,0:T(8,128)S(1)}, u32[]{:S(2)}, u32[]{:S(2)}) collective-permute-start(f32[96,384]{1,0:T(8,128)S(1)} %shard_map.96.refs_0_), channel_id=1, source_target_pairs={{2,4},{6,8},{10,12},{14,16},{18,20},{22,24},{26,28},{4,2},{8,6},{1... | collective-permute-start | bytes 442376 | tf_op jit(solution)/shard_map/ppermute | solution.py:563
  6.1 4.2 %collective-permute-start.1 = (f32[96,384]{1,0:T(8,128)S(1)}, f32[96,384]{1,0:T(8,128)S(1)}, u32[]{:S(2)}, u32[]{:S(2)}) collective-permute-start(f32[96,384]{1,0:T(8,128)S(1)} %shard_map.96.refs_0_), channel_id=1, source_target_pairs={{0,2},{2,0},{1,3},{3,1},{4,6},{6,4},{5,7},{7,5},{8,10},{10,8},{9,1... | collective-permute-start | bytes 442376 | tf_op jit(solution)/shard_map/ppermute | solution.py:555
  10.9 0.0 copy-start
  11.0 0.0 copy-start.1
  11.0 0.0 collective-permute-done.refs_1_
  11.0 0.1 collective-permute-start.2
  11.1 0.0 copy-done.2
  11.1 0.0 copy-done.5
  11.1 0.0 copy-done.6
  11.1 0.0 copy-done.7
  11.1 1.1 %shard_map.95 = (f32[2,192,256]{2,1,0:T(8,128)S(1)}, f32[2,192,256]{2,1,0:T(8,128)S(1)}, f32[2,192,256]{2,1,0:T(8,128)S(1)}, s32[8,128]{1,0:T(8,128)S(1)}) custom-call(s32[1,1,2,2]{3,2,1,0:T(2,128)S(1)} %copy-done.7, s32[1,1]{1,0:T(1,128)S(6)} %copy.10.counts_ref, f32[2,192,192]{2,1,0:T(8,128)S(1)} %copy-done.2, f32[192,192]{1,0:T(8,128)S(1)} %copy-done.6, ...), custom_call_target="tpu_custom_call" | custom-call | flops 10000000000 | bytes 10000000 | tf_op jit(solution)/shard_map/pallas_call | solution.py:624
  12.2 0.0 collective-permute-done.4.refs_5_
  12.2 0.0 collective-permute-done.3.refs_4_
  12.2 0.0 collective-permute-done.1.refs_2_
  12.2 0.2 collective-permute-done.2.refs_3_
  12.4 0.0 copy-done
  12.4 0.0 copy-done.1
  12.4 6.0 %shard_map.97 = (f32[4,2,384,128]{3,2,1,0:T(8,128)S(1)}, f32[3,96,128]{2,1,0:T(8,128)S(1)}, f32[3,96,128]{2,1,0:T(8,128)S(1)}) custom-call(s32[8,128]{1,0:T(8,128)S(1)} %get-tuple-element.14.places_ref, f32[96,384]{1,0:T(8,128)S(1)} %shard_map.96.refs_0_, f32[96,384]{1,0:T(8,128)S(1)} %collective-permute-done.refs_1_, ...), custom_call_target="tpu_custom_call" | custom-call | tf_op jit(solution)/shard_map/pallas_call | solution.py:653
  18.4 2.3 %collective-permute-start.5 = (f32[3,96,128]{2,1,0:T(8,128)S(1)}, f32[3,96,128]{2,1,0:T(8,128)S(1)}, u32[]{:S(2)}, u32[]{:S(2)}) collective-permute-start(f32[3,96,128]{2,1,0:T(8,128)S(1)} %get-tuple-element.19), channel_id=1, source_target_pairs={{0,2},{2,0},{1,3},{3,1},{4,6},{6,4},{5,7},{7,5},{8,10},{10,8},{9,1... | collective-permute-start | bytes 442376 | tf_op jit(solution)/shard_map/ppermute | solution.py:555
  20.8 1.0 %collective-permute-done.5 = f32[3,96,128]{2,1,0:T(8,128)S(1)} collective-permute-done((f32[3,96,128]{2,1,0:T(8,128)S(1)}, f32[3,96,128]{2,1,0:T(8,128)S(1)}, u32[]{:S(2)}, u32[]{:S(2)}) %collective-permute-start.5) | collective-permute-done | bytes 147488 | tf_op jit(solution)/shard_map/ppermute | solution.py:555
  21.8 0.7 %add.3 = f32[3,96,128]{2,1,0:T(8,128)} add(f32[3,96,128]{2,1,0:T(8,128)S(1)} %get-tuple-element.18, f32[3,96,128]{2,1,0:T(8,128)S(1)} %collective-permute-done.5) | non-fusion elementwise | flops 36864 | bytes 442368 | tf_op jit(solution)/shard_map/add | solution.py:675
  22.5 7.2 %all-to-all-start = ((f32[16,9,2,128]{3,2,1,0:T(2,128)}), f32[16,9,2,128]{3,2,1,0:T(2,128)S(1)}, u32[]{:S(2)}, u32[]{:S(2)}) async-start(f32[16,9,2,128]{3,2,1,0:T(2,128)} %bitcast), calls=%async_computation | async-start | bytes 294912 | tf_op jit(solution)/shard_map/all_to_all | solution.py:585
  29.7 0.0 copy-start.4
  29.7 1.6 %shard_map.98 = (f32[96,768]{1,0:T(8,128)S(1)}, f32[96,768]{1,0:T(8,128)S(1)}, f32[96,768]{1,0:T(8,128)S(1)}) custom-call(s32[8,128]{1,0:T(8,128)S(1)} %get-tuple-element.14.places_ref, f32[4,2,384,128]{3,2,1,0:T(8,128)S(1)} %get-tuple-element.20.window), custom_call_target="tpu_custom_call" | custom-call | tf_op jit(solution)/shard_map/pallas_call | solution.py:661
  31.3 0.1 collective-permute-start.7
  31.4 0.7 %collective-permute-start.8 = (f32[96,768]{1,0:T(8,128)S(1)}, f32[96,768]{1,0:T(8,128)S(1)}, u32[]{:S(2)}, u32[]{:S(2)}) collective-permute-start(f32[96,768]{1,0:T(8,128)S(1)} %get-tuple-element.23), channel_id=1, source_target_pairs={{2,4},{6,8},{10,12},{14,16},{18,20},{22,24},{26,28},{4,2},{8,6},{1... | collective-permute-start | bytes 884744 | tf_op jit(solution)/shard_map/ppermute | solution.py:563
  32.1 5.7 %all-to-all-done = f32[16,9,2,128]{3,2,1,0:T(2,128)S(1)} async-done(((f32[16,9,2,128]{3,2,1,0:T(2,128)}), f32[16,9,2,128]{3,2,1,0:T(2,128)S(1)}, u32[]{:S(2)}, u32[]{:S(2)}) %all-to-all-start) | async-done | bytes 147488 | tf_op jit(solution)/shard_map/all_to_all | solution.py:585
  37.8 0.1 reduce_sum.9
  37.9 0.7 %broadcast_in_dim.2 = f32[16,9,2,128]{3,2,1,0:T(2,128)} broadcast(f32[9,2,128]{2,1,0:T(2,128)S(1)} %reduce_sum.9), dimensions={1,2,3} | broadcast | bytes 156672 | tf_op jit(solution)/shard_map/broadcast_in_dim | solution.py:586
  38.6 3.5 %all-to-all-start.1 = ((f32[16,9,2,128]{3,2,1,0:T(2,128)}), f32[16,9,2,128]{3,2,1,0:T(2,128)S(1)}, u32[]{:S(2)}, u32[]{:S(2)}) async-start(f32[16,9,2,128]{3,2,1,0:T(2,128)} %broadcast_in_dim.2), calls=%async_computation.1 | async-start | bytes 294912 | tf_op jit(solution)/shard_map/all_to_all | solution.py:587
  42.1 0.0 collective-permute-done.7.near_ref
  42.1 0.0 collective-permute-done.8.far_ref
  42.2 1.9 %collective-permute-start.9 = (f32[96,384]{1,0:T(8,128)S(1)}, f32[96,384]{1,0:T(8,128)S(1)}, u32[]{:S(2)}, u32[]{:S(2)}) collective-permute-start(f32[96,384]{1,0:T(8,128)S(1)} %get-tuple-element.25), channel_id=1, source_target_pairs={{0,1},{1,0},{2,3},{3,2},{4,5},{5,4},{6,7},{7,6},{8,9},{9,8},{10,11... | collective-permute-start | bytes 442376 | tf_op jit(solution)/shard_map/ppermute | solution.py:692
  44.1 5.9 %all-to-all-done.1 = f32[16,9,2,128]{3,2,1,0:T(2,128)S(1)} async-done(((f32[16,9,2,128]{3,2,1,0:T(2,128)}), f32[16,9,2,128]{3,2,1,0:T(2,128)S(1)}, u32[]{:S(2)}, u32[]{:S(2)}) %all-to-all-start.1) | async-done | bytes 147488 | tf_op jit(solution)/shard_map/all_to_all | solution.py:587
  50.0 0.0 collective-permute-start.6
  50.0 0.0 collective-permute-done.9.refs_3_
  50.0 1.4 %collective-permute-done.6.refs_1_ = f32[3,96,128]{2,1,0:T(8,128)S(1)} collective-permute-done((f32[3,96,128]{2,1,0:T(8,128)S(1)}, f32[3,96,128]{2,1,0:T(8,128)S(1)}, u32[]{:S(2)}, u32[]{:S(2)}) %collective-permute-start.6) | collective-permute-done | bytes 147488 | tf_op jit(solution)/shard_map/ppermute | solution.py:555
  51.3 0.0 copy-done.4
  51.3 1.1 %shard_map.100 = (f32[2,2,96,96]{3,2,1,0:T(8,128)}, f32[2,192,192]{2,1,0:T(8,128)}) custom-call(f32[2,2,96,96]{3,2,1,0:T(8,128)S(1)} %copy-done.4, f32[2,192,192]{2,1,0:T(8,128)S(1)} %copy-done.2, f32[3,96,128]{2,1,0:T(8,128)S(1)} %bitcast.3, f32[3,96,128]{2,1,0:T(8,128)S(1)} %collective-permute-done.6.refs_1_, f32[96,384]{1,0:T(8,128)S(1)} %get-tuple-element.24.refs_2_, ...), custom_call_target="tpu_custom_call" | custom-call | tf_op jit(solution)/shard_map/pallas_call | solution.py:695
  (1 shorter events, 0.0 us)
Async XLA Ops:
  0.6 10.4 %copy-start.2 = (f32[2,192,192]{2,1,0:T(8,128)S(1)}, f32[2,192,192]{2,1,0:T(8,128)}, u32[]{:S(2)}) copy-start(f32[2,192,192]{2,1,0:T(8,128)} %probe_ref.3) | copy-start | bytes 884740
  0.6 1.0 %copy-start.3 = (f32[2,2,96,96]{3,2,1,0:T(8,128)S(1)}, f32[2,2,96,96]{3,2,1,0:T(8,128)}, u32[]{:S(2)}) copy-start(f32[2,2,96,96]{3,2,1,0:T(8,128)} %object_ref.3) | copy-start | bytes 442372
  1.6 9.5 %copy-start.5 = (f32[1,1,2,192,192]{4,3,2,1,0:T(8,128)S(1)}, f32[1,1,2,192,192]{4,3,2,1,0:T(8,128)}, u32[]{:S(2)}) copy-start(f32[1,1,2,192,192]{4,3,2,1,0:T(8,128)} %measured_ref.1) | copy-start | bytes 884740
  1.6 9.5 %copy-start.6 = (f32[192,192]{1,0:T(8,128)S(1)}, f32[192,192]{1,0:T(8,128)}, u32[]{:S(2)}) copy-start(f32[192,192]{1,0:T(8,128)} %phase_ref.1) | copy-start | bytes 442372
  1.6 9.5 %copy-start.7 = (s32[1,1,2,2]{3,2,1,0:T(2,128)S(1)}, s32[1,1,2,2]{3,2,1,0:T(2,128)}, u32[]{:S(2)}) copy-start(s32[1,1,2,2]{3,2,1,0:T(2,128)} %offsets_ref.1) | copy-start | bytes 52
  1.7 9.2 %collective-permute-start = (f32[96,384]{1,0:T(8,128)S(1)}, f32[96,384]{1,0:T(8,128)S(1)}, u32[]{:S(2)}, u32[]{:S(2)}) collective-permute-start(f32[96,384]{1,0:T(8,128)S(1)} %shard_map.96.refs_0_), channel_id=1, source_target_pairs={{0,1},{1,0},{2,3},{3,2},{4,5},{5,4},{6,7},{7,6},{8,9},{9,8},{10,11... | collective-permute-start | bytes 442376 | tf_op jit(solution)/shard_map/ppermute | solution.py:614
  4.8 7.4 %collective-permute-start.4 = (f32[96,384]{1,0:T(8,128)S(1)}, f32[96,384]{1,0:T(8,128)S(1)}, u32[]{:S(2)}, u32[]{:S(2)}) collective-permute-start(f32[96,384]{1,0:T(8,128)S(1)} %shard_map.96.refs_0_), channel_id=1, source_target_pairs={{2,5},{4,3},{3,4},{5,2},{6,9},{8,7},{7,8},{9,6},{10,13},{12,11},{1... | collective-permute-start | bytes 442376 | tf_op jit(solution)/shard_map/ppermute | solution.py:573
  5.5 6.8 %collective-permute-start.3 = (f32[96,384]{1,0:T(8,128)S(1)}, f32[96,384]{1,0:T(8,128)S(1)}, u32[]{:S(2)}, u32[]{:S(2)}) collective-permute-start(f32[96,384]{1,0:T(8,128)S(1)} %shard_map.96.refs_0_), channel_id=1, source_target_pairs={{2,4},{6,8},{10,12},{14,16},{18,20},{22,24},{26,28},{4,2},{8,6},{1... | collective-permute-start | bytes 442376 | tf_op jit(solution)/shard_map/ppermute | solution.py:563
  6.1 6.1 %collective-permute-start.1 = (f32[96,384]{1,0:T(8,128)S(1)}, f32[96,384]{1,0:T(8,128)S(1)}, u32[]{:S(2)}, u32[]{:S(2)}) collective-permute-start(f32[96,384]{1,0:T(8,128)S(1)} %shard_map.96.refs_0_), channel_id=1, source_target_pairs={{0,2},{2,0},{1,3},{3,1},{4,6},{6,4},{5,7},{7,5},{8,10},{10,8},{9,1... | collective-permute-start | bytes 442376 | tf_op jit(solution)/shard_map/ppermute | solution.py:555
  10.9 1.5 %copy-start = (bf16[3,2,256,256]{3,2,1,0:T(8,128)(2,1)S(1)}, bf16[3,2,256,256]{3,2,1,0:T(8,128)(2,1)}, u32[]{:S(2)}) copy-start(bf16[3,2,256,256]{3,2,1,0:T(8,128)(2,1)} %constant.6.clone.refs_9_) | copy-start | bytes 2359300
  11.0 1.5 %copy-start.1 = (bf16[3,384,192]{2,1,0:T(8,128)(2,1)S(1)}, bf16[3,384,192]{2,1,0:T(8,128)(2,1)}, u32[]{:S(2)}) copy-start(bf16[3,384,192]{2,1,0:T(8,128)(2,1)} %constant.7.clone.refs_10_) | copy-start | bytes 1327108
  11.0 1.4 %collective-permute-start.2 = (f32[96,384]{1,0:T(8,128)S(1)}, f32[96,384]{1,0:T(8,128)S(1)}, u32[]{:S(2)}, u32[]{:S(2)}) collective-permute-start(f32[96,384]{1,0:T(8,128)S(1)} %collective-permute-done.refs_1_), channel_id=1, source_target_pairs={{0,2},{2,0},{1,3},{3,1},{4,6},{6,4},{5,7},{7,5},{8,10},{10,8},{9,1... | collective-permute-start | bytes 442376 | tf_op jit(solution)/shard_map/ppermute | solution.py:555
  18.4 3.4 %collective-permute-start.5 = (f32[3,96,128]{2,1,0:T(8,128)S(1)}, f32[3,96,128]{2,1,0:T(8,128)S(1)}, u32[]{:S(2)}, u32[]{:S(2)}) collective-permute-start(f32[3,96,128]{2,1,0:T(8,128)S(1)} %get-tuple-element.19), channel_id=1, source_target_pairs={{0,2},{2,0},{1,3},{3,1},{4,6},{6,4},{5,7},{7,5},{8,10},{10,8},{9,1... | collective-permute-start | bytes 442376 | tf_op jit(solution)/shard_map/ppermute | solution.py:555
  22.5 15.4 %all-to-all-start = ((f32[16,9,2,128]{3,2,1,0:T(2,128)}), f32[16,9,2,128]{3,2,1,0:T(2,128)S(1)}, u32[]{:S(2)}, u32[]{:S(2)}) async-start(f32[16,9,2,128]{3,2,1,0:T(2,128)} %bitcast), calls=%async_computation | async-start | bytes 294912 | tf_op jit(solution)/shard_map/all_to_all | solution.py:585
  29.7 21.7 %copy-start.4 = (f32[2,2,96,96]{3,2,1,0:T(8,128)S(1)}, f32[2,2,96,96]{3,2,1,0:T(8,128)}, u32[]{:S(2)}) copy-start(f32[2,2,96,96]{3,2,1,0:T(8,128)} %object_ref.3) | copy-start | bytes 442372
  31.3 10.8 %collective-permute-start.7 = (f32[96,768]{1,0:T(8,128)S(1)}, f32[96,768]{1,0:T(8,128)S(1)}, u32[]{:S(2)}, u32[]{:S(2)}) collective-permute-start(f32[96,768]{1,0:T(8,128)S(1)} %get-tuple-element.22), channel_id=1, source_target_pairs={{0,2},{2,0},{1,3},{3,1},{4,6},{6,4},{5,7},{7,5},{8,10},{10,8},{9,1... | collective-permute-start | bytes 884744 | tf_op jit(solution)/shard_map/ppermute | solution.py:555
  31.4 10.7 %collective-permute-start.8 = (f32[96,768]{1,0:T(8,128)S(1)}, f32[96,768]{1,0:T(8,128)S(1)}, u32[]{:S(2)}, u32[]{:S(2)}) collective-permute-start(f32[96,768]{1,0:T(8,128)S(1)} %get-tuple-element.23), channel_id=1, source_target_pairs={{2,4},{6,8},{10,12},{14,16},{18,20},{22,24},{26,28},{4,2},{8,6},{1... | collective-permute-start | bytes 884744 | tf_op jit(solution)/shard_map/ppermute | solution.py:563
  38.6 11.4 %all-to-all-start.1 = ((f32[16,9,2,128]{3,2,1,0:T(2,128)}), f32[16,9,2,128]{3,2,1,0:T(2,128)S(1)}, u32[]{:S(2)}, u32[]{:S(2)}) async-start(f32[16,9,2,128]{3,2,1,0:T(2,128)} %broadcast_in_dim.2), calls=%async_computation.1 | async-start | bytes 294912 | tf_op jit(solution)/shard_map/all_to_all | solution.py:587
  42.2 7.8 %collective-permute-start.9 = (f32[96,384]{1,0:T(8,128)S(1)}, f32[96,384]{1,0:T(8,128)S(1)}, u32[]{:S(2)}, u32[]{:S(2)}) collective-permute-start(f32[96,384]{1,0:T(8,128)S(1)} %get-tuple-element.25), channel_id=1, source_target_pairs={{0,1},{1,0},{2,3},{3,2},{4,5},{5,4},{6,7},{7,6},{8,9},{9,8},{10,11... | collective-permute-start | bytes 442376 | tf_op jit(solution)/shard_map/ppermute | solution.py:692
  50.0 1.4 %collective-permute-start.6 = (f32[3,96,128]{2,1,0:T(8,128)S(1)}, f32[3,96,128]{2,1,0:T(8,128)S(1)}, u32[]{:S(2)}, u32[]{:S(2)}) collective-permute-start(f32[3,96,128]{2,1,0:T(8,128)S(1)} %bitcast.2), channel_id=1, source_target_pairs={{0,2},{2,0},{1,3},{3,1},{4,6},{6,4},{5,7},{7,5},{8,10},{10,8},{9,1... | collective-permute-start | bytes 442376 | tf_op jit(solution)/shard_map/ppermute | solution.py:555

commit v7 on v6

--- a/solution.py
+++ b/solution.py
@@ -226,8 +226,14 @@
             else:
                 place = (1, 0, 2)[side]
             ref = tiles[row * sides + side]
-            parts = [ref[:, j * LANES : (j + 1) * LANES] for j in range(3)]
-            parts.append(last_of(parts, tile))
+            if len(ref.shape) == 2:
+                parts = [ref[:, j * LANES : (j + 1) * LANES] for j in range(3)]
+                parts.append(last_of(parts, tile))
+            else:
+                pad = jnp.zeros((tile, LANES - tile), f32)
+                parts = [
+                    jnp.concatenate([ref[plane // 2, plane % 2], pad], 1) for plane in range(4)
+                ]
             for plane in range(4):
                 obj[plane, place, rows, :] = parts[plane]
         if paired:
@@ -512,6 +518,19 @@
         out[...] = own_ref[:, part] + near_ref[:, part] + far_ref[:, part]
 
 
+def add_kernel(first_ref, second_ref, out_ref):
+    out_ref[...] = first_ref[...] + second_ref[...]
+
+
+def spread_sum_kernel(count, pieces_ref, out_ref):
+    rows = pieces_ref.shape[0] // count
+    total = pieces_ref[:rows]
+    for k in range(1, count):
+        total = total + pieces_ref[k * rows : (k + 1) * rows]
+    for k in range(count):
+        out_ref[k * rows : (k + 1) * rows] = total
+
+
 def update_kernel(rate, cores, object_ref, probe_ref, *refs):
     object_out, probe_out = refs[-2:]
     sums = refs[:cores]
@@ -583,7 +602,14 @@
         x = jnp.pad(x, ((0, piece * count - pairs), (0, 0), (0, 0)))
     x = x.reshape(count, piece, 2, LANES)
     x = lax.all_to_all(x, group, 0, 0, tiled=True)
-    x = jnp.broadcast_to(jnp.sum(x, 0)[None], x.shape)
+    whole = x.shape
+    x = pl.pallas_call(
+        functools.partial(spread_sum_kernel, count),
+        out_shape=jax.ShapeDtypeStruct((count * piece * 2, LANES), f32),
+        in_specs=[VMEM],
+        out_specs=VMEM,
+        compiler_params=pltpu.CompilerParams(vmem_limit_bytes=6 * 1024 * 1024),
+    )(x.reshape(count * piece * 2, LANES)).reshape(whole)
     x = lax.all_to_all(x, group, 0, 0, tiled=True)
     return x.reshape(count * piece, 2, LANES)[:pairs].reshape(shape)
 
@@ -611,7 +637,7 @@
         compiler_params=small,
     )(object_slices)
     if paired:
-        beside = [lax.ppermute(cells, "col", [(0, 1), (1, 0)])]
+        beside = [lax.ppermute(object_slices, "col", [(0, 1), (1, 0)])]
     else:
         beside = [passed_along(cells, "col", 1), passed_along(cells, "col", -1)]
     own = [cells] + beside
@@ -672,7 +698,14 @@
     )(places, gradients)
 
     if cores == 2:
-        mine = all_sum(terms[0] + from_near(terms[1], cores), ("pair", "col"))
+        joined = pl.pallas_call(
+            add_kernel,
+            out_shape=term,
+            in_specs=[VMEM] * 2,
+            out_specs=VMEM,
+            compiler_params=small,
+        )(terms[0], from_near(terms[1], cores))
+        mine = all_sum(joined, ("pair", "col"))
         sums = [mine, from_near(mine, cores)]
     else:
         sums = [all_sum(terms[0], ("pair", "col"))]

time: 52.8 us -> 52.7 us (level)
  Pallas kernels: 9.93 us -> 11.2 us
  other arithmetic: 0.74 us -> 0 us
  local copies, waits for them, and re-layouts: 1.71 us -> 1 us
    pallas_call x0 -> x2, Pallas kernels: none -> 1.37 us  [the longest x1 0.69 us: all_sum(): pl.pallas_call(functools.partial(spread_sum_kernel, count), out_shape=jax...]
    broadcast_in_dim x1 -> x0, local copies, waits for them, and re-layouts: 0.7 us -> none  [all_sum(): x = jnp.broadcast_to(jnp.sum(x, 0)[None], x.shape)]
    add x1 -> x0, other arithmetic: 0.68 us -> none  [shards(): mine = all_sum(terms[0] + from_near(terms[1], cores), ('pair', 'col'))]
  transfers between devices with their start and end apart: 12 -> 12, of which waited for: 5 -> 5; matrix products, arithmetic and copies ran while one was open for 1% -> 0% of each run, Pallas kernels for 5% -> 7%
where the time goes in v7:
time: 52.7 us; the launch traced here: 52.4 us
  starting transfers between devices  24.4 us (46%)
  waiting for transfers between devices  14.2 us (27%)
  Pallas kernels  11.2 us (21%)
  between operations  1.48 us (3%)
  local copies, waits for them, and re-layouts  1 us (2%)
    all_to_all x2, waiting for transfers between devices, all_sum(): x = lax.all_to_all(x, group, 0, 0, tiled=True)  11.6 us
    all_to_all x2, starting transfers between devices, all_sum(): x = lax.all_to_all(x, group, 0, 0, tiled=True)  10.7 us
    ppermute x5, starting transfers between devices, from_near(): return lax.ppermute(x, 'core', [(0, 1), (1, 0)])  6.69 us
    pallas_call x1, Pallas kernels, shards(): pl.pallas_call(functools.partial(position_kernel, paired, cores), out_sha...  5.93 us
    ppermute x1, starting transfers between devices, shards(): beside = [lax.ppermute(object_slices, 'col', [(0, 1), (1, 0)])]  3.06 us
    ppermute x5, waiting for transfers between devices, from_near(): return lax.ppermute(x, 'core', [(0, 1), (1, 0)])  2.64 us
    ppermute x1, starting transfers between devices, shards(): received = [lax.ppermute(parts[1], 'col', [(0, 1), (1, 0)])]  1.87 us
    pallas_call x1, Pallas kernels, shards(): pl.pallas_call(functools.partial(place_kernel, paired, cores), out_shape=...  1.64 us
  transfers between devices with their start and end apart: 12, of which 5 were waited for; matrix products, arithmetic and copies ran while one was open for 0% of the time, Pallas kernels for 7%

profile of v7, /device:TPU:0, one launch (start us, length us, event | category | flops | bytes accessed | tf_op | source)
XLA Modules:
  0.0 52.4 jit_solution(1177949102622071494)
XLA Ops:
  0.6 0.0 copy-start.2
  0.6 3.1 %collective-permute-start = (f32[2,2,96,96]{3,2,1,0:T(8,128)}, f32[2,2,96,96]{3,2,1,0:T(8,128)S(1)}, u32[]{:S(2)}, u32[]{:S(2)}) collective-permute-start(f32[2,2,96,96]{3,2,1,0:T(8,128)} %object_ref.3), channel_id=1, source_target_pairs={{0,1},{1,0},{2,3},{3,2},{4,5},{5,4},{6,7},{7,6},{8,9},{9,8},{10,11... | collective-permute-start | bytes 442376 | tf_op jit(solution)/shard_map/ppermute | solution.py:640
  3.7 0.0 copy-start.3
  3.7 1.0 %copy-done.3 = f32[2,2,96,96]{3,2,1,0:T(8,128)S(1)} copy-done((f32[2,2,96,96]{3,2,1,0:T(8,128)S(1)}, f32[2,2,96,96]{3,2,1,0:T(8,128)}, u32[]{:S(2)}) %copy-start.3) | copy-done | bytes 147480
  4.7 0.0 copy-start.5
  4.7 0.0 copy-start.6
  4.7 0.0 copy-start.7
  4.7 0.1 shard_map.96.refs_0_
  4.8 0.8 %collective-permute-start.4 = (f32[96,384]{1,0:T(8,128)S(1)}, f32[96,384]{1,0:T(8,128)S(1)}, u32[]{:S(2)}, u32[]{:S(2)}) collective-permute-start(f32[96,384]{1,0:T(8,128)S(1)} %shard_map.96.refs_0_), channel_id=1, source_target_pairs={{2,5},{4,3},{3,4},{5,2},{6,9},{8,7},{7,8},{9,6},{10,13},{12,11},{1... | collective-permute-start | bytes 442376 | tf_op jit(solution)/shard_map/ppermute | solution.py:592
  5.6 0.7 %collective-permute-start.3 = (f32[96,384]{1,0:T(8,128)S(1)}, f32[96,384]{1,0:T(8,128)S(1)}, u32[]{:S(2)}, u32[]{:S(2)}) collective-permute-start(f32[96,384]{1,0:T(8,128)S(1)} %shard_map.96.refs_0_), channel_id=1, source_target_pairs={{2,4},{6,8},{10,12},{14,16},{18,20},{22,24},{26,28},{4,2},{8,6},{1... | collective-permute-start | bytes 442376 | tf_op jit(solution)/shard_map/ppermute | solution.py:582
  6.3 4.2 %collective-permute-start.1 = (f32[96,384]{1,0:T(8,128)S(1)}, f32[96,384]{1,0:T(8,128)S(1)}, u32[]{:S(2)}, u32[]{:S(2)}) collective-permute-start(f32[96,384]{1,0:T(8,128)S(1)} %shard_map.96.refs_0_), channel_id=1, source_target_pairs={{0,2},{2,0},{1,3},{3,1},{4,6},{6,4},{5,7},{7,5},{8,10},{10,8},{9,1... | collective-permute-start | bytes 442376 | tf_op jit(solution)/shard_map/ppermute | solution.py:574
  11.1 0.0 copy-start
  11.1 0.0 copy-start.1
  11.1 0.0 collective-permute-done.refs_1_
  11.1 0.1 collective-permute-start.2
  11.2 0.0 copy-done.2
  11.2 0.0 copy-done.5
  11.2 0.0 copy-done.6
  11.2 0.0 copy-done.7
  11.2 1.1 %shard_map.95 = (f32[2,192,256]{2,1,0:T(8,128)S(1)}, f32[2,192,256]{2,1,0:T(8,128)S(1)}, f32[2,192,256]{2,1,0:T(8,128)S(1)}, s32[8,128]{1,0:T(8,128)S(1)}) custom-call(s32[1,1,2,2]{3,2,1,0:T(2,128)S(1)} %copy-done.7, s32[1,1]{1,0:T(1,128)S(6)} %copy.10.counts_ref, f32[2,192,192]{2,1,0:T(8,128)S(1)} %copy-done.2, f32[192,192]{1,0:T(8,128)S(1)} %copy-done.6, ...), custom_call_target="tpu_custom_call" | custom-call | flops 10000000000 | bytes 10000000 | tf_op jit(solution)/shard_map/pallas_call | solution.py:650
  12.3 0.0 collective-permute-done.4.refs_5_
  12.3 0.0 collective-permute-done.3.refs_4_
  12.3 0.0 collective-permute-done.1.refs_2_
  12.4 0.3 collective-permute-done.2.refs_3_
  12.6 0.0 copy-done
  12.6 0.0 copy-done.1
  12.6 5.9 %shard_map.97 = (f32[4,2,384,128]{3,2,1,0:T(8,128)S(1)}, f32[3,96,128]{2,1,0:T(8,128)S(1)}, f32[3,96,128]{2,1,0:T(8,128)S(1)}) custom-call(s32[8,128]{1,0:T(8,128)S(1)} %get-tuple-element.14.places_ref, f32[96,384]{1,0:T(8,128)S(1)} %shard_map.96.refs_0_, f32[2,2,96,96]{3,2,1,0:T(8,128)S(1)} %collective-permute-done.refs_1_, ...), custom_call_target="tpu_custom_call" | custom-call | tf_op jit(solution)/shard_map/pallas_call | solution.py:679
  18.6 2.3 %collective-permute-start.5 = (f32[3,96,128]{2,1,0:T(8,128)S(1)}, f32[3,96,128]{2,1,0:T(8,128)S(1)}, u32[]{:S(2)}, u32[]{:S(2)}) collective-permute-start(f32[3,96,128]{2,1,0:T(8,128)S(1)} %get-tuple-element.19), channel_id=1, source_target_pairs={{0,2},{2,0},{1,3},{3,1},{4,6},{6,4},{5,7},{7,5},{8,10},{10,8},{9,1... | collective-permute-start | bytes 442376 | tf_op jit(solution)/shard_map/ppermute | solution.py:574
  20.9 1.0 %collective-permute-done.5.second_ref = f32[3,96,128]{2,1,0:T(8,128)S(1)} collective-permute-done((f32[3,96,128]{2,1,0:T(8,128)S(1)}, f32[3,96,128]{2,1,0:T(8,128)S(1)}, u32[]{:S(2)}, u32[]{:S(2)}) %collective-permute-start.5) | collective-permute-done | bytes 147488 | tf_op jit(solution)/shard_map/ppermute | solution.py:574
  21.9 0.7 %shard_map.98 = f32[3,96,128]{2,1,0:T(8,128)} custom-call(f32[3,96,128]{2,1,0:T(8,128)S(1)} %get-tuple-element.18.first_ref, f32[3,96,128]{2,1,0:T(8,128)S(1)} %collective-permute-done.5.second_ref), custom_call_target="tpu_custom_call" | custom-call | tf_op jit(solution)/shard_map/pallas_call | solution.py:701
  22.6 7.2 %all-to-all-start = ((f32[16,9,2,128]{3,2,1,0:T(2,128)}), f32[16,9,2,128]{3,2,1,0:T(2,128)S(1)}, u32[]{:S(2)}, u32[]{:S(2)}) async-start(f32[16,9,2,128]{3,2,1,0:T(2,128)} %bitcast), calls=%async_computation | async-start | bytes 294912 | tf_op jit(solution)/shard_map/all_to_all | solution.py:604
  29.7 0.0 copy-start.4
  29.8 1.6 %shard_map.100 = (f32[96,768]{1,0:T(8,128)S(1)}, f32[96,768]{1,0:T(8,128)S(1)}, f32[96,768]{1,0:T(8,128)S(1)}) custom-call(s32[8,128]{1,0:T(8,128)S(1)} %get-tuple-element.14.places_ref, f32[4,2,384,128]{3,2,1,0:T(8,128)S(1)} %get-tuple-element.20.window), custom_call_target="tpu_custom_call" | custom-call | tf_op jit(solution)/shard_map/pallas_call | solution.py:687
  31.4 0.1 collective-permute-start.7
  31.5 0.7 %collective-permute-start.8 = (f32[96,768]{1,0:T(8,128)S(1)}, f32[96,768]{1,0:T(8,128)S(1)}, u32[]{:S(2)}, u32[]{:S(2)}) collective-permute-start(f32[96,768]{1,0:T(8,128)S(1)} %get-tuple-element.23), channel_id=1, source_target_pairs={{2,4},{6,8},{10,12},{14,16},{18,20},{22,24},{26,28},{4,2},{8,6},{1... | collective-permute-start | bytes 884744 | tf_op jit(solution)/shard_map/ppermute | solution.py:582
  32.2 5.7 %all-to-all-done = f32[16,9,2,128]{3,2,1,0:T(2,128)S(1)} async-done(((f32[16,9,2,128]{3,2,1,0:T(2,128)}), f32[16,9,2,128]{3,2,1,0:T(2,128)S(1)}, u32[]{:S(2)}, u32[]{:S(2)}) %all-to-all-start) | async-done | bytes 147488 | tf_op jit(solution)/shard_map/all_to_all | solution.py:604
  37.9 0.7 %shard_map.99 = f32[288,128]{1,0:T(8,128)} custom-call(f32[288,128]{1,0:T(8,128)S(1)} %bitcast.6), custom_call_target="tpu_custom_call" | custom-call | tf_op jit(solution)/shard_map/pallas_call | solution.py:606
  38.6 3.5 %all-to-all-start.1 = ((f32[16,9,2,128]{3,2,1,0:T(2,128)}), f32[16,9,2,128]{3,2,1,0:T(2,128)S(1)}, u32[]{:S(2)}, u32[]{:S(2)}) async-start(f32[16,9,2,128]{3,2,1,0:T(2,128)} %bitcast.2), calls=%async_computation.1 | async-start | bytes 294912 | tf_op jit(solution)/shard_map/all_to_all | solution.py:613
  42.1 0.0 collective-permute-done.7.near_ref
  42.1 0.0 collective-permute-done.8.far_ref
  42.2 1.9 %collective-permute-start.9 = (f32[96,384]{1,0:T(8,128)S(1)}, f32[96,384]{1,0:T(8,128)S(1)}, u32[]{:S(2)}, u32[]{:S(2)}) collective-permute-start(f32[96,384]{1,0:T(8,128)S(1)} %get-tuple-element.25), channel_id=1, source_target_pairs={{0,1},{1,0},{2,3},{3,2},{4,5},{5,4},{6,7},{7,6},{8,9},{9,8},{10,11... | collective-permute-start | bytes 442376 | tf_op jit(solution)/shard_map/ppermute | solution.py:725
  44.1 5.9 %all-to-all-done.1 = f32[16,9,2,128]{3,2,1,0:T(2,128)S(1)} async-done(((f32[16,9,2,128]{3,2,1,0:T(2,128)}), f32[16,9,2,128]{3,2,1,0:T(2,128)S(1)}, u32[]{:S(2)}, u32[]{:S(2)}) %all-to-all-start.1) | async-done | bytes 147488 | tf_op jit(solution)/shard_map/all_to_all | solution.py:613
  49.9 0.0 collective-permute-start.6
  49.9 0.0 collective-permute-done.9.refs_3_
  50.0 1.4 %collective-permute-done.6.refs_1_ = f32[3,96,128]{2,1,0:T(8,128)S(1)} collective-permute-done((f32[3,96,128]{2,1,0:T(8,128)S(1)}, f32[3,96,128]{2,1,0:T(8,128)S(1)}, u32[]{:S(2)}, u32[]{:S(2)}) %collective-permute-start.6) | collective-permute-done | bytes 147488 | tf_op jit(solution)/shard_map/ppermute | solution.py:574
  51.3 0.0 copy-done.4
  51.3 1.1 %shard_map.102 = (f32[2,2,96,96]{3,2,1,0:T(8,128)}, f32[2,192,192]{2,1,0:T(8,128)}) custom-call(f32[2,2,96,96]{3,2,1,0:T(8,128)S(1)} %copy-done.4, f32[2,192,192]{2,1,0:T(8,128)S(1)} %copy-done.2, f32[3,96,128]{2,1,0:T(8,128)S(1)} %bitcast.5, f32[3,96,128]{2,1,0:T(8,128)S(1)} %collective-permute-done.6.refs_1_, f32[96,384]{1,0:T(8,128)S(1)} %get-tuple-element.24.refs_2_, ...), custom_call_target="tpu_custom_call" | custom-call | tf_op jit(solution)/shard_map/pallas_call | solution.py:728
  (1 shorter events, 0.0 us)
Async XLA Ops:
  0.6 10.6 %copy-start.2 = (f32[2,192,192]{2,1,0:T(8,128)S(1)}, f32[2,192,192]{2,1,0:T(8,128)}, u32[]{:S(2)}) copy-start(f32[2,192,192]{2,1,0:T(8,128)} %probe_ref.3) | copy-start | bytes 884740
  0.6 10.5 %collective-permute-start = (f32[2,2,96,96]{3,2,1,0:T(8,128)}, f32[2,2,96,96]{3,2,1,0:T(8,128)S(1)}, u32[]{:S(2)}, u32[]{:S(2)}) collective-permute-start(f32[2,2,96,96]{3,2,1,0:T(8,128)} %object_ref.3), channel_id=1, source_target_pairs={{0,1},{1,0},{2,3},{3,2},{4,5},{5,4},{6,7},{7,6},{8,9},{9,8},{10,11... | collective-permute-start | bytes 442376 | tf_op jit(solution)/shard_map/ppermute | solution.py:640
  3.7 1.0 %copy-start.3 = (f32[2,2,96,96]{3,2,1,0:T(8,128)S(1)}, f32[2,2,96,96]{3,2,1,0:T(8,128)}, u32[]{:S(2)}) copy-start(f32[2,2,96,96]{3,2,1,0:T(8,128)} %object_ref.3) | copy-start | bytes 442372
  4.7 6.5 %copy-start.5 = (f32[1,1,2,192,192]{4,3,2,1,0:T(8,128)S(1)}, f32[1,1,2,192,192]{4,3,2,1,0:T(8,128)}, u32[]{:S(2)}) copy-start(f32[1,1,2,192,192]{4,3,2,1,0:T(8,128)} %measured_ref.1) | copy-start | bytes 884740
  4.7 6.5 %copy-start.6 = (f32[192,192]{1,0:T(8,128)S(1)}, f32[192,192]{1,0:T(8,128)}, u32[]{:S(2)}) copy-start(f32[192,192]{1,0:T(8,128)} %phase_ref.1) | copy-start | bytes 442372
  4.7 6.6 %copy-start.7 = (s32[1,1,2,2]{3,2,1,0:T(2,128)S(1)}, s32[1,1,2,2]{3,2,1,0:T(2,128)}, u32[]{:S(2)}) copy-start(s32[1,1,2,2]{3,2,1,0:T(2,128)} %offsets_ref.1) | copy-start | bytes 52
  4.8 7.5 %collective-permute-start.4 = (f32[96,384]{1,0:T(8,128)S(1)}, f32[96,384]{1,0:T(8,128)S(1)}, u32[]{:S(2)}, u32[]{:S(2)}) collective-permute-start(f32[96,384]{1,0:T(8,128)S(1)} %shard_map.96.refs_0_), channel_id=1, source_target_pairs={{2,5},{4,3},{3,4},{5,2},{6,9},{8,7},{7,8},{9,6},{10,13},{12,11},{1... | collective-permute-start | bytes 442376 | tf_op jit(solution)/shard_map/ppermute | solution.py:592
  5.6 6.8 %collective-permute-start.3 = (f32[96,384]{1,0:T(8,128)S(1)}, f32[96,384]{1,0:T(8,128)S(1)}, u32[]{:S(2)}, u32[]{:S(2)}) collective-permute-start(f32[96,384]{1,0:T(8,128)S(1)} %shard_map.96.refs_0_), channel_id=1, source_target_pairs={{2,4},{6,8},{10,12},{14,16},{18,20},{22,24},{26,28},{4,2},{8,6},{1... | collective-permute-start | bytes 442376 | tf_op jit(solution)/shard_map/ppermute | solution.py:582
  6.3 6.1 %collective-permute-start.1 = (f32[96,384]{1,0:T(8,128)S(1)}, f32[96,384]{1,0:T(8,128)S(1)}, u32[]{:S(2)}, u32[]{:S(2)}) collective-permute-start(f32[96,384]{1,0:T(8,128)S(1)} %shard_map.96.refs_0_), channel_id=1, source_target_pairs={{0,2},{2,0},{1,3},{3,1},{4,6},{6,4},{5,7},{7,5},{8,10},{10,8},{9,1... | collective-permute-start | bytes 442376 | tf_op jit(solution)/shard_map/ppermute | solution.py:574
  11.1 1.5 %copy-start = (bf16[3,2,256,256]{3,2,1,0:T(8,128)(2,1)S(1)}, bf16[3,2,256,256]{3,2,1,0:T(8,128)(2,1)}, u32[]{:S(2)}) copy-start(bf16[3,2,256,256]{3,2,1,0:T(8,128)(2,1)} %constant.4.clone.refs_9_) | copy-start | bytes 2359300
  11.1 1.5 %copy-start.1 = (bf16[3,384,192]{2,1,0:T(8,128)(2,1)S(1)}, bf16[3,384,192]{2,1,0:T(8,128)(2,1)}, u32[]{:S(2)}) copy-start(bf16[3,384,192]{2,1,0:T(8,128)(2,1)} %constant.5.clone.refs_10_) | copy-start | bytes 1327108
  11.1 1.5 %collective-permute-start.2 = (f32[2,2,96,96]{3,2,1,0:T(8,128)S(1)}, f32[2,2,96,96]{3,2,1,0:T(8,128)S(1)}, u32[]{:S(2)}, u32[]{:S(2)}) collective-permute-start(f32[2,2,96,96]{3,2,1,0:T(8,128)S(1)} %collective-permute-done.refs_1_), channel_id=1, source_target_pairs={{0,2},{2,0},{1,3},{3,1},{4,6},{6,4},{5,7},{7,5},{8,10},{10,8},{9,1... | collective-permute-start | bytes 442376 | tf_op jit(solution)/shard_map/ppermute | solution.py:574
  18.6 3.3 %collective-permute-start.5 = (f32[3,96,128]{2,1,0:T(8,128)S(1)}, f32[3,96,128]{2,1,0:T(8,128)S(1)}, u32[]{:S(2)}, u32[]{:S(2)}) collective-permute-start(f32[3,96,128]{2,1,0:T(8,128)S(1)} %get-tuple-element.19), channel_id=1, source_target_pairs={{0,2},{2,0},{1,3},{3,1},{4,6},{6,4},{5,7},{7,5},{8,10},{10,8},{9,1... | collective-permute-start | bytes 442376 | tf_op jit(solution)/shard_map/ppermute | solution.py:574
  22.6 15.3 %all-to-all-start = ((f32[16,9,2,128]{3,2,1,0:T(2,128)}), f32[16,9,2,128]{3,2,1,0:T(2,128)S(1)}, u32[]{:S(2)}, u32[]{:S(2)}) async-start(f32[16,9,2,128]{3,2,1,0:T(2,128)} %bitcast), calls=%async_computation | async-start | bytes 294912 | tf_op jit(solution)/shard_map/all_to_all | solution.py:604
  29.7 21.6 %copy-start.4 = (f32[2,2,96,96]{3,2,1,0:T(8,128)S(1)}, f32[2,2,96,96]{3,2,1,0:T(8,128)}, u32[]{:S(2)}) copy-start(f32[2,2,96,96]{3,2,1,0:T(8,128)} %object_ref.3) | copy-start | bytes 442372
  31.4 10.7 %collective-permute-start.7 = (f32[96,768]{1,0:T(8,128)S(1)}, f32[96,768]{1,0:T(8,128)S(1)}, u32[]{:S(2)}, u32[]{:S(2)}) collective-permute-start(f32[96,768]{1,0:T(8,128)S(1)} %get-tuple-element.22), channel_id=1, source_target_pairs={{0,2},{2,0},{1,3},{3,1},{4,6},{6,4},{5,7},{7,5},{8,10},{10,8},{9,1... | collective-permute-start | bytes 884744 | tf_op jit(solution)/shard_map/ppermute | solution.py:574
  31.5 10.6 %collective-permute-start.8 = (f32[96,768]{1,0:T(8,128)S(1)}, f32[96,768]{1,0:T(8,128)S(1)}, u32[]{:S(2)}, u32[]{:S(2)}) collective-permute-start(f32[96,768]{1,0:T(8,128)S(1)} %get-tuple-element.23), channel_id=1, source_target_pairs={{2,4},{6,8},{10,12},{14,16},{18,20},{22,24},{26,28},{4,2},{8,6},{1... | collective-permute-start | bytes 884744 | tf_op jit(solution)/shard_map/ppermute | solution.py:582
  38.6 11.4 %all-to-all-start.1 = ((f32[16,9,2,128]{3,2,1,0:T(2,128)}), f32[16,9,2,128]{3,2,1,0:T(2,128)S(1)}, u32[]{:S(2)}, u32[]{:S(2)}) async-start(f32[16,9,2,128]{3,2,1,0:T(2,128)} %bitcast.2), calls=%async_computation.1 | async-start | bytes 294912 | tf_op jit(solution)/shard_map/all_to_all | solution.py:613
  42.2 7.8 %collective-permute-start.9 = (f32[96,384]{1,0:T(8,128)S(1)}, f32[96,384]{1,0:T(8,128)S(1)}, u32[]{:S(2)}, u32[]{:S(2)}) collective-permute-start(f32[96,384]{1,0:T(8,128)S(1)} %get-tuple-element.25), channel_id=1, source_target_pairs={{0,1},{1,0},{2,3},{3,2},{4,5},{5,4},{6,7},{7,6},{8,9},{9,8},{10,11... | collective-permute-start | bytes 442376 | tf_op jit(solution)/shard_map/ppermute | solution.py:725
  49.9 1.4 %collective-permute-start.6 = (f32[3,96,128]{2,1,0:T(8,128)S(1)}, f32[3,96,128]{2,1,0:T(8,128)S(1)}, u32[]{:S(2)}, u32[]{:S(2)}) collective-permute-start(f32[3,96,128]{2,1,0:T(8,128)S(1)} %bitcast.4), channel_id=1, source_target_pairs={{0,2},{2,0},{1,3},{3,1},{4,6},{6,4},{5,7},{7,5},{8,10},{10,8},{9,1... | collective-permute-start | bytes 442376 | tf_op jit(solution)/shard_map/ppermute | solution.py:574

commit v8 on v6

--- a/solution.py
+++ b/solution.py
@@ -43,7 +43,7 @@
         right[1, :half, 0, :half] = sine
         right[1, :half, 1, :half] = cosine
         high, low = halves(right.reshape(2 * LANES, 2 * LANES))
-        rights.append(np.stack([high, low]))
+        rights.append(np.concatenate([high, high, low], 0))
         high, low = halves(np.block([[cosine.T, sine.T], [-sine.T, cosine.T]]))
         lefts.append(np.concatenate([high, low], 0))
     return np.stack(rights), np.stack(lefts)
@@ -259,17 +259,18 @@
     span = 2 * LANES
 
     def put(slot, block, row, a, b):
+        rows = pl.ds(block * width + row, step)
         high, low = halves_of(jnp.concatenate([a, b], 1))
-        data[slot][block, pl.ds(row, step), :] = high
-        data[slot][block, pl.ds(width + row, step), :] = low
+        data[slot][rows, :span] = high
+        data[slot][rows, span:] = low
 
     def multiply_right(slot, odd):
         for block in range(2):
             rows = slice(block * width, (block + 1) * width)
-            left = data[slot][block]
-            out = jnp.dot(left, right_ref[odd * block, 0], preferred_element_type=f32)
-            low = jnp.dot(left[:width], right_ref[odd * block, 1], preferred_element_type=f32)
-            out_right[slot][rows, :] = out[:width] + (out[width:] + low)
+            left = jnp.concatenate([data[slot][rows, :], data[slot][rows, :span]], 1)
+            out_right[slot][rows, :] = jnp.dot(
+                left, right_ref[odd * block], preferred_element_type=f32
+            )
             yield
 
     def put_mid(slot, block, start, first, second):
@@ -645,7 +646,7 @@
         pltpu.SMEM((8, LANES), jnp.int32),
         pltpu.SemaphoreType.DMA,
     ]
-    scratch += [pltpu.VMEM((2, 2 * width, 2 * LANES), bf16)] * slots
+    scratch += [pltpu.VMEM((2 * width, 4 * LANES), bf16)] * slots
     scratch += [pltpu.VMEM((2 * width, 2 * LANES), f32)] * slots
     scratch += [pltpu.VMEM((2, 2 * width, 2 * LANES), bf16)] * slots
     scratch += [pltpu.VMEM((2, width, 2 * LANES), f32)] * slots

time: 52.8 us -> 52.8 us (level)
  no operation moved by 1% of the time
where the time goes in v8:
time: 52.8 us; the launch traced here: 52.4 us
  starting transfers between devices  24.4 us (46%)
  waiting for transfers between devices  14.2 us (27%)
  Pallas kernels  9.94 us (19%)
  local copies, waits for them, and re-layouts  1.71 us (3%)
  between operations  1.49 us (3%)
  other arithmetic  0.74 us (1%)
    all_to_all x2, waiting for transfers between devices, all_sum(): x = lax.all_to_all(x, group, 0, 0, tiled=True)  11.6 us
    all_to_all x2, starting transfers between devices, all_sum(): x = lax.all_to_all(x, group, 0, 0, tiled=True)  10.7 us
    ppermute x5, starting transfers between devices, from_near(): return lax.ppermute(x, 'core', [(0, 1), (1, 0)])  6.78 us
    pallas_call x1, Pallas kernels, shards(): pl.pallas_call(functools.partial(position_kernel, paired, cores), out_sha...  6.04 us
    ppermute x1, starting transfers between devices, shards(): beside = [lax.ppermute(cells, 'col', [(0, 1), (1, 0)])]  3.06 us
    ppermute x5, waiting for transfers between devices, from_near(): return lax.ppermute(x, 'core', [(0, 1), (1, 0)])  2.57 us
    ppermute x1, starting transfers between devices, shards(): received = [lax.ppermute(parts[1], 'col', [(0, 1), (1, 0)])]  1.87 us
    pallas_call x1, Pallas kernels, shards(): pl.pallas_call(functools.partial(place_kernel, paired, cores), out_shape=...  1.6 us
  transfers between devices with their start and end apart: 12, of which 5 were waited for; matrix products, arithmetic and copies ran while one was open for 1% of the time, Pallas kernels for 5%

profile of v8, /device:TPU:0, one launch (start us, length us, event | category | flops | bytes accessed | tf_op | source)
XLA Modules:
  0.0 52.4 jit_solution(15418750204056782833)
XLA Ops:
  0.6 0.0 copy-start.2
  0.6 0.0 copy-start.3
  0.7 1.0 %copy-done.3 = f32[2,2,96,96]{3,2,1,0:T(8,128)S(1)} copy-done((f32[2,2,96,96]{3,2,1,0:T(8,128)S(1)}, f32[2,2,96,96]{3,2,1,0:T(8,128)}, u32[]{:S(2)}) %copy-start.3) | copy-done | bytes 147480
  1.6 0.0 copy-start.5
  1.6 0.0 copy-start.6
  1.6 0.0 copy-start.7
  1.6 0.1 shard_map.96.refs_0_
  1.7 3.1 %collective-permute-start = (f32[96,384]{1,0:T(8,128)S(1)}, f32[96,384]{1,0:T(8,128)S(1)}, u32[]{:S(2)}, u32[]{:S(2)}) collective-permute-start(f32[96,384]{1,0:T(8,128)S(1)} %shard_map.96.refs_0_), channel_id=1, source_target_pairs={{0,1},{1,0},{2,3},{3,2},{4,5},{5,4},{6,7},{7,6},{8,9},{9,8},{10,11... | collective-permute-start | bytes 442376 | tf_op jit(solution)/shard_map/ppermute | solution.py:615
  4.8 0.7 %collective-permute-start.4 = (f32[96,384]{1,0:T(8,128)S(1)}, f32[96,384]{1,0:T(8,128)S(1)}, u32[]{:S(2)}, u32[]{:S(2)}) collective-permute-start(f32[96,384]{1,0:T(8,128)S(1)} %shard_map.96.refs_0_), channel_id=1, source_target_pairs={{2,5},{4,3},{3,4},{5,2},{6,9},{8,7},{7,8},{9,6},{10,13},{12,11},{1... | collective-permute-start | bytes 442376 | tf_op jit(solution)/shard_map/ppermute | solution.py:574
  5.5 0.7 %collective-permute-start.3 = (f32[96,384]{1,0:T(8,128)S(1)}, f32[96,384]{1,0:T(8,128)S(1)}, u32[]{:S(2)}, u32[]{:S(2)}) collective-permute-start(f32[96,384]{1,0:T(8,128)S(1)} %shard_map.96.refs_0_), channel_id=1, source_target_pairs={{2,4},{6,8},{10,12},{14,16},{18,20},{22,24},{26,28},{4,2},{8,6},{1... | collective-permute-start | bytes 442376 | tf_op jit(solution)/shard_map/ppermute | solution.py:564
  6.1 4.2 %collective-permute-start.1 = (f32[96,384]{1,0:T(8,128)S(1)}, f32[96,384]{1,0:T(8,128)S(1)}, u32[]{:S(2)}, u32[]{:S(2)}) collective-permute-start(f32[96,384]{1,0:T(8,128)S(1)} %shard_map.96.refs_0_), channel_id=1, source_target_pairs={{0,2},{2,0},{1,3},{3,1},{4,6},{6,4},{5,7},{7,5},{8,10},{10,8},{9,1... | collective-permute-start | bytes 442376 | tf_op jit(solution)/shard_map/ppermute | solution.py:556
  10.9 0.0 copy-start
  11.0 0.0 copy-start.1
  11.0 0.0 collective-permute-done.refs_1_
  11.0 0.1 collective-permute-start.2
  11.1 0.0 copy-done.2
  11.1 0.0 copy-done.5
  11.1 0.0 copy-done.6
  11.1 0.0 copy-done.7
  11.1 1.1 %shard_map.95 = (f32[2,192,256]{2,1,0:T(8,128)S(1)}, f32[2,192,256]{2,1,0:T(8,128)S(1)}, f32[2,192,256]{2,1,0:T(8,128)S(1)}, s32[8,128]{1,0:T(8,128)S(1)}) custom-call(s32[1,1,2,2]{3,2,1,0:T(2,128)S(1)} %copy-done.7, s32[1,1]{1,0:T(1,128)S(6)} %copy.10.counts_ref, f32[2,192,192]{2,1,0:T(8,128)S(1)} %copy-done.2, f32[192,192]{1,0:T(8,128)S(1)} %copy-done.6, ...), custom_call_target="tpu_custom_call" | custom-call | flops 10000000000 | bytes 10000000 | tf_op jit(solution)/shard_map/pallas_call | solution.py:625
  12.2 0.0 collective-permute-done.4.refs_5_
  12.2 0.0 collective-permute-done.3.refs_4_
  12.2 0.0 collective-permute-done.1.refs_2_
  12.2 0.2 collective-permute-done.2.refs_3_
  12.4 0.0 copy-done
  12.4 0.0 copy-done.1
  12.4 6.0 %shard_map.97 = (f32[4,2,384,128]{3,2,1,0:T(8,128)S(1)}, f32[3,96,128]{2,1,0:T(8,128)S(1)}, f32[3,96,128]{2,1,0:T(8,128)S(1)}) custom-call(s32[8,128]{1,0:T(8,128)S(1)} %get-tuple-element.14.places_ref, f32[96,384]{1,0:T(8,128)S(1)} %shard_map.96.refs_0_, f32[96,384]{1,0:T(8,128)S(1)} %collective-permute-done.refs_1_, ...), custom_call_target="tpu_custom_call" | custom-call | tf_op jit(solution)/shard_map/pallas_call | solution.py:654
  18.5 2.4 %collective-permute-start.5 = (f32[3,96,128]{2,1,0:T(8,128)S(1)}, f32[3,96,128]{2,1,0:T(8,128)S(1)}, u32[]{:S(2)}, u32[]{:S(2)}) collective-permute-start(f32[3,96,128]{2,1,0:T(8,128)S(1)} %get-tuple-element.19), channel_id=1, source_target_pairs={{0,2},{2,0},{1,3},{3,1},{4,6},{6,4},{5,7},{7,5},{8,10},{10,8},{9,1... | collective-permute-start | bytes 442376 | tf_op jit(solution)/shard_map/ppermute | solution.py:556
  20.8 1.0 %collective-permute-done.5 = f32[3,96,128]{2,1,0:T(8,128)S(1)} collective-permute-done((f32[3,96,128]{2,1,0:T(8,128)S(1)}, f32[3,96,128]{2,1,0:T(8,128)S(1)}, u32[]{:S(2)}, u32[]{:S(2)}) %collective-permute-start.5) | collective-permute-done | bytes 147488 | tf_op jit(solution)/shard_map/ppermute | solution.py:556
  21.9 0.7 %add.3 = f32[3,96,128]{2,1,0:T(8,128)} add(f32[3,96,128]{2,1,0:T(8,128)S(1)} %get-tuple-element.18, f32[3,96,128]{2,1,0:T(8,128)S(1)} %collective-permute-done.5) | non-fusion elementwise | flops 36864 | bytes 442368 | tf_op jit(solution)/shard_map/add | solution.py:676
  22.5 7.2 %all-to-all-start = ((f32[16,9,2,128]{3,2,1,0:T(2,128)}), f32[16,9,2,128]{3,2,1,0:T(2,128)S(1)}, u32[]{:S(2)}, u32[]{:S(2)}) async-start(f32[16,9,2,128]{3,2,1,0:T(2,128)} %bitcast), calls=%async_computation | async-start | bytes 294912 | tf_op jit(solution)/shard_map/all_to_all | solution.py:586
  29.7 0.0 copy-start.4
  29.7 1.6 %shard_map.98 = (f32[96,768]{1,0:T(8,128)S(1)}, f32[96,768]{1,0:T(8,128)S(1)}, f32[96,768]{1,0:T(8,128)S(1)}) custom-call(s32[8,128]{1,0:T(8,128)S(1)} %get-tuple-element.14.places_ref, f32[4,2,384,128]{3,2,1,0:T(8,128)S(1)} %get-tuple-element.20.window), custom_call_target="tpu_custom_call" | custom-call | tf_op jit(solution)/shard_map/pallas_call | solution.py:662
  31.3 0.2 collective-permute-start.7
  31.5 0.7 %collective-permute-start.8 = (f32[96,768]{1,0:T(8,128)S(1)}, f32[96,768]{1,0:T(8,128)S(1)}, u32[]{:S(2)}, u32[]{:S(2)}) collective-permute-start(f32[96,768]{1,0:T(8,128)S(1)} %get-tuple-element.23), channel_id=1, source_target_pairs={{2,4},{6,8},{10,12},{14,16},{18,20},{22,24},{26,28},{4,2},{8,6},{1... | collective-permute-start | bytes 884744 | tf_op jit(solution)/shard_map/ppermute | solution.py:564
  32.2 5.7 %all-to-all-done = f32[16,9,2,128]{3,2,1,0:T(2,128)S(1)} async-done(((f32[16,9,2,128]{3,2,1,0:T(2,128)}), f32[16,9,2,128]{3,2,1,0:T(2,128)S(1)}, u32[]{:S(2)}, u32[]{:S(2)}) %all-to-all-start) | async-done | bytes 147488 | tf_op jit(solution)/shard_map/all_to_all | solution.py:586
  37.9 0.1 reduce_sum.9
  37.9 0.7 %broadcast_in_dim.2 = f32[16,9,2,128]{3,2,1,0:T(2,128)} broadcast(f32[9,2,128]{2,1,0:T(2,128)S(1)} %reduce_sum.9), dimensions={1,2,3} | broadcast | bytes 156672 | tf_op jit(solution)/shard_map/broadcast_in_dim | solution.py:587
  38.6 3.5 %all-to-all-start.1 = ((f32[16,9,2,128]{3,2,1,0:T(2,128)}), f32[16,9,2,128]{3,2,1,0:T(2,128)S(1)}, u32[]{:S(2)}, u32[]{:S(2)}) async-start(f32[16,9,2,128]{3,2,1,0:T(2,128)} %broadcast_in_dim.2), calls=%async_computation.1 | async-start | bytes 294912 | tf_op jit(solution)/shard_map/all_to_all | solution.py:588
  42.2 0.0 collective-permute-done.7.near_ref
  42.2 0.0 collective-permute-done.8.far_ref
  42.2 1.9 %collective-permute-start.9 = (f32[96,384]{1,0:T(8,128)S(1)}, f32[96,384]{1,0:T(8,128)S(1)}, u32[]{:S(2)}, u32[]{:S(2)}) collective-permute-start(f32[96,384]{1,0:T(8,128)S(1)} %get-tuple-element.25), channel_id=1, source_target_pairs={{0,1},{1,0},{2,3},{3,2},{4,5},{5,4},{6,7},{7,6},{8,9},{9,8},{10,11... | collective-permute-start | bytes 442376 | tf_op jit(solution)/shard_map/ppermute | solution.py:693
  44.1 5.9 %all-to-all-done.1 = f32[16,9,2,128]{3,2,1,0:T(2,128)S(1)} async-done(((f32[16,9,2,128]{3,2,1,0:T(2,128)}), f32[16,9,2,128]{3,2,1,0:T(2,128)S(1)}, u32[]{:S(2)}, u32[]{:S(2)}) %all-to-all-start.1) | async-done | bytes 147488 | tf_op jit(solution)/shard_map/all_to_all | solution.py:588
  50.0 0.0 collective-permute-start.6
  50.0 0.0 collective-permute-done.9.refs_3_
  50.0 1.4 %collective-permute-done.6.refs_1_ = f32[3,96,128]{2,1,0:T(8,128)S(1)} collective-permute-done((f32[3,96,128]{2,1,0:T(8,128)S(1)}, f32[3,96,128]{2,1,0:T(8,128)S(1)}, u32[]{:S(2)}, u32[]{:S(2)}) %collective-permute-start.6) | collective-permute-done | bytes 147488 | tf_op jit(solution)/shard_map/ppermute | solution.py:556
  51.4 0.0 copy-done.4
  51.4 1.1 %shard_map.100 = (f32[2,2,96,96]{3,2,1,0:T(8,128)}, f32[2,192,192]{2,1,0:T(8,128)}) custom-call(f32[2,2,96,96]{3,2,1,0:T(8,128)S(1)} %copy-done.4, f32[2,192,192]{2,1,0:T(8,128)S(1)} %copy-done.2, f32[3,96,128]{2,1,0:T(8,128)S(1)} %bitcast.3, f32[3,96,128]{2,1,0:T(8,128)S(1)} %collective-permute-done.6.refs_1_, f32[96,384]{1,0:T(8,128)S(1)} %get-tuple-element.24.refs_2_, ...), custom_call_target="tpu_custom_call" | custom-call | tf_op jit(solution)/shard_map/pallas_call | solution.py:696
  (1 shorter events, 0.0 us)
Async XLA Ops:
  0.6 10.4 %copy-start.2 = (f32[2,192,192]{2,1,0:T(8,128)S(1)}, f32[2,192,192]{2,1,0:T(8,128)}, u32[]{:S(2)}) copy-start(f32[2,192,192]{2,1,0:T(8,128)} %probe_ref.3) | copy-start | bytes 884740
  0.6 1.0 %copy-start.3 = (f32[2,2,96,96]{3,2,1,0:T(8,128)S(1)}, f32[2,2,96,96]{3,2,1,0:T(8,128)}, u32[]{:S(2)}) copy-start(f32[2,2,96,96]{3,2,1,0:T(8,128)} %object_ref.3) | copy-start | bytes 442372
  1.6 9.5 %copy-start.5 = (f32[1,1,2,192,192]{4,3,2,1,0:T(8,128)S(1)}, f32[1,1,2,192,192]{4,3,2,1,0:T(8,128)}, u32[]{:S(2)}) copy-start(f32[1,1,2,192,192]{4,3,2,1,0:T(8,128)} %measured_ref.1) | copy-start | bytes 884740
  1.6 9.5 %copy-start.6 = (f32[192,192]{1,0:T(8,128)S(1)}, f32[192,192]{1,0:T(8,128)}, u32[]{:S(2)}) copy-start(f32[192,192]{1,0:T(8,128)} %phase_ref.1) | copy-start | bytes 442372
  1.6 9.5 %copy-start.7 = (s32[1,1,2,2]{3,2,1,0:T(2,128)S(1)}, s32[1,1,2,2]{3,2,1,0:T(2,128)}, u32[]{:S(2)}) copy-start(s32[1,1,2,2]{3,2,1,0:T(2,128)} %offsets_ref.1) | copy-start | bytes 52
  1.7 9.2 %collective-permute-start = (f32[96,384]{1,0:T(8,128)S(1)}, f32[96,384]{1,0:T(8,128)S(1)}, u32[]{:S(2)}, u32[]{:S(2)}) collective-permute-start(f32[96,384]{1,0:T(8,128)S(1)} %shard_map.96.refs_0_), channel_id=1, source_target_pairs={{0,1},{1,0},{2,3},{3,2},{4,5},{5,4},{6,7},{7,6},{8,9},{9,8},{10,11... | collective-permute-start | bytes 442376 | tf_op jit(solution)/shard_map/ppermute | solution.py:615
  4.8 7.4 %collective-permute-start.4 = (f32[96,384]{1,0:T(8,128)S(1)}, f32[96,384]{1,0:T(8,128)S(1)}, u32[]{:S(2)}, u32[]{:S(2)}) collective-permute-start(f32[96,384]{1,0:T(8,128)S(1)} %shard_map.96.refs_0_), channel_id=1, source_target_pairs={{2,5},{4,3},{3,4},{5,2},{6,9},{8,7},{7,8},{9,6},{10,13},{12,11},{1... | collective-permute-start | bytes 442376 | tf_op jit(solution)/shard_map/ppermute | solution.py:574
  5.5 6.8 %collective-permute-start.3 = (f32[96,384]{1,0:T(8,128)S(1)}, f32[96,384]{1,0:T(8,128)S(1)}, u32[]{:S(2)}, u32[]{:S(2)}) collective-permute-start(f32[96,384]{1,0:T(8,128)S(1)} %shard_map.96.refs_0_), channel_id=1, source_target_pairs={{2,4},{6,8},{10,12},{14,16},{18,20},{22,24},{26,28},{4,2},{8,6},{1... | collective-permute-start | bytes 442376 | tf_op jit(solution)/shard_map/ppermute | solution.py:564
  6.1 6.1 %collective-permute-start.1 = (f32[96,384]{1,0:T(8,128)S(1)}, f32[96,384]{1,0:T(8,128)S(1)}, u32[]{:S(2)}, u32[]{:S(2)}) collective-permute-start(f32[96,384]{1,0:T(8,128)S(1)} %shard_map.96.refs_0_), channel_id=1, source_target_pairs={{0,2},{2,0},{1,3},{3,1},{4,6},{6,4},{5,7},{7,5},{8,10},{10,8},{9,1... | collective-permute-start | bytes 442376 | tf_op jit(solution)/shard_map/ppermute | solution.py:556
  10.9 1.5 %copy-start = (bf16[3,768,256]{2,1,0:T(8,128)(2,1)S(1)}, bf16[3,768,256]{2,1,0:T(8,128)(2,1)}, u32[]{:S(2)}) copy-start(bf16[3,768,256]{2,1,0:T(8,128)(2,1)} %constant.6.clone.refs_9_) | copy-start | bytes 3538948
  11.0 1.5 %copy-start.1 = (bf16[3,384,192]{2,1,0:T(8,128)(2,1)S(1)}, bf16[3,384,192]{2,1,0:T(8,128)(2,1)}, u32[]{:S(2)}) copy-start(bf16[3,384,192]{2,1,0:T(8,128)(2,1)} %constant.7.clone.refs_10_) | copy-start | bytes 1327108
  11.0 1.4 %collective-permute-start.2 = (f32[96,384]{1,0:T(8,128)S(1)}, f32[96,384]{1,0:T(8,128)S(1)}, u32[]{:S(2)}, u32[]{:S(2)}) collective-permute-start(f32[96,384]{1,0:T(8,128)S(1)} %collective-permute-done.refs_1_), channel_id=1, source_target_pairs={{0,2},{2,0},{1,3},{3,1},{4,6},{6,4},{5,7},{7,5},{8,10},{10,8},{9,1... | collective-permute-start | bytes 442376 | tf_op jit(solution)/shard_map/ppermute | solution.py:556
  18.5 3.4 %collective-permute-start.5 = (f32[3,96,128]{2,1,0:T(8,128)S(1)}, f32[3,96,128]{2,1,0:T(8,128)S(1)}, u32[]{:S(2)}, u32[]{:S(2)}) collective-permute-start(f32[3,96,128]{2,1,0:T(8,128)S(1)} %get-tuple-element.19), channel_id=1, source_target_pairs={{0,2},{2,0},{1,3},{3,1},{4,6},{6,4},{5,7},{7,5},{8,10},{10,8},{9,1... | collective-permute-start | bytes 442376 | tf_op jit(solution)/shard_map/ppermute | solution.py:556
  22.5 15.3 %all-to-all-start = ((f32[16,9,2,128]{3,2,1,0:T(2,128)}), f32[16,9,2,128]{3,2,1,0:T(2,128)S(1)}, u32[]{:S(2)}, u32[]{:S(2)}) async-start(f32[16,9,2,128]{3,2,1,0:T(2,128)} %bitcast), calls=%async_computation | async-start | bytes 294912 | tf_op jit(solution)/shard_map/all_to_all | solution.py:586
  29.7 21.7 %copy-start.4 = (f32[2,2,96,96]{3,2,1,0:T(8,128)S(1)}, f32[2,2,96,96]{3,2,1,0:T(8,128)}, u32[]{:S(2)}) copy-start(f32[2,2,96,96]{3,2,1,0:T(8,128)} %object_ref.3) | copy-start | bytes 442372
  31.3 10.8 %collective-permute-start.7 = (f32[96,768]{1,0:T(8,128)S(1)}, f32[96,768]{1,0:T(8,128)S(1)}, u32[]{:S(2)}, u32[]{:S(2)}) collective-permute-start(f32[96,768]{1,0:T(8,128)S(1)} %get-tuple-element.22), channel_id=1, source_target_pairs={{0,2},{2,0},{1,3},{3,1},{4,6},{6,4},{5,7},{7,5},{8,10},{10,8},{9,1... | collective-permute-start | bytes 884744 | tf_op jit(solution)/shard_map/ppermute | solution.py:556
  31.5 10.7 %collective-permute-start.8 = (f32[96,768]{1,0:T(8,128)S(1)}, f32[96,768]{1,0:T(8,128)S(1)}, u32[]{:S(2)}, u32[]{:S(2)}) collective-permute-start(f32[96,768]{1,0:T(8,128)S(1)} %get-tuple-element.23), channel_id=1, source_target_pairs={{2,4},{6,8},{10,12},{14,16},{18,20},{22,24},{26,28},{4,2},{8,6},{1... | collective-permute-start | bytes 884744 | tf_op jit(solution)/shard_map/ppermute | solution.py:564
  38.6 11.4 %all-to-all-start.1 = ((f32[16,9,2,128]{3,2,1,0:T(2,128)}), f32[16,9,2,128]{3,2,1,0:T(2,128)S(1)}, u32[]{:S(2)}, u32[]{:S(2)}) async-start(f32[16,9,2,128]{3,2,1,0:T(2,128)} %broadcast_in_dim.2), calls=%async_computation.1 | async-start | bytes 294912 | tf_op jit(solution)/shard_map/all_to_all | solution.py:588
  42.2 7.8 %collective-permute-start.9 = (f32[96,384]{1,0:T(8,128)S(1)}, f32[96,384]{1,0:T(8,128)S(1)}, u32[]{:S(2)}, u32[]{:S(2)}) collective-permute-start(f32[96,384]{1,0:T(8,128)S(1)} %get-tuple-element.25), channel_id=1, source_target_pairs={{0,1},{1,0},{2,3},{3,2},{4,5},{5,4},{6,7},{7,6},{8,9},{9,8},{10,11... | collective-permute-start | bytes 442376 | tf_op jit(solution)/shard_map/ppermute | solution.py:693
  50.0 1.4 %collective-permute-start.6 = (f32[3,96,128]{2,1,0:T(8,128)S(1)}, f32[3,96,128]{2,1,0:T(8,128)S(1)}, u32[]{:S(2)}, u32[]{:S(2)}) collective-permute-start(f32[3,96,128]{2,1,0:T(8,128)S(1)} %bitcast.2), channel_id=1, source_target_pairs={{0,2},{2,0},{1,3},{3,1},{4,6},{6,4},{5,7},{7,5},{8,10},{10,8},{9,1... | collective-permute-start | bytes 442376 | tf_op jit(solution)/shard_map/ppermute | solution.py:556
